TPU v7x, 32 devices: a whole 2x2x4 slice. The times are simulated.
32 devices in a mesh: rows: 8 (over y, x, core), seq: 4 (over z).
Axes of the slice: x: 2, y: 2, z: 4, core: 2. Of those that a mesh axis runs over, the one named last changes fastest.
Arguments:
- tokens_in: bfloat16 [32, 4096, 512], P('rows', 'seq'), may hold values from -6 to 6
- layer_norm_gain: float32 [512], replicated, may hold values from 0.5 to 1.5
- layer_norm_bias: float32 [512], replicated, may hold values from -3 to 3
- input_real: bfloat16 [256, 512], replicated, may hold values from -0.1875 to 0.1875
- input_imag: bfloat16 [256, 512], replicated, may hold values from -0.1875 to 0.1875
- decay_log: float32 [256], replicated, may hold values from -7.5 to -3
- angle_log: float32 [256], replicated, may hold values from -5 to 0.5
- scale_log: float32 [256], replicated, may hold values from -0.5 to 0.5
- output_real: bfloat16 [512, 256], replicated, may hold values from -0.375 to 0.375
- output_imag: bfloat16 [512, 256], replicated, may hold values from -0.375 to 0.375
- skip_gain: float32 [512], replicated, may hold values from -3 to 3
- glu_value: bfloat16 [512, 512], replicated, may hold values from -0.5 to 0.5
- glu_gate: bfloat16 [512, 512], replicated, may hold values from -0.25 to 0.25
- glu_bias: float32 [1024], replicated, may hold values from -3 to 3
- doc_lengths: int32 [32, 8], P('rows'), may hold values from 1 to 1024, 4096 in all within a row
- out_grad: bfloat16 [32, 4096, 512], P('rows', 'seq'), may hold values from -6 to 6
Outputs:
- block_out: bfloat16 [32, 4096, 512], P('rows', 'seq')
- input_grad: bfloat16 [32, 4096, 512], P('rows', 'seq')
- norm_gain_grad: float32 [512], replicated
- norm_shift_grad: float32 [512], replicated
- input_real_grad: float32 [256, 512], replicated
- input_imag_grad: float32 [256, 512], replicated
- decay_log_grad: float32 [256], replicated
- angle_log_grad: float32 [256], replicated
- scale_log_grad: float32 [256], replicated
- output_real_grad: float32 [512, 256], replicated
- output_imag_grad: float32 [512, 256], replicated
- skip_gain_grad: float32 [512], replicated
- glu_value_grad: float32 [512, 512], replicated
- glu_gate_grad: float32 [512, 512], replicated
- glu_bias_grad: float32 [1024], replicated
Inputs may be any that keep to these rules, and one draw needn't show every extreme that they name: `doc_lengths`: each row's entries sum to 4096; the last entry is the row's trailing padding, the others are its documents' lengths in order.
All inputs are finite; a program needn't handle non-finite values.
Results may differ from a plain program's by a relative error of at most 0.014.
Values may be sent and summed in bfloat16 or wider, within the bound.
No kernel may reach another device: no remote copies, remote signals or barrier semaphores. Data moves between devices by JAX's collectives and lax.ppermute only.
A program may use at most 192 MiB of HBM per device.

v0:
```python
import jax
import jax.numpy as jnp
from jax import lax
from jax.sharding import PartitionSpec as P

EPSILON = 1e-05


def complex_mul(left_real, left_imag, right_real, right_imag):
    return (
        left_real * right_real - left_imag * right_imag,
        left_real * right_imag + left_imag * right_real,
    )


def compose(earlier, later):
    early_mult_real, early_mult_imag, early_add_real, early_add_imag = earlier
    late_mult_real, late_mult_imag, late_add_real, late_add_imag = later
    mult_real, mult_imag = complex_mul(
        late_mult_real, late_mult_imag, early_mult_real, early_mult_imag
    )
    moved_real, moved_imag = complex_mul(
        late_mult_real, late_mult_imag, early_add_real, early_add_imag
    )
    return (mult_real, mult_imag, late_add_real + moved_real, late_add_imag + moved_imag)


def serial_scan(elements, reverse):
    steps = elements[0].shape[1]
    order = list(range(steps))
    if reverse:
        order = order[::-1]
    results = [None] * steps
    running = None
    for place in order:
        current = tuple((item[:, place] for item in elements))
        running = current if running is None else compose(running, current)
        results[place] = running
    return tuple((jnp.stack([entry[member] for entry in results], axis=1) for member in range(4)))


def block_scan(elements, reverse):
    outer, steps, lanes_count = elements[0].shape
    block = 1
    for option in (16, 8, 4, 2):
        if steps % option == 0 and block == 1:
            block = option
    if steps <= 16 or block == 1:
        return serial_scan(elements, reverse)
    groups = steps // block
    grouped = tuple((item.reshape(outer * groups, block, lanes_count) for item in elements))
    local = serial_scan(grouped, reverse)
    edge = 0 if reverse else block - 1
    totals = tuple((item[:, edge].reshape(outer, groups, lanes_count) for item in local))
    prefix = block_scan(totals, reverse)
    ones_row = jnp.ones((outer, 1, lanes_count), jnp.float32)
    zero_row = jnp.zeros((outer, 1, lanes_count), jnp.float32)
    identity = (ones_row, zero_row, zero_row, zero_row)
    if reverse:
        carry = tuple(
            (jnp.concatenate([item[:, 1:], base], axis=1) for item, base in zip(prefix, identity))
        )
    else:
        carry = tuple(
            (jnp.concatenate([base, item[:, :-1]], axis=1) for item, base in zip(prefix, identity))
        )
    carry = tuple((item.reshape(outer * groups, 1, lanes_count) for item in carry))
    joined = compose(carry, local)
    return tuple((item.reshape(outer, steps, lanes_count) for item in joined))


def reset_keep(doc_lengths, first, count):
    places = first + jnp.arange(count, dtype=jnp.int32)
    starts = jnp.cumsum(doc_lengths, axis=1) - doc_lengths
    hits = jnp.any(places[None, :, None] == starts[:, None, :], axis=-1)
    return jnp.where(hits, 0.0, 1.0).astype(jnp.float32)


def valid_mask(doc_lengths, first, count):
    places = first + jnp.arange(count, dtype=jnp.int32)
    limit = jnp.sum(doc_lengths, axis=1) - doc_lengths[:, -1]
    return jnp.where(places[None, :] < limit[:, None], 1.0, 0.0).astype(jnp.float32)


def decay_terms(decay_log, angle_log, scale_log):
    rate = jnp.exp(decay_log)
    radius = jnp.exp(-rate)
    angle = jnp.exp(angle_log)
    scale = jnp.exp(scale_log) * jnp.sqrt(1.0 - jnp.exp(-2.0 * rate))
    return (radius * jnp.cos(angle), radius * jnp.sin(angle), scale)


def to_lanes(stacked, length, lanes):
    return stacked.transpose(0, 2, 1, 3).reshape(2, length, lanes).astype(jnp.float32)


def from_lanes(flat, length, rows_here, chans):
    return flat.reshape(length, rows_here, chans).transpose(1, 0, 2)


def body(
    tokens_in,
    layer_norm_gain,
    layer_norm_bias,
    input_real,
    input_imag,
    decay_log,
    angle_log,
    scale_log,
    output_real,
    output_imag,
    skip_gain,
    glu_value,
    glu_gate,
    glu_bias,
    doc_lengths,
    out_grad,
):
    rows_here, toks, width = tokens_in.shape
    channels = input_real.shape[0]
    parts = lax.axis_size("seq")
    seat = lax.axis_index("seq")
    length = toks * parts
    chans = channels // parts
    lanes = rows_here * chans
    first = seat * toks
    x_float = tokens_in.astype(jnp.float32)
    centered_input = x_float - jnp.mean(x_float, axis=-1, keepdims=True)
    inverse_deviation = lax.rsqrt(
        jnp.mean(centered_input * centered_input, axis=-1, keepdims=True) + EPSILON
    )
    standardized_input = centered_input * inverse_deviation
    normed_output = standardized_input * layer_norm_gain + layer_norm_bias
    normed_low = normed_output.astype(jnp.bfloat16)
    decay_real, decay_imag, scale = decay_terms(decay_log, angle_log, scale_log)
    real_float = input_real.astype(jnp.float32)
    imag_float = input_imag.astype(jnp.float32)
    scaled = jnp.stack([real_float * scale[:, None], imag_float * scale[:, None]]).astype(
        jnp.bfloat16
    )
    drive = jnp.einsum(
        "rth,pnh->prtn", normed_low, scaled, preferred_element_type=jnp.float32
    ).astype(jnp.bfloat16)
    moved = lax.all_to_all(drive, "seq", split_axis=3, concat_axis=2, tiled=True)
    flat_drive = to_lanes(moved, length, lanes)
    keep_all = reset_keep(doc_lengths, 0, length)
    keep_lane = jnp.repeat(keep_all.T, chans, axis=1)
    lane_real = jnp.tile(lax.dynamic_slice_in_dim(decay_real, seat * chans, chans), rows_here)
    lane_imag = jnp.tile(lax.dynamic_slice_in_dim(decay_imag, seat * chans, chans), rows_here)
    scanned = block_scan(
        (
            (keep_lane * lane_real)[None],
            (keep_lane * lane_imag)[None],
            flat_drive[0][None],
            flat_drive[1][None],
        ),
        False,
    )
    flat_state_real = scanned[2][0]
    flat_state_imag = scanned[3][0]
    state_stack = jnp.stack(
        [
            from_lanes(flat_state_real, length, rows_here, chans),
            from_lanes(flat_state_imag, length, rows_here, chans),
        ]
    ).astype(jnp.bfloat16)
    state_low = lax.all_to_all(state_stack, "seq", split_axis=2, concat_axis=3, tiled=True)
    out_stack = jnp.stack([output_real, -output_imag])
    mixed = (
        jnp.einsum("prtn,phn->rth", state_low, out_stack, preferred_element_type=jnp.float32)
        + skip_gain * normed_output
    )
    normal_cdf = 0.5 * (1.0 + lax.erf(mixed * 0.7071067811865476))
    activated = (mixed * normal_cdf).astype(jnp.bfloat16)
    value = (
        jnp.einsum("rth,hk->rtk", activated, glu_value, preferred_element_type=jnp.float32)
        + glu_bias[:width]
    )
    gate = (
        jnp.einsum("rth,hk->rtk", activated, glu_gate, preferred_element_type=jnp.float32)
        + glu_bias[width:]
    )
    sigma = jax.nn.sigmoid(gate)
    block_out = (x_float + value * sigma).astype(jnp.bfloat16)
    grad_out = out_grad.astype(jnp.float32) * valid_mask(doc_lengths, first, toks)[:, :, None]
    grad_value = (grad_out * sigma).astype(jnp.bfloat16)
    grad_gate = (grad_out * value * sigma * (1.0 - sigma)).astype(jnp.bfloat16)
    value_weight_grad = jnp.einsum(
        "rth,rtk->hk", activated, grad_value, preferred_element_type=jnp.float32
    )
    gate_weight_grad = jnp.einsum(
        "rth,rtk->hk", activated, grad_gate, preferred_element_type=jnp.float32
    )
    bias_grad = jnp.concatenate(
        [
            jnp.sum(grad_value.astype(jnp.float32), axis=(0, 1)),
            jnp.sum(grad_gate.astype(jnp.float32), axis=(0, 1)),
        ]
    )
    grad_act = jnp.einsum("rtk,hk->rth", grad_value, glu_value, preferred_element_type=jnp.float32)
    grad_act = grad_act + jnp.einsum(
        "rtk,hk->rth", grad_gate, glu_gate, preferred_element_type=jnp.float32
    )
    density = jnp.exp(-0.5 * mixed * mixed) * 0.3989422804014327
    grad_mixed = (grad_act * (normal_cdf + mixed * density)).astype(jnp.bfloat16)
    grad_mixed_float = grad_mixed.astype(jnp.float32)
    skip_grad = jnp.sum(grad_mixed_float * normed_output, axis=(0, 1))
    out_stack_grad = jnp.einsum(
        "rth,prtn->phn", grad_mixed, state_low, preferred_element_type=jnp.float32
    )
    grad_state = jnp.einsum(
        "rth,phn->prtn", grad_mixed, out_stack, preferred_element_type=jnp.float32
    ).astype(jnp.bfloat16)
    grad_moved = lax.all_to_all(grad_state, "seq", split_axis=3, concat_axis=2, tiled=True)
    flat_grad = to_lanes(grad_moved, length, lanes)
    keep_next = jnp.repeat(reset_keep(doc_lengths, 1, length).T, chans, axis=1)
    back_scanned = block_scan(
        (
            (keep_next * lane_real)[None],
            (keep_next * -lane_imag)[None],
            flat_grad[0][None],
            flat_grad[1][None],
        ),
        True,
    )
    flat_adj_real = back_scanned[2][0]
    flat_adj_imag = back_scanned[3][0]
    front = jnp.zeros((1, lanes), jnp.float32)
    prior_real = jnp.concatenate([front, flat_state_real[:-1]], axis=0)
    prior_imag = jnp.concatenate([front, flat_state_imag[:-1]], axis=0)
    lane_part_real = jnp.sum(
        keep_lane * (flat_adj_real * prior_real + flat_adj_imag * prior_imag), axis=0
    )
    lane_part_imag = jnp.sum(
        keep_lane * (flat_adj_imag * prior_real - flat_adj_real * prior_imag), axis=0
    )
    part = jnp.stack(
        [
            jnp.sum(lane_part_real.reshape(rows_here, chans), axis=0),
            jnp.sum(lane_part_imag.reshape(rows_here, chans), axis=0),
        ]
    )
    lambda_grad = lax.dynamic_update_slice(
        jnp.zeros((2, channels), jnp.float32), part, (jnp.int32(0), seat * chans)
    )
    adjoint_stack = jnp.stack(
        [
            from_lanes(flat_adj_real, length, rows_here, chans),
            from_lanes(flat_adj_imag, length, rows_here, chans),
        ]
    ).astype(jnp.bfloat16)
    adjoint_low = lax.all_to_all(adjoint_stack, "seq", split_axis=2, concat_axis=3, tiled=True)
    scaled_grad = jnp.einsum(
        "prtn,rth->pnh", adjoint_low, normed_low, preferred_element_type=jnp.float32
    )
    normed_gradient = jnp.einsum(
        "prtn,pnh->rth", adjoint_low, scaled, preferred_element_type=jnp.float32
    )
    normed_gradient = normed_gradient + skip_gain * grad_mixed_float
    gain_gradient_rows = jnp.sum(normed_gradient * standardized_input, axis=(0, 1))
    shift_grad = jnp.sum(normed_gradient, axis=(0, 1))
    gradient_through_hat = normed_gradient * layer_norm_gain
    grad_x = inverse_deviation * (
        gradient_through_hat
        - jnp.mean(gradient_through_hat, axis=-1, keepdims=True)
        - standardized_input
        * jnp.mean(gradient_through_hat * standardized_input, axis=-1, keepdims=True)
    )
    input_grad = (grad_x + grad_out).astype(jnp.bfloat16)
    totals = lax.psum(
        (
            scaled_grad,
            out_stack_grad,
            value_weight_grad,
            gate_weight_grad,
            bias_grad,
            skip_grad,
            gain_gradient_rows,
            shift_grad,
            lambda_grad,
        ),
        ("rows", "seq"),
    )
    (
        scaled_total,
        out_total,
        value_total,
        gate_total,
        bias_total,
        skip_total,
        gain_total,
        shift_total,
        lambda_total,
    ) = totals
    real_grad = scaled_total[0] * scale[:, None]
    imag_grad = scaled_total[1] * scale[:, None]
    scale_grad = jnp.sum(scaled_total[0] * real_float + scaled_total[1] * imag_float, axis=1)
    rate = jnp.exp(decay_log)
    radius = jnp.exp(-rate)
    angle = jnp.exp(angle_log)
    cosine = jnp.cos(angle)
    sine = jnp.sin(angle)
    radius_grad = lambda_total[0] * cosine + lambda_total[1] * sine
    angle_grad = radius * (lambda_total[1] * cosine - lambda_total[0] * sine) * angle
    norm_root = jnp.sqrt(1.0 - jnp.exp(-2.0 * rate))
    decay_grad = (
        -radius_grad * radius * rate
        + scale_grad * jnp.exp(scale_log) * jnp.exp(-2.0 * rate) * rate / norm_root
    )
    scale_log_grad = scale_grad * scale
    return (
        block_out,
        input_grad,
        gain_total,
        shift_total,
        real_grad,
        imag_grad,
        decay_grad,
        angle_grad,
        scale_log_grad,
        out_total[0],
        -out_total[1],
        skip_total,
        value_total,
        gate_total,
        bias_total,
    )


def solution(mesh):
    placed = (
        P("rows", "seq", None),
        P(),
        P(),
        P(),
        P(),
        P(),
        P(),
        P(),
        P(),
        P(),
        P(),
        P(),
        P(),
        P(),
        P("rows", None),
        P("rows", "seq", None),
    )
    return jax.shard_map(
        body,
        mesh=mesh,
        in_specs=placed,
        out_specs=(
            P("rows", "seq", None),
            P("rows", "seq", None),
            P(),
            P(),
            P(),
            P(),
            P(),
            P(),
            P(),
            P(),
            P(),
            P(),
            P(),
            P(),
            P(),
        ),
        check_vma=False,
    )
```

profile of v0, /device:TPU:0, one launch (start us, length us, event | category | flops | bytes accessed | tf_op | source)
XLA Modules:
  0.0 1042.2 jit_solution(6771881088870225730)
XLA Ops:
  35.6 6.9 broadcast_in_dim.26.clone
  42.5 8.6 reshape.8320
  57.0 8.7 reshape.8321
  65.7 11.9 %copy_multiply_fusion.1 = (f32[256,16,256]{2,0,1:T(8,128)}, f32[256,16,256]{2,0,1:T(8,128)}, f32[256,16,256]{2,0,1:T(8,128)S(1)}, f32[256,16,256]{2,0,1:T(8,128)}) fusion(f32[256,16,256]{2,1,0:T(8,128)} %reshape.8321, f32[256]{0:T(256)S(1)} %mul.16727, f32[256]{0:T(256)S(1)} %neg.29, f32[256]{0:T(256)S(1)} %mul.16732, f32[256,16,256]{2,1,0:T(8,128)} %reshape.8320), kind=kLoop, calls=%fused_computation.61 | loop fusion | flops 4194304 | bytes 25168896 | tf_op jit(solution)/shard_map/mul | solution.py:219
  89.7 35.9 %all-to-all-done = bf16[2,4,1024,256]{2,1,0,3:T(4,128)(2,1)} async-done(((bf16[2,4,1024,256]{2,1,0,3:T(4,128)(2,1)}), bf16[2,4,1024,256]{2,1,0,3:T(4,128)(2,1)}, u32[]{:S(2)}, u32[]{:S(2)}) %all-to-all-start) | async-done | bytes 4194336 | tf_op jit(solution)/shard_map/all_to_all | solution.py:144
  125.6 8.6 copy.583
  134.2 10.9 %reshape.8349 = f32[2,4,4096,64]{2,3,1,0:T(8,128)} reshape(f32[2,4,4,1024,64]{3,2,4,1,0:T(4,128)} %bitcast.1076) | data formatting | bytes 16777216 | tf_op jit(solution)/shard_map/convert_element_type | solution.py:94
  145.1 7.7 fusion.191
  152.8 8.3 copy.223
  161.2 8.8 reshape_broadcast_in_dim_squeeze.12
  169.9 15.2 %fusion.198 = (f32[256,1,256]{2,1,0:T(1,128)}, f32[256,1,256]{2,1,0:T(1,128)}, f32[256,1,256]{2,1,0:T(1,128)}, f32[256,1,256]{2,1,0:T(1,128)}, f32[256,1,256]{2,...) fusion(f32[256,16,256]{2,1,0:T(8,128)} %reshape_broadcast_in_di, ...), kind=kLoop, calls=%fused_computation.980 | loop fusion | bytes 8388608 | tf_op jit(solution)/shard_map/slice | solution.py:36
  185.8 8.3 copy.229
  194.2 8.6 reshape_broadcast_in_dim_squeeze.13
  202.8 15.8 %fusion.197 = (f32[256,1,256]{2,1,0:T(1,128)S(1)}, f32[256,1,256]{2,1,0:T(1,128)}, f32[256,1,256]{2,1,0:T(1,128)}, f32[256,1,256]{2,1,0:T(1,128)S(1)}, f32[256,1...) fusion(f32[256,16,256]{2,1,0:T(8,128)} %reshape_broadcast_in_di, ...), kind=kLoop, calls=%fused_computation.979 | loop fusion | bytes 8388608 | tf_op jit(solution)/shard_map/slice | solution.py:36
  257.1 9.6 fusion.174
  269.3 7.1 add.9533
  278.9 7.1 add.9538
  285.9 8.2 copy_bitcast_fusion.7
  294.1 9.5 reshape.8566
  309.1 92.6 %all-to-all-done.1 = bf16[4,2,262144]{2,1,0:T(2,128)(2,1)} async-done(((bf16[4,2,262144]{2,1,0:T(2,128)(2,1)}), bf16[4,2,262144]{2,1,0:T(2,128)(2,1)}, u32[]{:S(2)}, u32[]{:S(2)}) %all-to-all-start.1) | async-done | bytes 4194336 | tf_op jit(solution)/shard_map/all_to_all | solution.py:167
  401.7 9.3 reshape.8567
  411.0 12.8 %copy.264 = bf16[2,4,1024,4,64]{2,4,3,1,0:T(8,128)(2,1)} copy(bf16[2,4,1024,4,64]{4,1,0,2,3:T(4,128)(2,1)} %bitcast.1072) | data formatting | bytes 8388608 | tf_op jit(solution)/shard_map/all_to_all | solution.py:167
  423.8 10.0 multiply_convert_fusion.2
  439.5 12.4 %convert_reduce_fusion.1 = (f32[512]{0:T(512)}, bf16[4,1024,512]{2,1,0:T(8,128)(2,1)}, bf16[4,1024,512]{2,1,0:T(8,128)(2,1)}, f32[512]{0:T(512)}, bf16[4,1024,512]{2,1,0:T(8,128)(2,1)S(1)}) fusion(f32[4,1024,512]{2,1,0:T(8,128)} %fusion.49, f32[512]{0:T(512)S(1)} %get-tuple-element.841, f32[4,1024]{1,0:T(4,128)S(1)} %copy-done.144, ...), kind=kOutput, calls=%fused_computation.36 | convolution fusion | flops 2193619968 | bytes 34103296 | tf_op jit(solution)/shard_map/rth,hk->rtk/dot_general | solution.py:180
  455.7 7.0 fusion.25
  492.6 75.4 %all-to-all-done.2 = bf16[2,4,1024,256]{2,1,0,3:T(4,128)(2,1)} async-done(((bf16[2,4,1024,256]{2,1,0,3:T(4,128)(2,1)}), bf16[2,4,1024,256]{2,1,0,3:T(4,128)(2,1)}, u32[]{:S(2)}, u32[]{:S(2)}) %all-to-all-start.2) | async-done | bytes 4194336 | tf_op jit(solution)/shard_map/all_to_all | solution.py:214
  568.0 8.6 copy.582
  576.6 10.9 %reshape.8350 = f32[2,4,4096,64]{2,3,1,0:T(8,128)} reshape(f32[2,4,4,1024,64]{3,2,4,1,0:T(4,128)} %bitcast.1077) | data formatting | bytes 16777216 | tf_op jit(solution)/shard_map/convert_element_type | solution.py:94
  587.5 7.7 fusion.190
  595.2 8.3 copy.290
  603.6 8.6 reshape_broadcast_in_dim_squeeze.15
  612.1 15.2 %fusion.194 = (f32[256,1,256]{2,1,0:T(1,128)}, f32[256,1,256]{2,1,0:T(1,128)S(1)}, f32[256,1,256]{2,1,0:T(1,128)S(1)}, f32[256,1,256]{2,1,0:T(1,128)S(1)}, f32[2...) fusion(f32[256,16,256]{2,1,0:T(8,128)} %reshape_broadcast_in_di, ...), kind=kLoop, calls=%fused_computation.976 | loop fusion | bytes 8388608 | tf_op jit(solution)/shard_map/slice | solution.py:36
  634.0 8.3 copy.270
  642.3 8.6 reshape_broadcast_in_dim_squeeze.14
  650.9 15.5 %fusion.195 = (f32[256,1,256]{2,1,0:T(1,128)S(1)}, f32[256,1,256]{2,1,0:T(1,128)S(1)}, f32[256,1,256]{2,1,0:T(1,128)S(1)}, f32[256,1,256]{2,1,0:T(1,128)S(1)}, f...) fusion(f32[256,16,256]{2,1,0:T(8,128)} %reshape_broadcast_in_di, ...), kind=kLoop, calls=%fused_computation.977 | loop fusion | bytes 8388608 | tf_op jit(solution)/shard_map/slice | solution.py:36
  721.4 7.1 add.9831
  731.0 7.1 add.9836
  738.1 8.2 copy_bitcast_fusion.6
  746.4 9.5 reshape.8568
  822.1 7.2 fusion.26
  829.7 23.9 %all-to-all-done.3 = bf16[4,2,262144]{2,1,0:T(2,128)(2,1)} async-done(((bf16[4,2,262144]{2,1,0:T(2,128)(2,1)}), bf16[4,2,262144]{2,1,0:T(2,128)(2,1)}, u32[]{:S(2)}, u32[]{:S(2)}) %all-to-all-start.3) | async-done | bytes 4194336 | tf_op jit(solution)/shard_map/all_to_all | solution.py:252
  853.5 9.3 reshape.8569
  862.8 12.8 %copy.311 = bf16[2,4,1024,4,64]{2,4,3,1,0:T(8,128)(2,1)} copy(bf16[2,4,1024,4,64]{4,1,0,2,3:T(4,128)(2,1)} %bitcast.1073) | data formatting | bytes 8388608 | tf_op jit(solution)/shard_map/all_to_all | solution.py:252
  875.6 7.0 convolution_bitcast_fusion.2
  883.6 12.7 %fusion.15 = (f32[512]{0:T(512)S(1)}, f32[4,1024]{1,0:T(4,128)S(1)}, f32[4,1024]{1,0:T(4,128)S(1)}, f32[512]{0:T(512)S(1)}, f32[512]{0:T(512)S(1)}, /*index=5*/f32[4,1024,512]{2,1,0:T(8,128)}) fusion(bf16[4,1024,512]{2,1,0:T(8,128)(2,1)} %param.16, f32[4,1024]{1,0:T(4,128)S(1)} %copy-done.143, f32[4,1024]{1,0:T(4,128)S(1)} %copy-done.137, ...), kind=kOutput, calls=%fused_computation.21 | convolution fusion | flops 2183387648 | bytes 21573632 | tf_op jit(solution)/shard_map/prtn,pnh->rth/dot_general | solution.py:256
  896.3 38.3 %all-reduce.6 = (f32[512]{0:T(512)}, f32[512]{0:T(512)}, f32[2,256]{1,0:T(2,128)S(1)}, f32[512]{0:T(512)}, f32[1024]{0:T(1024)}) all-reduce(f32[512]{0:T(512)S(1)} %get-tuple-element.107, f32[512]{0:T(512)S(1)} %get-tuple-element.110, f32[2,256]{1,0:T(2,128)S(1)} %dynamic_update_slice.3, ...), channel_id=1, replica_groups=mesh['rows'=8,'seq'=4] {'rows','seq'}, use_global_device_ids=true, to_apply=%region_9.10 | all-reduce | flops 3072 | bytes 24576 | tf_op jit(solution)/shard_map/psum | solution.py:270
  934.6 10.3 fusion.14
  945.0 80.5 %all-reduce.10.cloned.1.call-done = (f32[2,256,512]{2,1,0:T(8,128)}, f32[2,512,256]{1,2,0:T(8,128)}, f32[512,512]{1,0:T(8,128)}, f32[512,512]{1,0:T(8,128)}) async-done(((f32[2,256,512]{2,1,0:T(8,128)}, f32[2,512,256]{1,2,0:T(8,128)}, f32[512,512]{1,0:T(8,128)}, f32[512,512]{1,0:T(8,128)}), (f32[2,256,512]{2,1,0:T(8,128)}, f32[2,512,256]{1,2,0:T(8,128)}, f32[512,512]{1,0:T(8,128)}, ...) | async-done | bytes 4194320 | tf_op jit(solution)/shard_map/psum | solution.py:270
  (663 shorter events, 274.6 us)
Async XLA Ops:
  7.2 432.3 %copy-start = (bf16[512,512]{1,0:T(8,128)(2,1)S(1)}, bf16[512,512]{1,0:T(8,128)(2,1)}, u32[]{:S(2)}) copy-start(bf16[512,512]{1,0:T(8,128)(2,1)} %param.28) | copy-start | bytes 1572868
  13.2 410.6 %copy-start.136 = (f32[4,1024]{1,0:T(4,128)}, f32[4,1024]{1,0:T(4,128)S(1)}, u32[]{:S(2)}) copy-start(f32[4,1024]{1,0:T(4,128)S(1)} %broadcast_multiply_fusion.2) | copy-start | bytes 49156
  15.7 408.1 %copy-start.142 = (f32[4,1024]{1,0:T(4,128)}, f32[4,1024]{1,0:T(4,128)S(1)}, u32[]{:S(2)}) copy-start(f32[4,1024]{1,0:T(4,128)S(1)} %get-tuple-element.862) | copy-start | bytes 49156
  25.8 99.8 %all-to-all-start = ((bf16[2,4,1024,256]{2,1,0,3:T(4,128)(2,1)}), bf16[2,4,1024,256]{2,1,0,3:T(4,128)(2,1)}, u32[]{:S(2)}, u32[]{:S(2)}) async-start(bf16[2,4,1024,256]{2,1,0,3:T(4,128)(2,1)} %copy.221), calls=%async_computation | async-start | bytes 8388608 | tf_op jit(solution)/shard_map/all_to_all | solution.py:144
  33.0 9.5 copy-start.129
  77.6 11.1 %copy-start.2 = (f32[256,16,256]{2,0,1:T(8,128)}, f32[256,16,256]{2,0,1:T(8,128)S(1)}, u32[]{:S(2)}) copy-start(f32[256,16,256]{2,0,1:T(8,128)S(1)} %get-tuple-element.852) | copy-start | bytes 12582916
  194.2 24.5 %copy-start.34 = (f32[256,1,256]{2,0,1:T(8,128)S(1)}, f32[256,1,256]{2,0,1:T(8,128)}, u32[]{:S(2)}) copy-start(f32[256,1,256]{2,0,1:T(8,128)} %get-tuple-element.557) | copy-start | bytes 786436
  202.8 15.9 %copy-start.3 = (f32[256,16,256]{2,0,1:T(8,128)S(1)}, f32[256,16,256]{2,0,1:T(8,128)}, u32[]{:S(2)}) copy-start(f32[256,16,256]{2,0,1:T(8,128)} %copy-done.2) | copy-start | bytes 12582916
  202.8 15.9 %copy-start.5 = (f32[256,16,256]{2,0,1:T(8,128)S(1)}, f32[256,16,256]{2,0,1:T(8,128)}, u32[]{:S(2)}) copy-start(f32[256,16,256]{2,0,1:T(8,128)} %get-tuple-element.853) | copy-start | bytes 12582916
  303.7 98.1 %all-to-all-start.1 = ((bf16[4,2,262144]{2,1,0:T(2,128)(2,1)}), bf16[4,2,262144]{2,1,0:T(2,128)(2,1)}, u32[]{:S(2)}, u32[]{:S(2)}) async-start(bf16[4,2,262144]{2,1,0:T(2,128)(2,1)} %reshape.8566), calls=%async_computation.1 | async-start | bytes 8388608 | tf_op jit(solution)/shard_map/all_to_all | solution.py:167
  411.0 12.8 %copy-start.159 = (bf16[512,256]{1,0:T(8,128)(2,1)S(1)}, bf16[512,256]{1,0:T(8,128)(2,1)}, u32[]{:S(2)}) copy-start(bf16[512,256]{1,0:T(8,128)(2,1)} %param.24) | copy-start | bytes 786436
  411.0 12.8 %copy-start.162 = (f32[512]{0:T(512)S(1)}, f32[512]{0:T(512)}, u32[]{:S(2)}) copy-start(f32[512]{0:T(512)} %param.26) | copy-start | bytes 6148
  423.8 10.0 copy-start.40
  470.4 97.6 %all-to-all-start.2 = ((bf16[2,4,1024,256]{2,1,0,3:T(4,128)(2,1)}), bf16[2,4,1024,256]{2,1,0,3:T(4,128)(2,1)}, u32[]{:S(2)}, u32[]{:S(2)}) async-start(bf16[2,4,1024,256]{2,1,0,3:T(4,128)(2,1)} %copy.268), calls=%async_computation.2 | async-start | bytes 8388608 | tf_op jit(solution)/shard_map/all_to_all | solution.py:214
  481.0 10.1 copy-start.7
  627.4 46.4 %copy-start.28 = (f32[256,1,256]{2,1,0:T(1,128)}, f32[256,1,256]{2,1,0:T(1,128)S(1)}, u32[]{:S(2)}) copy-start(f32[256,1,256]{2,1,0:T(1,128)S(1)} %get-tuple-element.653) | copy-start | bytes 786436
  650.9 22.8 %copy-start.8 = (f32[256,16,256]{2,0,1:T(8,128)S(1)}, f32[256,16,256]{2,0,1:T(8,128)}, u32[]{:S(2)}) copy-start(f32[256,16,256]{2,0,1:T(8,128)} %get-tuple-element.670) | copy-start | bytes 12582916
  650.9 22.8 %copy-start.87 = (f32[256,1,256]{2,1,0:T(1,128)S(1)}, f32[256,1,256]{2,1,0:T(1,128)}, u32[]{:S(2)}) copy-start(f32[256,1,256]{2,1,0:T(1,128)} %get-tuple-element.652) | copy-start | bytes 786436
  666.4 7.3 copy-start.6
  691.8 10.3 copy-start.52
  692.1 10.8 %copy-start.51 = (f32[256,1,256]{2,0,1:T(8,128)S(1)}, f32[256,1,256]{2,0,1:T(8,128)}, u32[]{:S(2)}) copy-start(f32[256,1,256]{2,0,1:T(8,128)} %get-tuple-element.134) | copy-start | bytes 786436
  692.3 11.2 %copy-start.50 = (f32[256,1,256]{2,0,1:T(8,128)S(1)}, f32[256,1,256]{2,0,1:T(8,128)}, u32[]{:S(2)}) copy-start(f32[256,1,256]{2,0,1:T(8,128)} %get-tuple-element.137) | copy-start | bytes 786436
  692.8 11.5 %copy-start.49 = (f32[256,1,256]{2,0,1:T(8,128)S(1)}, f32[256,1,256]{2,0,1:T(8,128)}, u32[]{:S(2)}) copy-start(f32[256,1,256]{2,0,1:T(8,128)} %get-tuple-element.138) | copy-start | bytes 786436
  693.8 11.3 %copy-start.48 = (f32[256,1,256]{2,0,1:T(8,128)S(1)}, f32[256,1,256]{2,0,1:T(8,128)}, u32[]{:S(2)}) copy-start(f32[256,1,256]{2,0,1:T(8,128)} %get-tuple-element.141) | copy-start | bytes 786436
  694.2 11.6 %copy-start.47 = (f32[256,1,256]{2,0,1:T(8,128)S(1)}, f32[256,1,256]{2,0,1:T(8,128)}, u32[]{:S(2)}) copy-start(f32[256,1,256]{2,0,1:T(8,128)} %get-tuple-element.142) | copy-start | bytes 786436
  694.6 11.9 %copy-start.46 = (f32[256,1,256]{2,0,1:T(8,128)S(1)}, f32[256,1,256]{2,0,1:T(8,128)}, u32[]{:S(2)}) copy-start(f32[256,1,256]{2,0,1:T(8,128)} %get-tuple-element.145) | copy-start | bytes 786436
  696.6 10.6 %copy-start.45 = (f32[256,1,256]{2,0,1:T(8,128)S(1)}, f32[256,1,256]{2,0,1:T(8,128)}, u32[]{:S(2)}) copy-start(f32[256,1,256]{2,0,1:T(8,128)} %get-tuple-element.146) | copy-start | bytes 786436
  699.9 8.7 copy-start.92
  701.2 8.1 copy-start.91
  701.2 8.9 copy-start.90
  701.3 9.6 copy-start.89
  701.3 10.3 copy-start.29
  701.4 11.0 %copy-start.17 = (f32[256,16,256]{2,0,1:T(8,128)S(1)}, f32[256,16,256]{2,0,1:T(8,128)}, u32[]{:S(2)}) copy-start(f32[256,16,256]{2,0,1:T(8,128)} %copy-done.16) | copy-start | bytes 12582916
  701.4 11.0 %copy-start.20 = (f32[256,16,256]{2,0,1:T(8,128)S(1)}, f32[256,16,256]{2,0,1:T(8,128)}, u32[]{:S(2)}) copy-start(f32[256,16,256]{2,0,1:T(8,128)} %copy-done.19) | copy-start | bytes 12582916
  755.9 97.6 %all-to-all-start.3 = ((bf16[4,2,262144]{2,1,0:T(2,128)(2,1)}), bf16[4,2,262144]{2,1,0:T(2,128)(2,1)}, u32[]{:S(2)}, u32[]{:S(2)}) async-start(bf16[4,2,262144]{2,1,0:T(2,128)(2,1)} %reshape.8568), calls=%async_computation.3 | async-start | bytes 8388608 | tf_op jit(solution)/shard_map/all_to_all | solution.py:252
  760.8 264.7 %all-reduce.10.cloned.1.call-start = ((), (), s32[]{:S(2)}) async-start(), calls=%async_computation.4 | async-start | bytes 8388608 | tf_op jit(solution)/shard_map/psum | solution.py:270
  862.8 12.8 %copy-start.137 = (f32[4,1024]{1,0:T(4,128)S(1)}, f32[4,1024]{1,0:T(4,128)}, u32[]{:S(2)}) copy-start(f32[4,1024]{1,0:T(4,128)} %copy-done.136) | copy-start | bytes 49156
  862.8 12.8 %copy-start.143 = (f32[4,1024]{1,0:T(4,128)S(1)}, f32[4,1024]{1,0:T(4,128)}, u32[]{:S(2)}) copy-start(f32[4,1024]{1,0:T(4,128)} %copy-done.142) | copy-start | bytes 49156
  862.8 12.8 %copy-start.156 = (f32[512]{0:T(512)S(1)}, f32[512]{0:T(512)}, u32[]{:S(2)}) copy-start(f32[512]{0:T(512)} %param.17) | copy-start | bytes 6148
  862.8 12.8 %copy-start.161 = (f32[512]{0:T(512)S(1)}, f32[512]{0:T(512)}, u32[]{:S(2)}) copy-start(f32[512]{0:T(512)} %param.18) | copy-start | bytes 6148
  883.6 51.0 %copy-start.145 = (f32[4,1024]{1,0:T(4,128)S(1)}, f32[4,1024]{1,0:T(4,128)}, u32[]{:S(2)}) copy-start(f32[4,1024]{1,0:T(4,128)} %get-tuple-element.863) | copy-start | bytes 49156
  934.6 90.9 %copy-start.69 = (bf16[256,512]{1,0:T(8,128)(2,1)S(1)}, bf16[256,512]{1,0:T(8,128)(2,1)}, u32[]{:S(2)}) copy-start(bf16[256,512]{1,0:T(8,128)(2,1)} %param.19) | copy-start | bytes 786436
  934.6 90.9 %copy-start.71 = (bf16[256,512]{1,0:T(8,128)(2,1)S(1)}, bf16[256,512]{1,0:T(8,128)(2,1)}, u32[]{:S(2)}) copy-start(bf16[256,512]{1,0:T(8,128)(2,1)} %param.20) | copy-start | bytes 786436
  934.6 90.9 %copy-start.147 = (f32[256]{0:T(256)S(1)}, f32[256]{0:T(256)}, u32[]{:S(2)}) copy-start(f32[256]{0:T(256)} %copy-done.146) | copy-start | bytes 3076
  944.9 86.3 %copy-start.150 = (f32[256]{0:T(256)S(1)}, f32[256]{0:T(256)}, u32[]{:S(2)}) copy-start(f32[256]{0:T(256)} %param.22) | copy-start | bytes 3076
  944.9 86.3 %copy-start.152 = (f32[256]{0:T(256)S(1)}, f32[256]{0:T(256)}, u32[]{:S(2)}) copy-start(f32[256]{0:T(256)} %param.21) | copy-start | bytes 3076
  945.0 86.3 %copy-start.154 = (f32[256]{0:T(256)S(1)}, f32[256]{0:T(256)}, u32[]{:S(2)}) copy-start(f32[256]{0:T(256)} %param.23) | copy-start | bytes 3076
  1025.5 8.7 copy-start.116
  (122 other events, 316.2 us)
Sparse Core Ops, SparseCore 0:
  882.7 142.7 all-reduce.9
where the time goes:
time: 1060 us; the launch traced here: 1040 us
  local copies, waits for them, and re-layouts  443 us (42%)
  waiting for transfers between devices  308 us (29%)
  other arithmetic  137 us (13%)
  matrix products  77.2 us (7%)
  blocking collectives  38.3 us (4%)
  starting transfers between devices  21.6 us (2%)
  between operations  16.6 us (2%)
    unnamed x485, local copies, waits for them, and re-layouts  106 us
    all_to_all x1, waiting for transfers between devices, body(): lax.all_to_all(state_stack, 'seq', split_axis=2, concat_axis=3, tiled=True)  92.6 us
    psum x1, waiting for transfers between devices, body(): lax.psum((scaled_grad, out_stack_grad, value_weight_grad, gate_weight_gra...  80.5 us
    all_to_all x1, waiting for transfers between devices, body(): lax.all_to_all(grad_state, 'seq', split_axis=3, concat_axis=2, tiled=True)  75.4 us
    slice x8, local copies, waits for them, and re-layouts, serial_scan(): current = tuple((item[:, place] for item in elements))  63.2 us
    unnamed x42, other arithmetic  58.1 us
    convert_element_type x4, local copies, waits for them, and re-layouts, to_lanes(): stacked.transpose(0, 2, 1, 3).reshape(2, length, lanes).astype(jnp.float32)  39 us
    psum x1, blocking collectives, body(): lax.psum((scaled_grad, out_stack_grad, value_weight_grad, gate_weight_gra...  38.3 us
  transfers between devices with their start and end apart: 5, of which 5 were waited for; matrix products, arithmetic and copies ran while one was open for 16% of the time, Pallas kernels for 0%

commit v1 on v0

v1 whole, which is shorter than its diff:
```python
import functools

import jax
import jax.numpy as jnp
from jax import lax
from jax.experimental import pallas as pl
from jax.experimental.pallas import tpu as pltpu
from jax.sharding import PartitionSpec as P

EPSILON = 1e-05
SEGMENTS = 16
SUBLANES = 8
LANES = 128
F32 = jnp.float32
BF16 = jnp.bfloat16
VMEM_LIMIT = 60 * 1024 * 1024


def nt_dot(left, right):
    return lax.dot_general(
        left, right, (((1,), (1,)), ((), ())), preferred_element_type=F32
    )


def nn_dot(left, right):
    return lax.dot_general(
        left, right, (((1,), (0,)), ((), ())), preferred_element_type=F32
    )


def tn_dot(left, right):
    return lax.dot_general(
        left, right, (((0,), (0,)), ((), ())), preferred_element_type=F32
    )


def rows_of(step, half, span):
    return pl.ds(step + half * SUBLANES * span, SUBLANES, stride=span)


def fill_keep(lens_ref, row, shift, keep, segs, span):
    toks = keep.shape[0]
    docs = lens_ref.shape[1]
    keep[...] = jnp.ones_like(keep)
    segs[...] = jnp.ones_like(segs)
    start = -shift
    for j in range(docs):

        @pl.when((start >= 0) & (start < toks))
        def _(start=start):
            keep[pl.ds(start, 1), :] = jnp.zeros((1, keep.shape[1]), F32)
            segs[pl.ds(start // span, 1), :] = jnp.zeros((1, segs.shape[1]), F32)

        start = start + lens_ref[row, j]


def power_of(real, imag, times):
    while times > 1:
        real, imag = real * real - imag * imag, 2.0 * real * imag
        times //= 2
    return real, imag


def to_blocks(work, part, value):
    for b in range(work.shape[0]):
        work[b, part, :] = value[:, b * LANES : (b + 1) * LANES]


def from_blocks(work, part):
    return jnp.concatenate([work[b, part, :] for b in range(work.shape[0])], axis=1)


def lane_blocks(vector, sign=1.0):
    n = vector.shape[1]
    return [
        jnp.broadcast_to(sign * vector[:, b * LANES : (b + 1) * LANES], (SUBLANES, LANES))
        for b in range(n // LANES)
    ]


def segment_ends(work, keep, real, imag, ends, span, reverse):
    groups = SEGMENTS // SUBLANES
    half = len(real)
    n = half * LANES
    zero = jnp.zeros((SUBLANES, LANES), F32)

    def body(i, carry):
        t = span - 1 - i if reverse else i
        out = []
        at = 0
        for g in range(groups):
            rows = rows_of(t, g, span)
            k = keep[rows, :]
            for b in range(half):
                sr, si = carry[at], carry[at + 1]
                at += 2
                ar, ai = k * real[b], k * imag[b]
                out.append((ar * sr + work[b, rows, :]) - ai * si)
                out.append((ar * si + work[half + b, rows, :]) + ai * sr)
        return tuple(out)

    final = lax.fori_loop(0, span, body, (zero,) * (2 * groups * half), unroll=4)
    at = 0
    for g in range(groups):
        for b in range(half):
            lanes = slice(b * LANES, (b + 1) * LANES)
            ends[g * SUBLANES : (g + 1) * SUBLANES, lanes] = final[at]
            lanes = slice(n + b * LANES, n + (b + 1) * LANES)
            ends[g * SUBLANES : (g + 1) * SUBLANES, lanes] = final[at + 1]
            at += 2


def starting_states(inits, half):
    n = half * LANES
    begin = []
    for g in range(SEGMENTS // SUBLANES):
        for b in range(half):
            for base in (0, n):
                lanes = slice(base + b * LANES, base + (b + 1) * LANES)
                begin.append(inits[g * SUBLANES : (g + 1) * SUBLANES, lanes])
    return tuple(begin)


def compose_segments(ends, segs, real, imag, span, start_real, start_imag, inits, reverse):
    n = real.shape[1]
    pr, pi = power_of(real, imag, span)
    cr, ci = start_real, start_imag
    order = range(SEGMENTS - 1, -1, -1) if reverse else range(SEGMENTS)
    for s in order:
        if inits is not None:
            inits[s : s + 1, 0:n] = cr
            inits[s : s + 1, n : 2 * n] = ci
        k = segs[s : s + 1, :]
        ar, ai = k * pr, k * pi
        er, ei = ends[s : s + 1, 0:n], ends[s : s + 1, n : 2 * n]
        cr, ci = (ar * cr + er) - ai * ci, (ar * ci + ei) + ai * cr
    return cr, ci


def forward_kernel(
    lens, first, x_ref, gain, bias, scaled, lam, drive_ref, xhat_ref, rstd_ref, ends_ref,
    fin_ref, work, keep, segs
):
    row = pl.program_id(0)
    toks = x_ref.shape[1]
    n = lam.shape[1]
    span = toks // SEGMENTS
    fill_keep(lens, row, first[0], keep, segs, span)
    chunk = 256
    for c in range(toks // chunk):
        part = slice(c * chunk, (c + 1) * chunk)
        x = x_ref[0, part, :].astype(F32)
        cent = x - jnp.mean(x, axis=-1, keepdims=True)
        rstd = lax.rsqrt(jnp.mean(cent * cent, axis=-1, keepdims=True) + EPSILON)
        xhat = cent * rstd
        rstd_ref[0, part, :] = jnp.broadcast_to(rstd, (chunk, rstd_ref.shape[2]))
        xhat_ref[0, part, :] = xhat.astype(BF16)
        low = (xhat * gain[...] + bias[...]).astype(BF16)
        drive = nt_dot(low, scaled[...]).astype(BF16)
        drive_ref[0, part, :] = drive
        to_blocks(work, part, drive.astype(F32))
    real, imag = lam[0:1, :], lam[1:2, :]
    ends = ends_ref.at[0]
    segment_ends(work, keep, lane_blocks(real), lane_blocks(imag), ends, span, False)
    zero = jnp.zeros((1, n), F32)
    cr, ci = compose_segments(ends, segs, real, imag, span, zero, zero, None, False)
    fin_ref[0, :, 0:n] = cr
    fin_ref[0, :, n : 2 * n] = ci


TAIL_P = 0.3275911 * 0.7071067811865476
TAIL = (0.254829592, -0.284496736, 1.421413741, -1.453152027, 1.061405429)


def gelu_parts(m):
    bell = jnp.exp(-0.5 * m * m)
    t = 1.0 / (1.0 + TAIL_P * jnp.abs(m))
    poly = t * (0.5 * TAIL[0] + t * (0.5 * TAIL[1] + t * (0.5 * TAIL[2] + t * (0.5 * TAIL[3] + t * (0.5 * TAIL[4])))))
    tail = poly * bell
    return jnp.where(m < 0, tail, 1.0 - tail), bell


def middle_kernel(
    lens, first, drive_ref, ends_ref, carry_ref, xhat_ref, x_ref, og_ref, lam, out_cat, gain,
    bias, skip, wv, wg, gbias, block_ref, gm_ref, gs_ref, st_ref, bends_ref, bfin_ref, wglu_ref,
    wout_ref, gbias_ref, sums_ref, work, keep, segs, inits, act_s, gvg_s
):
    row = pl.program_id(0)
    toks, width = x_ref.shape[1], x_ref.shape[2]
    n = lam.shape[1]
    span = toks // SEGMENTS
    groups = SEGMENTS // SUBLANES

    @pl.when(row == 0)
    def _():
        wglu_ref[...] = jnp.zeros_like(wglu_ref)
        wout_ref[...] = jnp.zeros_like(wout_ref)
        gbias_ref[...] = jnp.zeros_like(gbias_ref)
        sums_ref[...] = jnp.zeros_like(sums_ref)

    fill_keep(lens, row, first[0], keep, segs, span)
    everything = slice(0, toks)
    to_blocks(work, everything, drive_ref[0].astype(F32))
    real, imag = lam[0:1, :], lam[1:2, :]
    half = n // LANES
    real_b, imag_b = lane_blocks(real), lane_blocks(imag)
    compose_segments(
        ends_ref.at[0], segs, real, imag, span, carry_ref[0, :, 0:n],
        carry_ref[0, :, n : 2 * n], inits, False
    )

    def body(t, carry):
        out = []
        at = 0
        for g in range(groups):
            rows = rows_of(t, g, span)
            k = keep[rows, :]
            for b in range(half):
                sr, si = carry[at], carry[at + 1]
                at += 2
                ar, ai = k * real_b[b], k * imag_b[b]
                nr = (ar * sr + work[b, rows, :]) - ai * si
                ni = (ar * si + work[half + b, rows, :]) + ai * sr
                work[b, rows, :] = nr
                work[half + b, rows, :] = ni
                out += [nr, ni]
        return tuple(out)

    lax.fori_loop(0, span, body, starting_states(inits, half), unroll=4)

    docs = lens.shape[1]
    limit = -first[0]
    for j in range(docs - 1):
        limit = limit + lens[row, j]
    chunk = 256
    ones = jnp.ones((SUBLANES, chunk), BF16)

    @pl.loop(0, toks // chunk)
    def _(c):
        part = pl.ds(pl.multiple_of(c * chunk, chunk), chunk)
        state = from_blocks(work, part).astype(BF16)
        st_ref[0, part, :] = state
        xhat = xhat_ref[0, part, :].astype(F32)
        mixed = nt_dot(state, out_cat[...]) + (xhat * (gain[...] * skip[...]) + bias[...] * skip[...])
        cdf, bell = gelu_parts(mixed)
        act = (mixed * cdf).astype(BF16)
        act_s[part, :] = act
        slope = cdf + mixed * (bell * 0.3989422804014327)
        value = nn_dot(act, wv[...]) + gbias[:, 0:width]
        gate = nn_dot(act, wg[...]) + gbias[:, width : 2 * width]
        sigma = 0.5 * jnp.tanh(0.5 * gate) + 0.5
        gated = value * sigma
        block_ref[0, part, :] = (x_ref[0, part, :].astype(F32) + gated).astype(BF16)
        place = lax.broadcasted_iota(jnp.int32, (chunk, width), 0) + c * chunk
        grad = jnp.where(place < limit, og_ref[0, part, :].astype(F32), 0.0)
        gv = (grad * sigma).astype(BF16)
        gg = (grad * gated * (1.0 - sigma)).astype(BF16)
        gvg_s[part, 0:width] = gv
        gvg_s[part, width : 2 * width] = gg
        gbias_ref[0:1, 0:width] += jnp.sum(gv.astype(F32), axis=0, keepdims=True)
        gbias_ref[0:1, width : 2 * width] += jnp.sum(gg.astype(F32), axis=0, keepdims=True)
        gact = nt_dot(gv, wv[...]) + nt_dot(gg, wg[...])
        gm = (gact * slope).astype(BF16)
        gm_ref[0, part, :] = gm
        gmf = gm.astype(F32)
        sums_ref[0:1, :] += jnp.sum(gmf, axis=0, keepdims=True)
        sums_ref[1:2, :] += jnp.sum(gmf * xhat, axis=0, keepdims=True)
        gs = nn_dot(gm, out_cat[...]).astype(BF16)
        gs_ref[0, part, :] = gs
        to_blocks(work, part, gs.astype(F32))

    wglu_ref[...] += tn_dot(act_s[...], gvg_s[...])
    wout_ref[...] += tn_dot(gm_ref[0], st_ref[0])

    fill_keep(lens, row, first[0] + 1, keep, segs, span)
    bends = bends_ref.at[0]
    segment_ends(work, keep, real_b, lane_blocks(imag, -1.0), bends, span, True)
    zero = jnp.zeros((1, n), F32)
    cr, ci = compose_segments(bends, segs, real, -imag, span, zero, zero, None, True)
    bfin_ref[0, :, 0:n] = cr
    bfin_ref[0, :, n : 2 * n] = ci


def backward_kernel(
    lens, first, gs_ref, bends_ref, carry_ref, st_ref, xhat_ref, gm_ref, og_ref, rstd_ref, lam,
    scaled, gain, skip, ig_ref, wg_ref, col_ref, lamg_ref, work, state, keep, segs, inits
):
    row = pl.program_id(0)
    toks, width = xhat_ref.shape[1], xhat_ref.shape[2]
    n = lam.shape[1]
    span = toks // SEGMENTS
    groups = SEGMENTS // SUBLANES

    @pl.when(row == 0)
    def _():
        wg_ref[...] = jnp.zeros_like(wg_ref)
        col_ref[...] = jnp.zeros_like(col_ref)
        lamg_ref[...] = jnp.zeros_like(lamg_ref)

    fill_keep(lens, row, first[0] + 1, keep, segs, span)
    everything = slice(0, toks)
    to_blocks(work, everything, gs_ref[0].astype(F32))
    to_blocks(state, everything, st_ref[0].astype(F32))
    real, imag = lam[0:1, :], -lam[1:2, :]
    half = n // LANES
    real_b, imag_b = lane_blocks(real), lane_blocks(imag)
    compose_segments(
        bends_ref.at[0], segs, real, imag, span, carry_ref[0, :, 0:n],
        carry_ref[0, :, n : 2 * n], inits, True
    )
    n_states = 2 * groups * half

    def body(i, carry):
        t = span - 1 - i
        out = []
        tot = list(carry[n_states:])
        at = 0
        for g in range(groups):
            rows = rows_of(t, g, span)
            k = keep[rows, :]
            for b in range(half):
                sr, si = carry[at], carry[at + 1]
                at += 2
                ur, ui = k * sr, k * si
                nr = (real_b[b] * ur + work[b, rows, :]) - imag_b[b] * ui
                ni = (real_b[b] * ui + work[half + b, rows, :]) + imag_b[b] * ur
                work[b, rows, :] = nr
                work[half + b, rows, :] = ni
                hr, hi = state[b, rows, :], state[half + b, rows, :]
                tot[4 * b] = tot[4 * b] + (ur * hr + ui * hi)
                tot[4 * b + 1] = tot[4 * b + 1] + (ui * hr - ur * hi)
                tot[4 * b + 2] = tot[4 * b + 2] + nr
                tot[4 * b + 3] = tot[4 * b + 3] + ni
                out += [nr, ni]
        return tuple(out) + tuple(tot)

    zero8 = jnp.zeros((SUBLANES, LANES), F32)
    final = lax.fori_loop(
        0, span, body, starting_states(inits, half) + (zero8,) * (4 * half), unroll=2
    )
    tot = final[n_states:]
    for b in range(half):
        low_lanes = slice(b * LANES, (b + 1) * LANES)
        high_lanes = slice(n + b * LANES, n + (b + 1) * LANES)
        lamg_ref[:, low_lanes] += tot[4 * b]
        lamg_ref[:, high_lanes] += tot[4 * b + 1]
        col_ref[:, low_lanes] += tot[4 * b + 2]
        col_ref[:, high_lanes] += tot[4 * b + 3]

    docs = lens.shape[1]
    limit = -first[0]
    for j in range(docs - 1):
        limit = limit + lens[row, j]
    adj = from_blocks(work, everything).astype(BF16)
    wg_ref[...] += tn_dot(adj, xhat_ref[0])
    chunk = 256
    mix = gain[...] * skip[...]

    @pl.loop(0, toks // chunk)
    def _(c):
        part = pl.ds(pl.multiple_of(c * chunk, chunk), chunk)
        low = from_blocks(work, part).astype(BF16)
        xhat = xhat_ref[0, part, :].astype(F32)
        g = nn_dot(low, scaled[...]) * gain[...] + gm_ref[0, part, :].astype(F32) * mix
        place = lax.broadcasted_iota(jnp.int32, (chunk, width), 0) + c * chunk
        grad = jnp.where(place < limit, og_ref[0, part, :].astype(F32), 0.0)
        m1 = jnp.mean(g, axis=-1, keepdims=True)
        m2 = jnp.mean(g * xhat, axis=-1, keepdims=True)
        ig_ref[0, part, :] = (grad + rstd_ref[0, part, 0:1] * (g - m1 - xhat * m2)).astype(BF16)


def whole(shape):
    return pl.BlockSpec(shape, lambda r: (0,) * len(shape))


def per_row(*shape):
    return pl.BlockSpec((1,) + shape, lambda r: (r,) + (0,) * len(shape))


SCALARS = pl.BlockSpec(memory_space=pltpu.SMEM)


def carry_over(fin, through, axis, parts, hops, reverse):
    def shift(v):
        pairs = [(i, i + 1) for i in range(parts - 1)]
        if reverse:
            pairs = [(b, a) for a, b in pairs]
        return lax.ppermute(v, axis, pairs)

    if hops == 1:
        return shift(fin)
    n = fin.shape[-1] // 2
    total = shift(fin)
    for _ in range(hops - 1):
        tr, ti = through[..., :n], through[..., n:]
        sr, si = total[..., :n], total[..., n:]
        passed = jnp.concatenate([tr * sr - ti * si, tr * si + ti * sr], axis=-1)
        total = shift(fin + passed)
    return total


def all_sum(v):
    return lax.psum(v, ("rows", "seq"))


def body(
    tokens_in, layer_norm_gain, layer_norm_bias, input_real, input_imag, decay_log, angle_log,
    scale_log, output_real, output_imag, skip_gain, glu_value, glu_gate, glu_bias, doc_lengths,
    out_grad
):
    rows_here, toks, width = tokens_in.shape
    n = input_real.shape[0]
    parts = lax.axis_size("seq")
    seat = lax.axis_index("seq")
    length = toks * parts
    hops = max(1, (length // 4) // toks)
    first = (seat * toks).astype(jnp.int32).reshape(1)
    rate = jnp.exp(decay_log)
    radius = jnp.exp(-rate)
    angle = jnp.exp(angle_log)
    cosine, sine = jnp.cos(angle), jnp.sin(angle)
    norm_root = jnp.sqrt(1.0 - jnp.exp(-2.0 * rate))
    scale = jnp.exp(scale_log) * norm_root
    lam = jnp.stack([radius * cosine, radius * sine])
    inputs = jnp.concatenate([input_real, input_imag], axis=0).astype(F32)
    scale2 = jnp.concatenate([scale, scale])
    scaled = (inputs * scale2[:, None]).astype(BF16)
    out_cat = jnp.concatenate([output_real, -output_imag], axis=1)
    gain, bias, skip = layer_norm_gain[None], layer_norm_bias[None], skip_gain[None]
    gbias = glu_bias[None]
    params = pltpu.CompilerParams(
        dimension_semantics=("arbitrary",), vmem_limit_bytes=VMEM_LIMIT
    )
    act = per_row(toks, width)
    sds = jax.ShapeDtypeStruct
    big = sds((rows_here, toks, width), BF16)
    drive, xhat, rstd, ends, fin = pl.pallas_call(
        forward_kernel,
        grid=(rows_here,),
        in_specs=[SCALARS, SCALARS, act, whole((1, width)), whole((1, width)),
                  whole((2 * n, width)), whole((2, n))],
        out_specs=[per_row(toks, 2 * n), act, per_row(toks, 128), per_row(SEGMENTS, 2 * n),
                   per_row(1, 2 * n)],
        out_shape=[sds((rows_here, toks, 2 * n), BF16), big, sds((rows_here, toks, 128), F32),
                   sds((rows_here, SEGMENTS, 2 * n), F32), sds((rows_here, 1, 2 * n), F32)],
        scratch_shapes=[pltpu.VMEM((2 * n // LANES, toks, LANES), F32), pltpu.VMEM((toks, LANES), F32),
                        pltpu.VMEM((SEGMENTS, n), F32)],
        compiler_params=params,
        name="forward",
    )(doc_lengths, first, tokens_in, gain, bias, scaled, lam)

    through = None
    back_through = None
    if hops > 1:
        starts = jnp.cumsum(doc_lengths, axis=1) - doc_lengths
        here = (starts >= first[0]) & (starts < first[0] + toks)
        clear = jnp.where(jnp.any(here, axis=1), 0.0, 1.0).astype(F32)
        here_next = (starts >= first[0] + 1) & (starts < first[0] + toks + 1)
        clear_next = jnp.where(jnp.any(here_next, axis=1), 0.0, 1.0).astype(F32)
        far = jnp.exp(-rate * toks)
        fr, fi = power_of(lam[0], lam[1], toks)
        through = clear[:, None, None] * jnp.concatenate([fr, fi])[None, None]
        back_through = clear_next[:, None, None] * jnp.concatenate([fr, -fi])[None, None]
    carry = carry_over(fin, through, "seq", parts, hops, False)

    block_out, gm, gs, st, bends, bfin, wglu, wout, gbias_g, sums = pl.pallas_call(
        middle_kernel,
        grid=(rows_here,),
        in_specs=[SCALARS, SCALARS, per_row(toks, 2 * n), per_row(SEGMENTS, 2 * n),
                  per_row(1, 2 * n), act, act, act, whole((2, n)), whole((width, 2 * n)),
                  whole((1, width)), whole((1, width)), whole((1, width)),
                  whole((width, width)), whole((width, width)), whole((1, 2 * width))],
        out_specs=[act, act, per_row(toks, 2 * n), per_row(toks, 2 * n),
                   per_row(SEGMENTS, 2 * n), per_row(1, 2 * n), whole((width, 2 * width)),
                   whole((width, 2 * n)), whole((1, 2 * width)), whole((2, width))],
        out_shape=[big, big, sds((rows_here, toks, 2 * n), BF16),
                   sds((rows_here, toks, 2 * n), BF16), sds((rows_here, SEGMENTS, 2 * n), F32),
                   sds((rows_here, 1, 2 * n), F32), sds((width, 2 * width), F32),
                   sds((width, 2 * n), F32), sds((1, 2 * width), F32), sds((2, width), F32)],
        scratch_shapes=[pltpu.VMEM((2 * n // LANES, toks, LANES), F32), pltpu.VMEM((toks, LANES), F32),
                        pltpu.VMEM((SEGMENTS, n), F32), pltpu.VMEM((SEGMENTS, 2 * n), F32),
                        pltpu.VMEM((toks, width), BF16), pltpu.VMEM((toks, 2 * width), BF16)],
        compiler_params=params,
        name="middle",
    )(doc_lengths, first, drive, ends, carry, xhat, tokens_in, out_grad, lam, out_cat, gain,
      bias, skip, glu_value, glu_gate, gbias)

    back_carry = carry_over(bfin, back_through, "seq", parts, hops, True)

    input_grad, win, col, lamg = pl.pallas_call(
        backward_kernel,
        grid=(rows_here,),
        in_specs=[SCALARS, SCALARS, per_row(toks, 2 * n), per_row(SEGMENTS, 2 * n),
                  per_row(1, 2 * n), per_row(toks, 2 * n), act, act, act, per_row(toks, 128),
                  whole((2, n)), whole((2 * n, width)), whole((1, width)), whole((1, width))],
        out_specs=[act, whole((2 * n, width)), whole((SUBLANES, 2 * n)),
                   whole((SUBLANES, 2 * n))],
        out_shape=[big, sds((2 * n, width), F32), sds((SUBLANES, 2 * n), F32),
                   sds((SUBLANES, 2 * n), F32)],
        scratch_shapes=[pltpu.VMEM((2 * n // LANES, toks, LANES), F32), pltpu.VMEM((2 * n // LANES, toks, LANES), F32),
                        pltpu.VMEM((toks, LANES), F32), pltpu.VMEM((SEGMENTS, n), F32),
                        pltpu.VMEM((SEGMENTS, 2 * n), F32)],
        compiler_params=params,
        name="backward",
    )(doc_lengths, first, gs, bends, back_carry, st, xhat, gm, out_grad, rstd, lam, scaled, gain,
      skip)

    wglu, wout, gbias_g, sums, win, col, lamg = all_sum(
        (wglu, wout, gbias_g, sums, win, jnp.sum(col, axis=0), jnp.sum(lamg, axis=0))
    )
    scaled_f = scaled.astype(F32)
    gain_grad = jnp.sum(scaled_f * win, axis=0) + skip_gain * sums[1]
    shift_grad = jnp.sum(scaled_f * col[:, None], axis=0) + skip_gain * sums[0]
    skip_grad = layer_norm_gain * sums[1] + layer_norm_bias * sums[0]
    scaled_total = win * layer_norm_gain[None] + col[:, None] * layer_norm_bias[None]
    in_grad = scaled_total * scale2[:, None]
    per_state = jnp.sum(scaled_total * inputs, axis=1)
    scale_grad = per_state[:n] + per_state[n:]
    lr, li = lamg[:n], lamg[n:]
    radius_grad = lr * cosine + li * sine
    angle_grad = radius * (li * cosine - lr * sine) * angle
    decay_grad = (
        -radius_grad * radius * rate
        + scale_grad * jnp.exp(scale_log) * jnp.exp(-2.0 * rate) * rate / norm_root
    )
    return (
        block_out, input_grad, gain_grad, shift_grad, in_grad[:n], in_grad[n:], decay_grad,
        angle_grad, scale_grad * scale, wout[:, :n], -wout[:, n:], skip_grad,
        wglu[:, :width], wglu[:, width:], gbias_g[0]
    )


def solution(mesh):
    tokens = P("rows", "seq", None)
    placed = (tokens,) + (P(),) * 13 + (P("rows", None), tokens)
    return jax.shard_map(
        body, mesh=mesh, in_specs=placed, out_specs=(tokens, tokens) + (P(),) * 13,
        check_vma=False,
    )
```

time: 1060 us -> 315 us (0.30); the launches traced: 1040 us -> 315 us
  local copies, waits for them, and re-layouts: 443 us -> 4.41 us
  waiting for transfers between devices: 308 us -> 108 us
  Pallas kernels: 0 us -> 132 us
  other arithmetic: 137 us -> 8.49 us
  matrix products: 77.2 us -> 0 us
  starting transfers between devices: 21.6 us -> 6.27 us
    all_to_all x4 -> x0, waiting for transfers between devices: 228 us -> none  [the longest x1 92.6 us: body(): lax.all_to_all(state_stack, 'seq', split_axis=2, concat_axis=3, tiled=True)]
    pallas_call x0 -> x3, Pallas kernels: none -> 132 us  [the longest x1 71.1 us: body(): pl.pallas_call(middle_kernel, grid=(rows_here,), in_specs=[SCALARS, SCALA...]
    slice x19 -> x3, local copies, waits for them, and re-layouts: 113 us -> 2.54 us  [the longest x1 1.51 us: body(): wglu[:, width:]]
    unnamed x485 -> x38, local copies, waits for them, and re-layouts: 106 us -> 1.87 us
    dot_general x12 -> x0, matrix products: 77.2 us -> none  [the longest x1 12.7 us: body(): jnp.einsum('prtn,pnh->rth', adjoint_low, scaled, preferred_element_type=j...]
    add x10 -> x0, local copies, waits for them, and re-layouts: 64.4 us -> none  [the longest x5 33.1 us: compose(): late_add_imag + moved_imag]
    unnamed x42 -> x0, other arithmetic: 58.1 us -> none
    another operation x20 -> x0, local copies, waits for them, and re-layouts: 53.2 us -> none  [the longest x4 34.6 us: block_scan(): item.reshape(outer * groups, block, lanes_count)]
  transfers between devices with their start and end apart: 5 -> 3, of which waited for: 5 -> 3; matrix products, arithmetic and copies ran while one was open for 16% -> 0% of each run, Pallas kernels for 0% -> 0%
where the time goes in v1:
time: 315 us
  Pallas kernels  132 us (42%)
  waiting for transfers between devices  108 us (34%)
  blocking collectives  41.8 us (13%)
  between operations  14.3 us (5%)
  other arithmetic  8.49 us (3%)
  starting transfers between devices  6.27 us (2%)
  local copies, waits for them, and re-layouts  4.41 us (1%)
    psum x1, waiting for transfers between devices, all_sum(): return lax.psum(v, ('rows', 'seq'))  102 us
    pallas_call x1, Pallas kernels, body(): pl.pallas_call(middle_kernel, grid=(rows_here,), in_specs=[SCALARS, SCALA...  71.1 us
    pallas_call x1, Pallas kernels, body(): pl.pallas_call(backward_kernel, grid=(rows_here,), in_specs=[SCALARS, SCA...  44.3 us
    psum x1, blocking collectives, all_sum(): return lax.psum(v, ('rows', 'seq'))  41.8 us
    pallas_call x1, Pallas kernels, body(): pl.pallas_call(forward_kernel, grid=(rows_here,), in_specs=[SCALARS, SCAL...  16.4 us
  transfers between devices with their start and end apart: 3, of which 3 were waited for; matrix products, arithmetic and copies ran while one was open for 0% of the time, Pallas kernels for 0%

profile of v1, /device:TPU:0, one launch (start us, length us, event | category | flops | bytes accessed | tf_op | source)
XLA Modules:
  0.0 314.7 jit_solution(4749064207017121985)
XLA Ops:
  7.2 0.0 copy-start.5
  7.2 0.0 copy-start.6
  7.2 0.0 all-reduce.4.cloned.1.call-start
  7.2 0.8 fusion.6
  8.1 0.6 pad_maximum_fusion.3.lam
  8.7 2.0 fusion.scaled
  10.7 16.4 %forward.1 = (bf16[4,1024,512]{2,1,0:T(8,128)(2,1)}, bf16[4,1024,512]{2,1,0:T(8,128)(2,1)}, f32[4,1024,128]{2,1,0:T(8,128)}, f32[4,16,512]{2,1,0:T(8,128)}, f32[4,1,512]{2,1,0:T(1,128)}) custom-call(s32[4,8]{1,0:T(4,128)} %lens.5, s32[1]{0:T(128)} %bitcast.first, bf16[4,1024,512]{2,1,0:T(8,128)(2,1)} %x_ref.3, f32[1,512]{1,0:T(1,128)} %bitcast.10, ...), custom_call_target="tpu_custom_call" | custom-call | tf_op jit(solution)/shard_map/forward/pallas_call | solution.py:437
  27.1 4.9 %collective-permute-start = (f32[4,1,512]{2,1,0:T(1,128)}, f32[4,1,512]{2,1,0:T(1,128)S(1)}, u32[]{:S(2)}, u32[]{:S(2)}) collective-permute-start(f32[4,1,512]{2,1,0:T(1,128)} %get-tuple-element.36), channel_id=1, source_target_pairs={{0,1},{1,2},{2,3},{4,5},{5,6},{6,7},{8,9},{9,10},{10,11},{12,13},{... | collective-permute-start | bytes 24584 | tf_op jit(solution)/shard_map/ppermute | solution.py:388
  32.0 0.0 copy-done.5
  32.1 0.0 copy-done.6
  32.1 0.8 pad_maximum_fusion.1.out_cat
  32.9 0.7 collective-permute-done.carry_ref
  33.6 0.6 copy-done.12
  34.2 71.1 %middle.1 = (bf16[4,1024,512]{2,1,0:T(8,128)(2,1)}, bf16[4,1024,512]{2,1,0:T(8,128)(2,1)}, bf16[4,1024,512]{2,1,0:T(8,128)(2,1)}, bf16[4,1024,512]{2,1,0:T(8,128...) custom-call(s32[4,8]{1,0:T(4,128)} %lens.5, ...), custom_call_target="tpu_custom_call" | custom-call | tf_op jit(solution)/shard_map/middle/pallas_call | solution.py:466
  105.3 1.3 collective-permute-start.1
  106.6 4.7 %collective-permute-done.1.carry_ref = f32[4,1,512]{2,1,0:T(1,128)S(1)} collective-permute-done((f32[4,1,512]{2,1,0:T(1,128)}, f32[4,1,512]{2,1,0:T(1,128)S(1)}, u32[]{:S(2)}, u32[]{:S(2)}) %collective-permute-start.1) | collective-permute-done | bytes 8224 | tf_op jit(solution)/shard_map/ppermute | solution.py:388
  111.3 0.6 copy-done.13
  111.9 44.3 %backward.1 = (bf16[4,1024,512]{2,1,0:T(8,128)(2,1)}, f32[512,512]{1,0:T(8,128)}, f32[8,512]{1,0:T(8,128)}, f32[8,512]{1,0:T(8,128)}) custom-call(s32[4,8]{1,0:T(4,128)} %lens.5, s32[1]{0:T(128)} %bitcast.first, bf16[4,1024,512]{2,1,0:T(8,128)(2,1)} %get-tuple-element.39.gs_ref, f32[4,16,512]{2,1,0:T(8,128)} %get-tuple-element.40.bends_ref, ...), custom_call_target="tpu_custom_call" | custom-call | tf_op jit(solution)/shard_map/backward/pallas_call | solution.py:490
  156.2 0.0 copy-start.11
  156.3 0.0 copy-start.10
  156.3 0.0 copy-start.14
  156.3 0.0 copy-start.15
  156.3 0.0 copy-start
  156.3 0.0 copy-start.3
  156.3 0.0 copy-start.4
  156.3 0.0 copy-start.7
  156.3 0.0 copy-start.8
  156.3 0.0 all-reduce.4.cloned.1.call-update
  156.4 0.6 copy-done.11
  157.0 0.0 copy-done.10
  157.0 0.0 copy-done.14
  157.0 0.0 copy-done.15
  157.0 41.8 %all-reduce = (f32[512]{0:T(512)S(1)}, f32[2,512]{1,0:T(2,128)S(1)}, f32[512]{0:T(512)S(1)}, f32[1024]{0:T(1024)}) all-reduce(f32[512]{0:T(512)S(1)} %reduce_sum.46, f32[2,512]{1,0:T(2,128)S(1)} %copy-done.15, f32[512]{0:T(512)S(1)} %reduce_sum.48, f32[1024]{0:T(1024)S(1)} %bitcast.19), channel_id=1, replica_groups=mesh['rows'=8,'seq'=4] {'rows','seq'}, use_global_device_ids=true, to_apply=%region_4.0 | all-reduce | flops 3072 | bytes 24576 | tf_op jit(solution)/shard_map/psum | solution.py:403
  198.8 102.2 %all-reduce.4.cloned.1.call-done = (f32[512,512]{1,0:T(8,128)}, f32[512,512]{1,0:T(8,128)}, f32[512,1024]{1,0:T(8,128)}) async-done(((f32[512,512]{1,0:T(8,128)}, f32[512,512]{1,0:T(8,128)}, f32[512,1024]{1,0:T(8,128)}), (f32[512,512]{1,0:T(8,128)}, f32[512,512]{1,0:T(8,128)}, f32[512,1024]{1,0:T(8,128)})) %all-reduce.4.cloned.1.call-update) | async-done | bytes 4194320 | tf_op jit(solution)/shard_map/psum | solution.py:403
  301.0 0.0 copy-done
  301.0 0.0 copy-done.3
  301.0 0.0 copy-done.4
  301.1 1.9 fusion.1
  303.0 0.0 copy-start.16
  303.0 0.0 copy-start.17
  303.0 0.0 copy-start.18
  303.0 0.0 copy-start.9
  303.1 1.0 fusion.10
  304.1 1.0 slice_negate_fusion
  305.1 1.5 fusion.9
  306.6 0.6 multiply_multiply_fusion
  307.3 0.0 copy-done.9
  307.3 0.6 multiply_add_fusion.1
  (16 shorter events, 0.1 us)
Async XLA Ops:
  7.2 24.8 %copy-start.5 = (bf16[512,256]{1,0:T(8,128)(2,1)S(1)}, bf16[512,256]{1,0:T(8,128)(2,1)}, u32[]{:S(2)}) copy-start(bf16[512,256]{1,0:T(8,128)(2,1)} %param.25) | copy-start | bytes 786436
  7.2 24.9 %copy-start.6 = (bf16[512,256]{1,0:T(8,128)(2,1)S(1)}, bf16[512,256]{1,0:T(8,128)(2,1)}, u32[]{:S(2)}) copy-start(bf16[512,256]{1,0:T(8,128)(2,1)} %param.24) | copy-start | bytes 786436
  7.2 293.8 %all-reduce.4.cloned.1.call-start = ((), (), s32[]{:S(2)}) async-start(), calls=%async_computation | async-start | bytes 8388608 | tf_op jit(solution)/shard_map/psum | solution.py:403
  27.1 6.5 %collective-permute-start = (f32[4,1,512]{2,1,0:T(1,128)}, f32[4,1,512]{2,1,0:T(1,128)S(1)}, u32[]{:S(2)}, u32[]{:S(2)}) collective-permute-start(f32[4,1,512]{2,1,0:T(1,128)} %get-tuple-element.36), channel_id=1, source_target_pairs={{0,1},{1,2},{2,3},{4,5},{5,6},{6,7},{8,9},{9,10},{10,11},{12,13},{... | collective-permute-start | bytes 24584 | tf_op jit(solution)/shard_map/ppermute | solution.py:388
  33.6 0.6 copy-start.12
  105.3 6.0 %collective-permute-start.1 = (f32[4,1,512]{2,1,0:T(1,128)}, f32[4,1,512]{2,1,0:T(1,128)S(1)}, u32[]{:S(2)}, u32[]{:S(2)}) collective-permute-start(f32[4,1,512]{2,1,0:T(1,128)} %get-tuple-element.41), channel_id=1, source_target_pairs={{1,0},{2,1},{3,2},{5,4},{6,5},{7,6},{9,8},{10,9},{11,10},{13,12},{... | collective-permute-start | bytes 24584 | tf_op jit(solution)/shard_map/ppermute | solution.py:388
  111.3 0.6 copy-start.13
  156.2 0.7 copy-start.11
  156.3 0.7 copy-start.10
  156.3 0.7 copy-start.14
  156.3 0.7 copy-start.15
  156.3 144.7 %copy-start = (bf16[512,512]{1,0:T(8,128)(2,1)S(1)}, bf16[512,512]{1,0:T(8,128)(2,1)}, u32[]{:S(2)}) copy-start(bf16[512,512]{1,0:T(8,128)(2,1)} %fusion.scaled) | copy-start | bytes 1572868
  156.3 144.7 %copy-start.3 = (bf16[256,512]{1,0:T(8,128)(2,1)S(1)}, bf16[256,512]{1,0:T(8,128)(2,1)}, u32[]{:S(2)}) copy-start(bf16[256,512]{1,0:T(8,128)(2,1)} %param.20) | copy-start | bytes 786436
  156.3 144.7 %copy-start.4 = (bf16[256,512]{1,0:T(8,128)(2,1)S(1)}, bf16[256,512]{1,0:T(8,128)(2,1)}, u32[]{:S(2)}) copy-start(bf16[256,512]{1,0:T(8,128)(2,1)} %param.19) | copy-start | bytes 786436
  156.3 144.7 %copy-start.7 = (f32[512]{0:T(512)S(1)}, f32[512]{0:T(512)}, u32[]{:S(2)}) copy-start(f32[512]{0:T(512)} %param.17) | copy-start | bytes 6148
  156.3 144.7 %copy-start.8 = (f32[512]{0:T(512)S(1)}, f32[512]{0:T(512)}, u32[]{:S(2)}) copy-start(f32[512]{0:T(512)} %param.18) | copy-start | bytes 6148
  301.0 3.1 copy-start.2
  301.0 4.1 %copy-start.1 = (f32[512,1024]{1,0:T(8,128)S(1)}, f32[512,1024]{1,0:T(8,128)}, u32[]{:S(2)}) copy-start(f32[512,1024]{1,0:T(8,128)} %get-tuple-element.62) | copy-start | bytes 6291460
  303.0 3.6 %copy-start.16 = (f32[256]{0:T(256)S(1)}, f32[256]{0:T(256)}, u32[]{:S(2)}) copy-start(f32[256]{0:T(256)} %param.22) | copy-start | bytes 3076
  303.0 3.6 %copy-start.17 = (f32[256]{0:T(256)S(1)}, f32[256]{0:T(256)}, u32[]{:S(2)}) copy-start(f32[256]{0:T(256)} %param.21) | copy-start | bytes 3076
  303.0 3.6 %copy-start.18 = (f32[256]{0:T(256)S(1)}, f32[256]{0:T(256)}, u32[]{:S(2)}) copy-start(f32[256]{0:T(256)} %param.23) | copy-start | bytes 3076
  303.0 4.2 %copy-start.9 = (f32[512]{0:T(512)S(1)}, f32[512]{0:T(512)}, u32[]{:S(2)}) copy-start(f32[512]{0:T(512)} %param.26) | copy-start | bytes 6148
Sparse Core Ops, SparseCore 0:
  156.5 144.4 all-reduce.3

commit v2 on v1

v2 whole, which is shorter than its diff:
```python
import functools

import jax
import jax.numpy as jnp
from jax import lax
from jax.experimental import pallas as pl
from jax.experimental.pallas import tpu as pltpu
from jax.sharding import PartitionSpec as P

EPSILON = 1e-05
SEGMENTS = 16
SUBLANES = 8
LANES = 128
EXTRA = 16
F32 = jnp.float32
BF16 = jnp.bfloat16
VMEM_LIMIT = 60 * 1024 * 1024
GLUE_LIMIT = 16 * 1024 * 1024


def nt_dot(left, right):
    return lax.dot_general(
        left, right, (((1,), (1,)), ((), ())), preferred_element_type=F32
    )


def nn_dot(left, right):
    return lax.dot_general(
        left, right, (((1,), (0,)), ((), ())), preferred_element_type=F32
    )


def tn_dot(left, right):
    return lax.dot_general(
        left, right, (((0,), (0,)), ((), ())), preferred_element_type=F32
    )


def skewed_scan(step, inits, extra, span, reverse, ends=False):
    groups = SEGMENTS // SUBLANES
    per_group = len(inits) // groups
    seat = lax.broadcasted_iota(jnp.int32, (SUBLANES, LANES), 0)
    order = SUBLANES - 1 - seat if reverse else seat
    last = span + SUBLANES - 2

    def rows(i):
        base = last - i if reverse else i
        return [pl.ds(base + g * SUBLANES * span, SUBLANES, stride=span - 1) for g in range(groups)]

    states = list(inits)
    for i in range(SUBLANES):
        if i:
            states = [jnp.where(order == i, x, y) for x, y in zip(inits, states)]
        states, extra = step(rows(i), states, extra, order <= i)

    def body(i, carry):
        return step(rows(i), *carry, None)

    states, extra = lax.fori_loop(SUBLANES, span - 1, body, (states, extra), unroll=5)
    final = states
    for i in range(span - 1, last + 1):
        states, extra = step(rows(i), states, extra, order >= i - span + 1)
        if ends:
            final = [jnp.where(order == i - span + 1, x, y) for x, y in zip(states, final)]
    return final if ends else extra


def fill_keep(lens_ref, row, shift, keep, segs, span):
    toks = keep.shape[0]
    docs = lens_ref.shape[1]
    keep[...] = jnp.ones_like(keep)
    segs[...] = jnp.ones_like(segs)
    start = -shift
    for j in range(docs):

        @pl.when((start >= 0) & (start < toks))
        def _(start=start):
            keep[pl.ds(start, 1), :] = jnp.zeros((1, keep.shape[1]), F32)
            segs[pl.ds(start // span, 1), :] = jnp.zeros((1, segs.shape[1]), F32)

        start = start + lens_ref[row, j]


def power_of(real, imag, times):
    while times > 1:
        real, imag = real * real - imag * imag, 2.0 * real * imag
        times //= 2
    return real, imag


def to_blocks(work, part, value):
    for b in range(work.shape[0]):
        work[b, part, :] = value[:, b * LANES : (b + 1) * LANES]


def from_blocks(work, part):
    return jnp.concatenate([work[b, part, :] for b in range(work.shape[0])], axis=1)


def lane_blocks(vector, sign=1.0):
    n = vector.shape[1]
    return [
        jnp.broadcast_to(sign * vector[:, b * LANES : (b + 1) * LANES], (SUBLANES, LANES))
        for b in range(n // LANES)
    ]


def segment_ends(work, keep, real, imag, ends, span, reverse):
    groups = SEGMENTS // SUBLANES
    half = len(real)
    n = half * LANES
    zero = jnp.zeros((SUBLANES, LANES), F32)

    def step(rows, states, extra, live):
        out = []
        at = 0
        for g in range(groups):
            k = keep[rows[g], :]
            for b in range(half):
                sr, si = states[at], states[at + 1]
                at += 2
                ar, ai = k * real[b], k * imag[b]
                out.append((ar * sr + work[b, rows[g], :]) - ai * si)
                out.append((ar * si + work[half + b, rows[g], :]) + ai * sr)
        return out, extra

    final = skewed_scan(step, [zero] * (2 * groups * half), [], span, reverse, ends=True)
    at = 0
    for g in range(groups):
        for b in range(half):
            lanes = slice(b * LANES, (b + 1) * LANES)
            ends[g * SUBLANES : (g + 1) * SUBLANES, lanes] = final[at]
            lanes = slice(n + b * LANES, n + (b + 1) * LANES)
            ends[g * SUBLANES : (g + 1) * SUBLANES, lanes] = final[at + 1]
            at += 2


def starting_states(inits, half):
    n = half * LANES
    begin = []
    for g in range(SEGMENTS // SUBLANES):
        for b in range(half):
            for base in (0, n):
                lanes = slice(base + b * LANES, base + (b + 1) * LANES)
                begin.append(inits[g * SUBLANES : (g + 1) * SUBLANES, lanes])
    return begin


def compose_segments(ends, segs, real, imag, span, start_real, start_imag, inits, reverse):
    n = real.shape[1]
    pr, pi = power_of(real, imag, span)
    cr, ci = start_real, start_imag
    order = range(SEGMENTS - 1, -1, -1) if reverse else range(SEGMENTS)
    for s in order:
        if inits is not None:
            inits[s : s + 1, 0:n] = cr
            inits[s : s + 1, n : 2 * n] = ci
        k = segs[s : s + 1, :]
        ar, ai = k * pr, k * pi
        er, ei = ends[s : s + 1, 0:n], ends[s : s + 1, n : 2 * n]
        cr, ci = (ar * cr + er) - ai * ci, (ar * ci + ei) + ai * cr
    return cr, ci


def forward_kernel(
    lens, first, x_ref, gain, bias, scaled, lam, drive_ref, xhat_ref, rstd_ref, ends_ref,
    fin_ref, work, keep, segs
):
    row = pl.program_id(0)
    toks = x_ref.shape[1]
    n = lam.shape[1]
    span = toks // SEGMENTS
    fill_keep(lens, row, first[0], keep, segs, span)
    chunk = 256
    for c in range(toks // chunk):
        part = slice(c * chunk, (c + 1) * chunk)
        x = x_ref[0, part, :].astype(F32)
        cent = x - jnp.mean(x, axis=-1, keepdims=True)
        rstd = lax.rsqrt(jnp.mean(cent * cent, axis=-1, keepdims=True) + EPSILON)
        xhat = cent * rstd
        rstd_ref[0, part, :] = jnp.broadcast_to(rstd, (chunk, rstd_ref.shape[2]))
        xhat_ref[0, part, :] = xhat.astype(BF16)
        low = (xhat * gain[...] + bias[...]).astype(BF16)
        drive = nt_dot(low, scaled[...]).astype(BF16)
        drive_ref[0, part, :] = drive
        to_blocks(work, part, drive.astype(F32))
    real, imag = lam[0:1, :], lam[1:2, :]
    ends = ends_ref.at[0]
    segment_ends(work, keep, lane_blocks(real), lane_blocks(imag), ends, span, False)
    zero = jnp.zeros((1, n), F32)
    cr, ci = compose_segments(ends, segs, real, imag, span, zero, zero, None, False)
    fin_ref[0, :, 0:n] = cr
    fin_ref[0, :, n : 2 * n] = ci


TAIL_P = 0.3275911 * 0.7071067811865476
TAIL = (0.254829592, -0.284496736, 1.421413741, -1.453152027, 1.061405429)


def gelu_parts(m):
    bell = jnp.exp(-0.5 * m * m)
    t = 1.0 / (1.0 + TAIL_P * jnp.abs(m))
    poly = t * (0.5 * TAIL[0] + t * (0.5 * TAIL[1] + t * (0.5 * TAIL[2] + t * (0.5 * TAIL[3] + t * (0.5 * TAIL[4])))))
    tail = poly * bell
    return jnp.where(m < 0, tail, 1.0 - tail), bell


def middle_kernel(
    lens, first, drive_ref, ends_ref, carry_ref, xhat_ref, x_ref, og_ref, lam, out_cat, gain,
    bias, skip, wv, wg, gbias, block_ref, gm_ref, gs_ref, st_ref, bends_ref, bfin_ref, mine_ref,
    send_ref, gbias_ref, sums_ref, work, keep, segs, done, inits, act_s, gvg_s, acc
):
    row = pl.program_id(0)
    toks, width = x_ref.shape[1], x_ref.shape[2]
    n = lam.shape[1]
    span = toks // SEGMENTS
    groups = SEGMENTS // SUBLANES

    @pl.when(row == 0)
    def _():
        acc[...] = jnp.zeros_like(acc)
        gbias_ref[...] = jnp.zeros_like(gbias_ref)
        sums_ref[...] = jnp.zeros_like(sums_ref)

    fill_keep(lens, row, first[0], keep, segs, span)
    everything = slice(0, toks)
    to_blocks(work, everything, drive_ref[0].astype(F32))
    real, imag = lam[0:1, :], lam[1:2, :]
    half = n // LANES
    real_b, imag_b = lane_blocks(real), lane_blocks(imag)
    compose_segments(
        ends_ref.at[0], segs, real, imag, span, carry_ref[0, :, 0:n],
        carry_ref[0, :, n : 2 * n], inits, False
    )

    def step(rows, states, extra, live):
        out = []
        at = 0
        for g in range(groups):
            k = keep[rows[g], :]
            for b in range(half):
                sr, si = states[at], states[at + 1]
                at += 2
                ar, ai = k * real_b[b], k * imag_b[b]
                nr = (ar * sr + work[b, rows[g], :]) - ai * si
                ni = (ar * si + work[half + b, rows[g], :]) + ai * sr
                done[b, rows[g], :] = nr
                done[half + b, rows[g], :] = ni
                out += [nr, ni]
        return out, extra

    skewed_scan(step, starting_states(inits, half), [], span, False)

    docs = lens.shape[1]
    limit = -first[0]
    for j in range(docs - 1):
        limit = limit + lens[row, j]
    chunk = 256
    ones = jnp.ones((SUBLANES, chunk), BF16)

    @pl.loop(0, toks // chunk)
    def _(c):
        part = pl.ds(pl.multiple_of(c * chunk, chunk), chunk)
        state = from_blocks(done, part).astype(BF16)
        st_ref[0, part, :] = state
        xhat = xhat_ref[0, part, :].astype(F32)
        mixed = nt_dot(state, out_cat[...]) + (xhat * (gain[...] * skip[...]) + bias[...] * skip[...])
        cdf, bell = gelu_parts(mixed)
        act = (mixed * cdf).astype(BF16)
        act_s[part, :] = act
        slope = cdf + mixed * (bell * 0.3989422804014327)
        value = nn_dot(act, wv[...]) + gbias[:, 0:width]
        gate = nn_dot(act, wg[...]) + gbias[:, width : 2 * width]
        sigma = 0.5 * jnp.tanh(0.5 * gate) + 0.5
        gated = value * sigma
        block_ref[0, part, :] = (x_ref[0, part, :].astype(F32) + gated).astype(BF16)
        place = lax.broadcasted_iota(jnp.int32, (chunk, width), 0) + c * chunk
        grad = jnp.where(place < limit, og_ref[0, part, :].astype(F32), 0.0)
        gv = (grad * sigma).astype(BF16)
        gg = (grad * gated * (1.0 - sigma)).astype(BF16)
        gvg_s[part, 0:width] = gv
        gvg_s[part, width : 2 * width] = gg
        gbias_ref[0:1, 0:width] += jnp.sum(gv.astype(F32), axis=0, keepdims=True)
        gbias_ref[0:1, width : 2 * width] += jnp.sum(gg.astype(F32), axis=0, keepdims=True)
        gact = nt_dot(gv, wv[...]) + nt_dot(gg, wg[...])
        gm = (gact * slope).astype(BF16)
        gm_ref[0, part, :] = gm
        gmf = gm.astype(F32)
        sums_ref[0:1, :] += jnp.sum(gmf, axis=0, keepdims=True)
        sums_ref[1:2, :] += jnp.sum(gmf * xhat, axis=0, keepdims=True)
        gs = nn_dot(gm, out_cat[...]).astype(BF16)
        gs_ref[0, part, :] = gs
        to_blocks(work, part, gs.astype(F32))

    acc[:, 0 : 2 * width] += tn_dot(act_s[...], gvg_s[...])
    acc[:, 2 * width :] += tn_dot(gm_ref[0], st_ref[0])

    fill_keep(lens, row, first[0] + 1, keep, segs, span)
    bends = bends_ref.at[0]
    segment_ends(work, keep, real_b, lane_blocks(imag, -1.0), bends, span, True)
    zero = jnp.zeros((1, n), F32)
    cr, ci = compose_segments(bends, segs, real, -imag, span, zero, zero, None, True)
    bfin_ref[0, :, 0:n] = cr
    bfin_ref[0, :, n : 2 * n] = ci

    @pl.when(row == pl.num_programs(0) - 1)
    def _():
        split_halves(acc, first[1], mine_ref, send_ref)


def split_halves(acc, core, mine_ref, send_ref):
    half = acc.shape[0] // 2
    mine_ref[0:half, :] = acc[pl.ds(pl.multiple_of(core * half, half), half), :].astype(BF16)
    send_ref[0:half, :] = acc[pl.ds(pl.multiple_of((1 - core) * half, half), half), :].astype(BF16)


def put_pair(vec, ref, at):
    high = vec.astype(BF16)
    low = (vec - high.astype(F32)).astype(BF16)
    ref[at : at + 2 * SUBLANES, :] = jnp.concatenate([high, low], axis=0)


def get_pair(ref, at):
    return (
        ref[at : at + SUBLANES, :].astype(F32)
        + ref[at + SUBLANES : at + 2 * SUBLANES, :].astype(F32)
    )


def adjoint_kernel(
    lens, first, gs_ref, bends_ref, carry_ref, st_ref, xhat_ref, lam, gbias_ref, sums_ref, adj_ref,
    mine_ref, send_ref, state, work, keep, segs, done, inits, acc, tots
):
    row = pl.program_id(0)
    toks, width = xhat_ref.shape[1], xhat_ref.shape[2]
    n = lam.shape[1]
    span = toks // SEGMENTS
    groups = SEGMENTS // SUBLANES

    @pl.when(row == 0)
    def _():
        acc[...] = jnp.zeros_like(acc)
        tots[...] = jnp.zeros_like(tots)

    fill_keep(lens, row, first[0] + 1, keep, segs, span)
    everything = slice(0, toks)
    to_blocks(work, everything, gs_ref[0].astype(F32))
    to_blocks(state, everything, st_ref[0].astype(F32))
    real, imag = lam[0:1, :], -lam[1:2, :]
    half = n // LANES
    real_b, imag_b = lane_blocks(real), lane_blocks(imag)
    compose_segments(
        bends_ref.at[0], segs, real, imag, span, carry_ref[0, :, 0:n],
        carry_ref[0, :, n : 2 * n], inits, True
    )

    def step(rows, states, tot, live):
        out = []
        tot = list(tot)
        at = 0
        for g in range(groups):
            k = keep[rows[g], :]
            for b in range(half):
                sr, si = states[at], states[at + 1]
                at += 2
                ur, ui = k * sr, k * si
                nr = (real_b[b] * ur + work[b, rows[g], :]) - imag_b[b] * ui
                ni = (real_b[b] * ui + work[half + b, rows[g], :]) + imag_b[b] * ur
                done[b, rows[g], :] = nr
                done[half + b, rows[g], :] = ni
                out += [nr, ni]
                hr, hi = state[b, rows[g], :], state[half + b, rows[g], :]
                if live is not None:
                    ur, ui, nr, ni = (jnp.where(live, v, 0.0) for v in (ur, ui, nr, ni))
                tot[4 * b] = tot[4 * b] + (ur * hr + ui * hi)
                tot[4 * b + 1] = tot[4 * b + 1] + (ui * hr - ur * hi)
                tot[4 * b + 2] = tot[4 * b + 2] + nr
                tot[4 * b + 3] = tot[4 * b + 3] + ni
        return out, tot

    zero8 = jnp.zeros((SUBLANES, LANES), F32)
    tot = skewed_scan(step, starting_states(inits, half), [zero8] * (4 * half), span, True)
    for b in range(half):
        low_lanes = slice(b * LANES, (b + 1) * LANES)
        high_lanes = slice(n + b * LANES, n + (b + 1) * LANES)
        tots[0, :, low_lanes] += tot[4 * b]
        tots[0, :, high_lanes] += tot[4 * b + 1]
        tots[1, :, low_lanes] += tot[4 * b + 2]
        tots[1, :, high_lanes] += tot[4 * b + 3]

    adj = from_blocks(done, everything).astype(BF16)
    adj_ref[0] = adj
    acc[...] += tn_dot(adj, xhat_ref[0])

    @pl.when(row == pl.num_programs(0) - 1)
    def _():
        split_halves(acc, first[1], mine_ref, send_ref)
        vec = jnp.concatenate(
            [gbias_ref[:, 0:width], gbias_ref[:, width : 2 * width], sums_ref[...],
             jnp.sum(tots[0], axis=0, keepdims=True), jnp.sum(tots[1], axis=0, keepdims=True),
             jnp.zeros((2, width), F32)], axis=0
        )
        put_pair(vec, mine_ref, n)
        put_pair(vec, send_ref, n)


def input_kernel(
    begin, lens, first, adj_ref, xhat_ref, gm_ref, og_ref, rstd_ref, scaled, gain, skip, *refs
):
    ig_ref = refs[-1]
    row = pl.program_id(0) + begin
    toks, width = xhat_ref.shape[1], xhat_ref.shape[2]
    docs = lens.shape[1]
    limit = -first[0]
    for j in range(docs - 1):
        limit = limit + lens[row, j]
    chunk = 256
    mix = gain[...] * skip[...]

    @pl.loop(0, toks // chunk)
    def _(c):
        part = pl.ds(pl.multiple_of(c * chunk, chunk), chunk)
        xhat = xhat_ref[0, part, :].astype(F32)
        g = nn_dot(adj_ref[0, part, :], scaled[...]) * gain[...]
        g = g + gm_ref[0, part, :].astype(F32) * mix
        place = lax.broadcasted_iota(jnp.int32, (chunk, width), 0) + c * chunk
        grad = jnp.where(place < limit, og_ref[0, part, :].astype(F32), 0.0)
        m1 = jnp.mean(g, axis=-1, keepdims=True)
        m2 = jnp.mean(g * xhat, axis=-1, keepdims=True)
        ig_ref[0, part, :] = (grad + rstd_ref[0, part, 0:1] * (g - m1 - xhat * m2)).astype(BF16)


def tree_sum(items):
    while len(items) > 1:
        items = [items[i] + items[i + 1] for i in range(0, len(items), 2)]
    return items[0]


def split_kernel(extra, place, mine_ref, got_ref, own_ref, *send_refs):
    half = mine_ref.shape[0] - extra
    piece = own_ref.shape[0] - extra

    def part(index):
        rows = pl.ds(pl.multiple_of(index * piece, piece), piece)
        return mine_ref[rows, :].astype(F32) + got_ref[rows, :].astype(F32)

    refs = (own_ref,) + send_refs
    for j, ref in enumerate(refs):
        ref[0:piece, :] = part(place[2] ^ j).astype(BF16)
    if extra:
        vec = get_pair(mine_ref, half) + get_pair(got_ref, half)
        for ref in refs:
            put_pair(vec, ref, piece)


def sum_kernel(extra, *refs):
    out = refs[-1]
    rows = out.shape[0] - extra
    out[0:rows, :] = tree_sum([r[0:rows, :].astype(F32) for r in refs[:-1]]).astype(BF16)
    if extra:
        put_pair(tree_sum([get_pair(r, rows) for r in refs[:-1]]), out, rows)


def gather_kernel(place, own_ref, *refs):
    out_ref = refs[-1]
    piece = refs[0].shape[0]
    for j, ref in enumerate((own_ref,) + refs[:-1]):
        rows = pl.ds(pl.multiple_of((place[2] ^ j) * piece, piece), piece)
        out_ref[rows, :] = ref[0:piece, :]


def weights_kernel(place, mine_ref, got_ref, value_ref, gate_ref, real_ref, imag_ref):
    width = value_ref.shape[1]
    n = real_ref.shape[1]
    total = jnp.where(pl.program_id(0) == 0, mine_ref[...], got_ref[...]).astype(F32)
    value_ref[...] = total[:, 0:width]
    gate_ref[...] = total[:, width : 2 * width]
    real_ref[...] = total[:, 2 * width : 2 * width + n]
    imag_ref[...] = -total[:, 2 * width + n :]


def exact_dot(left, right, dims):
    return lax.dot_general(
        left, right, (dims, ((), ())), precision=lax.Precision.HIGHEST, preferred_element_type=F32
    )


def last_kernel(
    place, mine_ref, got_ref, own_ref, scaled_ref, real_ref, imag_ref, scale_ref, gain, bias, skip,
    real_out, imag_out, small_out
):
    n, width = real_ref.shape
    vec = get_pair(own_ref, own_ref.shape[0] - 2 * SUBLANES)
    sum_gm, sum_gmx = vec[2:3, :], vec[3:4, :]
    col = jnp.broadcast_to(vec[5:6, :], (SUBLANES, 2 * n))
    lead = lax.broadcasted_iota(jnp.int32, (SUBLANES, width), 0) == 0
    spread = exact_dot(jnp.where(lead, col, 0.0), jnp.broadcast_to(bias[...], (SUBLANES, width)),
                       ((0,), (0,)))
    ones = jnp.ones((SUBLANES, width), F32)
    shift = exact_dot(col, scaled_ref[...].astype(F32), ((1,), (0,)))
    gain_sum = jnp.zeros((1, width), F32)
    scale_grad = jnp.zeros((SUBLANES, n), F32)
    first_core = place[1] == 0
    for part, weight_ref, out_ref in ((0, real_ref, real_out), (1, imag_ref, imag_out)):
        rows = slice(part * n, (part + 1) * n)
        keep_mine = first_core if part == 0 else jnp.logical_not(first_core)
        total = jnp.where(keep_mine, mine_ref[...], got_ref[...]).astype(F32)
        gain_sum = gain_sum + jnp.sum(total * scaled_ref[rows, :].astype(F32), axis=0, keepdims=True)
        full = total * gain[...] + spread[rows, :]
        out_ref[...] = full * scale_ref[rows, 0:1]
        scale_grad = scale_grad + exact_dot(ones, full * weight_ref[...].astype(F32), ((1,), (1,)))
    small_out[0:1, :] = gain_sum + skip[...] * sum_gmx
    small_out[1:2, :] = shift[0:1, :] + skip[...] * sum_gm
    small_out[2:3, :] = gain[...] * sum_gmx + bias[...] * sum_gm
    small_out[3:4, :] = jnp.concatenate([scale_grad[0:1, :]] * 2, axis=1)
    small_out[4:5, :] = vec[4:5, :]
    small_out[5:7, :] = vec[0:2, :]
    small_out[7:8, :] = jnp.zeros((1, width), F32)


def whole(shape):
    return pl.BlockSpec(shape, lambda r: (0,) * len(shape))


def per_row(*shape):
    return pl.BlockSpec((1,) + shape, lambda r: (r,) + (0,) * len(shape))


SCALARS = pl.BlockSpec(memory_space=pltpu.SMEM)


def carry_over(fin, through, axis, parts, hops, reverse):
    def shift(v):
        pairs = [(i, i + 1) for i in range(parts - 1)]
        if reverse:
            pairs = [(b, a) for a, b in pairs]
        return lax.ppermute(v, axis, pairs)

    if hops == 1:
        return shift(fin)
    n = fin.shape[-1] // 2
    total = shift(fin)
    for _ in range(hops - 1):
        tr, ti = through[..., :n], through[..., n:]
        sr, si = total[..., :n], total[..., n:]
        passed = jnp.concatenate([tr * sr - ti * si, tr * si + ti * sr], axis=-1)
        total = shift(fin + passed)
    return total


def glue(kernel, outs, *args, name, scalars=True):
    def spec(v):
        return pl.BlockSpec(v.shape, lambda i: (0,) * len(v.shape))

    specs = [SCALARS] * scalars + [spec(v) for v in args[scalars:]]
    many = isinstance(outs, list)
    return pl.pallas_call(
        kernel, grid=(1,), in_specs=specs, out_specs=[spec(v) for v in outs] if many else spec(outs),
        out_shape=outs, cost_estimate=cost(1.7),
        compiler_params=pltpu.CompilerParams(vmem_limit_bytes=GLUE_LIMIT), name=name,
    )(*args)


def from_core(v):
    return lax.ppermute(v, "rows", [(i, i ^ 1) for i in range(lax.axis_size("rows"))])


def from_plane(v, offset):
    count = lax.axis_size("rows")
    return lax.ppermute(v, "rows", [(i, i ^ (2 * offset)) for i in range(count)])


def from_line(v, offset):
    return lax.ppermute(v, "seq", [(i, i ^ offset) for i in range(lax.axis_size("seq"))])


def after(v, *others):
    return lax.optimization_barrier((v,) + others)[0]


class Exchange:
    def __init__(self, place, mine, send, extra, name):
        self.place, self.mine, self.extra, self.name = place, mine, extra, name
        self.plane = lax.axis_size("rows") // 2
        self.line = lax.axis_size("seq")
        self.half, self.cols = mine.shape[0] - extra, mine.shape[1]
        self.piece = SDS((self.half // self.plane + extra, self.cols), BF16)
        self.got = [from_core(send)]

    def split(self, place):
        self.own, *cuts = glue(
            functools.partial(split_kernel, self.extra), [self.piece] * self.plane, place,
            self.mine, *self.got, name=self.name + "_split"
        )
        self.got = [from_plane(c, j + 1) for j, c in enumerate(cuts)]
        return self.own

    def add(self, step, own=None):
        return glue(
            functools.partial(sum_kernel, self.extra), self.piece,
            self.own if own is None else own, *self.got, name=self.name + step, scalars=False
        )

    def add_plane(self, own=None):
        self.own = self.add("_plane", own)
        self.got = [from_line(self.own, j) for j in range(1, self.line)]
        return self.own

    def add_line(self, own=None):
        self.own = self.add("_line", own)
        total = self.own[: self.half // self.plane] if self.extra else self.own
        self.got = [from_plane(total, j) for j in range(1, self.plane)]
        return self.own

    def gather(self, place):
        self.mine = glue(
            gather_kernel, SDS((self.half, self.cols), BF16), place, self.own, *self.got,
            name=self.name + "_gather"
        )
        self.got = [from_core(self.mine)]
        return self.mine


def cost(us):
    return pl.CostEstimate(flops=int(us * 1e9), bytes_accessed=1 << 20, transcendentals=0)


PARAMS = pltpu.CompilerParams(
    dimension_semantics=("arbitrary",), vmem_limit_bytes=VMEM_LIMIT
)
SDS = jax.ShapeDtypeStruct


def scan_scratch(toks, n):
    return [
        pltpu.VMEM((2 * n // LANES, toks, LANES), F32), pltpu.VMEM((toks, LANES), F32),
        pltpu.VMEM((SEGMENTS, n), F32),
    ]


def run_forward(lens, place, x, gain, bias, scaled, lam):
    rows_here, toks, width = x.shape
    n = lam.shape[1]
    act = per_row(toks, width)
    return pl.pallas_call(
        forward_kernel,
        grid=(rows_here,),
        in_specs=[SCALARS, SCALARS, act, whole((1, width)), whole((1, width)),
                  whole((2 * n, width)), whole((2, n))],
        out_specs=[per_row(toks, 2 * n), act, per_row(toks, 128), per_row(SEGMENTS, 2 * n),
                   per_row(1, 2 * n)],
        out_shape=[SDS((rows_here, toks, 2 * n), BF16), SDS(x.shape, BF16),
                   SDS((rows_here, toks, 128), F32), SDS((rows_here, SEGMENTS, 2 * n), F32),
                   SDS((rows_here, 1, 2 * n), F32)],
        scratch_shapes=scan_scratch(toks, n),
        compiler_params=PARAMS,
        cost_estimate=cost(10.6),
        name="forward",
    )(lens, place, x, gain, bias, scaled, lam)


def run_middle(
    lens, place, drive, ends, carry, xhat, x, og, lam, out_cat, gain, bias, skip, wv, wg, gbias
):
    rows_here, toks, width = x.shape
    n = lam.shape[1]
    cols = 2 * width + 2 * n
    act, chan = per_row(toks, width), per_row(toks, 2 * n)
    return pl.pallas_call(
        middle_kernel,
        grid=(rows_here,),
        in_specs=[SCALARS, SCALARS, chan, per_row(SEGMENTS, 2 * n),
                  per_row(1, 2 * n), act, act, act, whole((2, n)), whole((width, 2 * n)),
                  whole((1, width)), whole((1, width)), whole((1, width)),
                  whole((width, width)), whole((width, width)), whole((1, 2 * width))],
        out_specs=[act, act, chan, chan, per_row(SEGMENTS, 2 * n), per_row(1, 2 * n),
                   whole((width // 2, cols)), whole((width // 2, cols)), whole((1, 2 * width)),
                   whole((2, width))],
        out_shape=[SDS(x.shape, BF16), SDS(x.shape, BF16), SDS((rows_here, toks, 2 * n), BF16),
                   SDS((rows_here, toks, 2 * n), BF16), SDS((rows_here, SEGMENTS, 2 * n), F32),
                   SDS((rows_here, 1, 2 * n), F32), SDS((width // 2, cols), BF16),
                   SDS((width // 2, cols), BF16), SDS((1, 2 * width), F32),
                   SDS((2, width), F32)],
        scratch_shapes=scan_scratch(toks, n) + [
            pltpu.VMEM((2 * n // LANES, toks, LANES), F32), pltpu.VMEM((SEGMENTS, 2 * n), F32),
            pltpu.VMEM((toks, width), BF16),
            pltpu.VMEM((toks, 2 * width), BF16), pltpu.VMEM((width, cols), F32)],
        compiler_params=PARAMS,
        cost_estimate=cost(48),
        name="middle",
    )(lens, place, drive, ends, carry, xhat, x, og, lam, out_cat, gain, bias, skip, wv, wg, gbias)


def run_adjoint(lens, place, gs, bends, carry, st, xhat, lam, gbias_g, sums):
    rows_here, toks, width = xhat.shape
    n = lam.shape[1]
    act, chan = per_row(toks, width), per_row(toks, 2 * n)
    return pl.pallas_call(
        adjoint_kernel,
        grid=(rows_here,),
        in_specs=[SCALARS, SCALARS, chan, per_row(SEGMENTS, 2 * n), per_row(1, 2 * n), chan, act,
                  whole((2, n)), whole((1, 2 * width)), whole((2, width))],
        out_specs=[chan, whole((n + EXTRA, width)), whole((n + EXTRA, width))],
        out_shape=[SDS((rows_here, toks, 2 * n), BF16), SDS((n + EXTRA, width), BF16),
                   SDS((n + EXTRA, width), BF16)],
        scratch_shapes=[pltpu.VMEM((2 * n // LANES, toks, LANES), F32)] + scan_scratch(toks, n) + [
            pltpu.VMEM((2 * n // LANES, toks, LANES), F32), pltpu.VMEM((SEGMENTS, 2 * n), F32),
            pltpu.VMEM((2 * n, width), F32),
            pltpu.VMEM((2, SUBLANES, 2 * n), F32)],
        compiler_params=PARAMS,
        cost_estimate=cost(12),
        name="adjoint",
    )(lens, place, gs, bends, carry, st, xhat, lam, gbias_g, sums)


def run_input(lens, place, adj, xhat, gm, og, rstd, scaled, gain, skip, begin=0, end=None, into=None):
    rows_here, toks, width = xhat.shape
    end = rows_here if end is None else end

    def rows(*shape):
        return pl.BlockSpec((1,) + shape, lambda r: (r + begin if begin else r, 0, 0))

    act = rows(toks, width)
    args = (lens, place, adj, xhat, gm, og, rstd, scaled, gain, skip)
    specs = [SCALARS, SCALARS, rows(toks, adj.shape[2]), act, act, act,
             rows(toks, 128), whole(scaled.shape), whole((1, width)), whole((1, width))]
    if into is not None:
        args, specs = args + (into,), specs + [pl.BlockSpec(memory_space=pl.ANY)]
    return pl.pallas_call(
        functools.partial(input_kernel, begin),
        grid=(end - begin,),
        in_specs=specs,
        out_specs=act,
        out_shape=SDS(xhat.shape, BF16),
        input_output_aliases={} if into is None else {len(args) - 1: 0},
        compiler_params=PARAMS,
        cost_estimate=cost(8),
        name="input",
    )(*args)


def run_weights(place, mine, got, width, n):
    half, cols = mine.shape
    blocks = 2
    tall = half // blocks
    source = pl.BlockSpec((tall, cols), lambda p, i, place: (i, 0))

    def out(c):
        return pl.BlockSpec((tall, c), lambda p, i, place: ((place[1] ^ p) * blocks + i, 0))

    return pl.pallas_call(
        weights_kernel,
        grid_spec=pltpu.PrefetchScalarGridSpec(
            num_scalar_prefetch=1, grid=(2, blocks), in_specs=[source, source],
            out_specs=[out(width), out(width), out(n), out(n)],
        ),
        out_shape=[SDS((2 * half, width), F32)] * 2 + [SDS((2 * half, n), F32)] * 2,
        compiler_params=pltpu.CompilerParams(vmem_limit_bytes=VMEM_LIMIT),
        cost_estimate=cost(4.8),
        name="early_out",
    )(place, mine, got)


def body(
    tokens_in, layer_norm_gain, layer_norm_bias, input_real, input_imag, decay_log, angle_log,
    scale_log, output_real, output_imag, skip_gain, glu_value, glu_gate, glu_bias, doc_lengths,
    out_grad
):
    rows_here, toks, width = tokens_in.shape
    n = input_real.shape[0]
    parts = lax.axis_size("seq")
    seat = lax.axis_index("seq")
    length = toks * parts
    hops = max(1, (length // 4) // toks)
    row_seat = lax.axis_index("rows")
    place = jnp.stack([seat * toks, row_seat % 2, row_seat // 2, seat]).astype(jnp.int32)
    rate = jnp.exp(decay_log)
    radius = jnp.exp(-rate)
    angle = jnp.exp(angle_log)
    cosine, sine = jnp.cos(angle), jnp.sin(angle)
    norm_root = jnp.sqrt(1.0 - jnp.exp(-2.0 * rate))
    scale = jnp.exp(scale_log) * norm_root
    lam = jnp.stack([radius * cosine, radius * sine])
    inputs = jnp.concatenate([input_real, input_imag], axis=0).astype(F32)
    scale2 = jnp.concatenate([scale, scale])
    scaled = (inputs * scale2[:, None]).astype(BF16)
    scale_b = jnp.broadcast_to(scale2[:, None], (2 * n, LANES))
    out_cat = jnp.concatenate([output_real, -output_imag], axis=1)
    gain, bias, skip = layer_norm_gain[None], layer_norm_bias[None], skip_gain[None]
    gbias = glu_bias[None]
    through = back_through = None
    if hops > 1:
        starts = jnp.cumsum(doc_lengths, axis=1) - doc_lengths - seat * toks
        clear = 1.0 - jnp.any((starts >= 0) & (starts < toks), axis=1).astype(F32)
        clear_next = 1.0 - jnp.any((starts >= 1) & (starts < toks + 1), axis=1).astype(F32)
        fr, fi = power_of(lam[0], lam[1], toks)
        through = clear[:, None, None] * jnp.concatenate([fr, fi])[None, None]
        back_through = clear_next[:, None, None] * jnp.concatenate([fr, -fi])[None, None]

    drive, xhat, rstd, ends, fin = run_forward(
        doc_lengths, place, tokens_in, gain, bias, scaled, lam
    )
    carry = carry_over(fin, through, "seq", parts, hops, False)
    block_out, gm, gs, st, bends, bfin, mine, send, gbias_g, sums = run_middle(
        doc_lengths, place, drive, ends, carry, xhat, tokens_in, out_grad, lam, out_cat, gain,
        bias, skip, glu_value, glu_gate, gbias
    )
    back_carry = carry_over(bfin, back_through, "seq", parts, hops, True)
    early = Exchange(place, mine, send, 0, "early")
    done = early.split(place)
    adj, mine_in, send_in = run_adjoint(
        doc_lengths, after(place, done), gs, bends, back_carry, st, xhat, lam, gbias_g, sums
    )
    late = Exchange(place, mine_in, send_in, EXTRA, "late")
    early.add_plane(after(early.own, adj))
    done = late.split(after(place, early.own))
    half_rows = rows_here // 2
    args = (adj, xhat, gm, out_grad, rstd, scaled, gain, skip)
    input_grad = run_input(doc_lengths, after(place, done), *args, 0, half_rows)
    late.add_plane(after(late.own, input_grad))
    early.add_line(after(early.own, late.own))
    input_grad = run_input(
        doc_lengths, after(place, early.own, late.own), *args, half_rows, rows_here, input_grad
    )
    late.add_line(after(late.own, input_grad))
    done = early.gather(after(place, late.own))
    done = late.gather(after(place, done))
    value_g, gate_g, real_g, imag_g = run_weights(
        after(place, done), early.mine, early.got[0], width, n
    )
    in_real_g, in_imag_g, small = glue(
        last_kernel,
        [SDS((n, width), F32), SDS((n, width), F32), SDS((SUBLANES, width), F32)],
        after(place, value_g), late.mine, late.got[0], late.own, scaled, input_real, input_imag,
        scale_b, gain, bias, skip, name="late_out",
    )
    gain_grad, shift_grad, skip_grad = small[0], small[1], small[2]
    scale_grad, lamg, gbias_g = small[3, :n], small[4], small[5:7].reshape(2 * width)
    lr, li = lamg[:n], lamg[n:]
    radius_grad = lr * cosine + li * sine
    angle_grad = radius * (li * cosine - lr * sine) * angle
    decay_grad = (
        -radius_grad * radius * rate
        + scale_grad * jnp.exp(scale_log) * jnp.exp(-2.0 * rate) * rate / norm_root
    )
    return (
        block_out, input_grad, gain_grad, shift_grad, in_real_g, in_imag_g, decay_grad,
        angle_grad, scale_grad * scale, real_g, imag_g, skip_grad, value_g, gate_g, gbias_g
    )


def solution(mesh):
    tokens = P("rows", "seq", None)
    placed = (tokens,) + (P(),) * 13 + (P("rows", None), tokens)
    return jax.shard_map(
        body, mesh=mesh, in_specs=placed, out_specs=(tokens, tokens) + (P(),) * 13,
        check_vma=False,
    )
```

time: 315 us -> 154 us (0.49)
  the two profiles are of different devices: /device:TPU:0 before, /device:TPU:17 now
where the time goes in v2:
time: 154 us; the launch traced here: 153 us
  Pallas kernels  98.3 us (64%)
  starting transfers between devices  31.4 us (20%)
  waiting for transfers between devices  11.7 us (8%)
  other arithmetic  5.43 us (4%)
  local copies, waits for them, and re-layouts  5.18 us (3%)
    pallas_call x1, Pallas kernels, run_middle(): pl.pallas_call(middle_kernel, grid=(rows_here,), in_specs=[SCALARS, SCALA...  47.8 us
    pallas_call x2, Pallas kernels, run_input(): pl.pallas_call(functools.partial(input_kernel, begin), grid=(end - begin,...  16.4 us
    pallas_call x1, Pallas kernels, run_adjoint(): pl.pallas_call(adjoint_kernel, grid=(rows_here,), in_specs=[SCALARS, SCAL...  12 us
    ppermute x12, starting transfers between devices, from_plane(): return lax.ppermute(v, 'rows', [(i, i ^ 2 * offset) for i in range(count)])  11.2 us
    pallas_call x1, Pallas kernels, run_forward(): pl.pallas_call(forward_kernel, grid=(rows_here,), in_specs=[SCALARS, SCAL...  10.8 us
    ppermute x4, starting transfers between devices, from_core(): lax.ppermute(v, 'rows', [(i, i ^ 1) for i in range(lax.axis_size('rows'))])  9.06 us
    ppermute x6, waiting for transfers between devices, from_line(): lax.ppermute(v, 'seq', [(i, i ^ offset) for i in range(lax.axis_size('seq...  7.02 us
    pallas_call x9, Pallas kernels, glue(): pl.pallas_call(kernel, grid=(1,), in_specs=specs, out_specs=[spec(v) for...  6.53 us
  transfers between devices with their start and end apart: 24, of which 6 were waited for; matrix products, arithmetic and copies ran while one was open for 1% of the time, Pallas kernels for 23%

profile of v2, /device:TPU:17, one launch (start us, length us, event | category | flops | bytes accessed | tf_op | source)
XLA Modules:
  0.0 153.1 jit_solution(7468281125027040489)
XLA Ops:
  0.7 0.8 fusion.1
  1.5 0.6 pad_maximum_fusion.2.lam
  2.0 2.0 %multiply_convert_fusion.scaled.scaled_ref = bf16[512,512]{1,0:T(8,128)(2,1)} fusion(bf16[256,512]{1,0:T(8,128)(2,1)} %imag_ref.1, bf16[256,512]{1,0:T(8,128)(2,1)} %real_ref.1, f32[512]{0:T(512)S(1)} %pad_maximum_fusion.1), kind=kLoop, calls=%fused_computation | loop fusion | flops 1572864 | bytes 1050624 | tf_op jit(solution)/shard_map/convert_element_type | solution.py:786
  4.0 0.6 pad_add_fusion.first.place
  4.6 10.8 %forward.1 = (bf16[4,1024,512]{2,1,0:T(8,128)(2,1)}, bf16[4,1024,512]{2,1,0:T(8,128)(2,1)}, f32[4,1024,128]{2,1,0:T(8,128)}, f32[4,16,512]{2,1,0:T(8,128)}, f32[4,1,512]{2,1,0:T(1,128)}) custom-call(s32[4,8]{1,0:T(4,128)} %lens.9, s32[4]{0:T(128)} %pad_add_fusion.first.place, bf16[4,1024,512]{2,1,0:T(8,128)(2,1)} %x_ref.3, f32[1,512]{1,0:T(1,128)} %bitcast.19, ...), custom_call_target="tpu_custom_call" | custom-call | flops 10599999488 | bytes 1048576 | tf_op jit(solution)/shard_map/forward/pallas_call | solution.py:645
  15.4 3.2 %collective-permute-start = (f32[4,1,512]{2,1,0:T(1,128)}, f32[4,1,512]{2,1,0:T(1,128)S(1)}, u32[]{:S(2)}, u32[]{:S(2)}) collective-permute-start(f32[4,1,512]{2,1,0:T(1,128)} %get-tuple-element.62), channel_id=1, source_target_pairs={{0,1},{1,2},{2,3},{4,5},{5,6},{6,7},{8,9},{9,10},{10,11},{12,13},{... | collective-permute-start | bytes 24584 | tf_op jit(solution)/shard_map/ppermute | solution.py:537
  18.7 0.8 pad_maximum_fusion.out_cat
  19.5 0.5 collective-permute-done.carry_ref
  20.0 0.6 copy-done.20
  20.6 47.8 %middle.1 = (bf16[4,1024,512]{2,1,0:T(8,128)(2,1)}, bf16[4,1024,512]{2,1,0:T(8,128)(2,1)}, bf16[4,1024,512]{2,1,0:T(8,128)(2,1)}, bf16[4,1024,512]{2,1,0:T(8,128...) custom-call(s32[4,8]{1,0:T(4,128)} %lens.9, ...), custom_call_target="tpu_custom_call" | custom-call | flops 48000000000 | bytes 1048576 | tf_op jit(solution)/shard_map/middle/pallas_call | solution.py:669
  68.4 2.0 %collective-permute-start.1 = (bf16[256,1536]{1,0:T(8,128)(2,1)}, bf16[256,1536]{1,0:T(8,128)(2,1)S(1)}, u32[]{:S(2)}, u32[]{:S(2)}) collective-permute-start(bf16[256,1536]{1,0:T(8,128)(2,1)} %get-tuple-element.66), channel_id=1, source_target_pairs={{0,4},{4,0},{8,12},{12,8},{16,20},{20,16},{24,28},{28,24},{1,5},{5... | collective-permute-start | bytes 2359304 | tf_op jit(solution)/shard_map/ppermute | solution.py:565
  70.4 2.2 %collective-permute-start.2 = (f32[4,1,512]{2,1,0:T(1,128)}, f32[4,1,512]{2,1,0:T(1,128)S(1)}, u32[]{:S(2)}, u32[]{:S(2)}) collective-permute-start(f32[4,1,512]{2,1,0:T(1,128)} %get-tuple-element.71), channel_id=1, source_target_pairs={{1,0},{2,1},{3,2},{5,4},{6,5},{7,6},{9,8},{10,9},{11,10},{13,12},{... | collective-permute-start | bytes 24584 | tf_op jit(solution)/shard_map/ppermute | solution.py:537
  72.6 1.1 copy-done.11
  73.8 0.7 early_split.1
  74.5 1.3 collective-permute-start.3
  75.8 1.2 collective-permute-start.4
  77.2 0.6 copy-done.19
  77.8 12.0 %adjoint.1 = (bf16[4,1024,512]{2,1,0:T(8,128)(2,1)}, bf16[272,512]{1,0:T(8,128)(2,1)}, bf16[272,512]{1,0:T(8,128)(2,1)}) custom-call(s32[4,8]{1,0:T(4,128)} %lens.9, s32[4]{0:T(128)} %pad_add_fusion.first.place, bf16[4,1024,512]{2,1,0:T(8,128)(2,1)} %get-tuple-element.69.gs_ref, f32[4,16,512]{2,1,0:T(8,128)} %get-tuple-element.70.bends_ref, ...), custom_call_target="tpu_custom_call" | custom-call | flops 12000000000 | bytes 1048576 | tf_op jit(solution)/shard_map/adjoint/pallas_call | solution.py:698
  89.8 1.2 collective-permute-start.6
  91.2 1.3 collective-permute-done.6.got_ref
  92.5 0.6 late_split.1
  93.1 1.2 collective-permute-start.7
  94.3 1.3 collective-permute-start.10
  95.6 1.4 collective-permute-start.12
  97.0 1.2 collective-permute-start.8
  98.2 0.7 collective-permute-start.9
  98.9 8.2 %input.2.refs_0_ = bf16[4,1024,512]{2,1,0:T(8,128)(2,1)} custom-call(s32[4,8]{1,0:T(4,128)} %lens.9, s32[4]{0:T(128)} %pad_add_fusion.first.place, bf16[4,1024,512]{2,1,0:T(8,128)(2,1)} %get-tuple-element.75.adj_ref, bf16[4,1024,512]{2,1,0:T(8,128)(2,1)} %get-tuple-element.63.xhat_ref, bf16[4,1024,512]{2,1,0:T(8,128)(2,1)} %get-tuple-element.85.gm_ref, ...), custom_call_target="tpu_custom_call" | custom-call | flops 8000000000 | bytes 1048576 | tf_op jit(solution)/shard_map/input/pallas_call | solution.py:729
  107.1 1.8 %collective-permute-start.13 = (bf16[80,512]{1,0:T(8,128)(2,1)S(1)}, bf16[80,512]{1,0:T(8,128)(2,1)S(1)}, u32[]{:S(2)}, u32[]{:S(2)}) collective-permute-start(bf16[80,512]{1,0:T(8,128)(2,1)S(1)} %late_plane.1.refs_0_), channel_id=1, source_target_pairs={{0,1},{1,0},{2,3},{3,2},{4,5},{5,4},{6,7},{7,6},{8,9},{9,8},{10,11... | collective-permute-start | bytes 245768 | tf_op jit(solution)/shard_map/ppermute | solution.py:574
  109.0 1.3 collective-permute-start.15
  110.3 7.0 %collective-permute-done.12.refs_3_ = bf16[64,1536]{1,0:T(8,128)(2,1)S(1)} collective-permute-done((bf16[64,1536]{1,0:T(8,128)(2,1)S(1)}, bf16[64,1536]{1,0:T(8,128)(2,1)S(1)}, u32[]{:S(2)}, u32[]{:S(2)}) %collective-permute-start.12) | collective-permute-done | bytes 196640 | tf_op jit(solution)/shard_map/ppermute | solution.py:574
  117.4 1.3 collective-permute-start.17
  118.7 1.3 collective-permute-start.18
  120.1 8.2 %input.3 = bf16[4,1024,512]{2,1,0:T(8,128)(2,1)} custom-call(s32[4,8]{1,0:T(4,128)} %lens.9, s32[4]{0:T(128)} %pad_add_fusion.first.place, bf16[4,1024,512]{2,1,0:T(8,128)(2,1)} %get-tuple-element.75.adj_ref, bf16[4,1024,512]{2,1,0:T(8,128)(2,1)} %get-tuple-element.63.xhat_ref, ...), custom_call_target="tpu_custom_call", output_to_operand_aliasing={{}: (10, {})} | custom-call | flops 8000000000 | bytes 1048576 | tf_op jit(solution)/shard_map/input/pallas_call | solution.py:729
  128.4 0.5 copy-done.5
  128.9 0.6 early_gather.1.mine_ref
  129.5 4.0 %collective-permute-start.22 = (bf16[256,1536]{1,0:T(8,128)(2,1)S(1)}, bf16[256,1536]{1,0:T(8,128)(2,1)S(1)}, u32[]{:S(2)}, u32[]{:S(2)}) collective-permute-start(bf16[256,1536]{1,0:T(8,128)(2,1)S(1)} %early_gather.1.mine_ref), channel_id=1, source_target_pairs={{0,4},{4,0},{8,12},{12,8},{16,20},{20,16},{24,28},{28,24},{1,5},{5... | collective-permute-start | bytes 2359304 | tf_op jit(solution)/shard_map/ppermute | solution.py:565
  133.8 1.2 collective-permute-start.20
  135.1 1.1 collective-permute-start.21
  136.2 0.9 collective-permute-done.19.refs_0_
  137.2 1.8 %collective-permute-done.21.refs_2_ = bf16[64,512]{1,0:T(8,128)(2,1)S(1)} collective-permute-done((bf16[64,512]{1,0:T(8,128)(2,1)S(1)}, bf16[64,512]{1,0:T(8,128)(2,1)S(1)}, u32[]{:S(2)}, u32[]{:S(2)}) %collective-permute-start.21) | collective-permute-done | bytes 65568 | tf_op jit(solution)/shard_map/ppermute | solution.py:570
  139.1 0.6 late_gather.1.mine_ref
  139.7 1.9 %collective-permute-start.23 = (bf16[256,512]{1,0:T(8,128)(2,1)S(1)}, bf16[256,512]{1,0:T(8,128)(2,1)S(1)}, u32[]{:S(2)}, u32[]{:S(2)}) collective-permute-start(bf16[256,512]{1,0:T(8,128)(2,1)S(1)} %late_gather.1.mine_ref), channel_id=1, source_target_pairs={{0,4},{4,0},{8,12},{12,8},{16,20},{20,16},{24,28},{28,24},{1,5},{5... | collective-permute-start | bytes 786440 | tf_op jit(solution)/shard_map/ppermute | solution.py:565
  141.6 0.9 copy-done.18
  142.5 4.8 %early_out.1 = (f32[512,512]{1,0:T(8,128)}, f32[512,512]{1,0:T(8,128)}, f32[512,256]{1,0:T(8,128)}, f32[512,256]{1,0:T(8,128)}) custom-call(s32[4]{0:T(128)} %pad_add_fusion.first.place, bf16[256,1536]{1,0:T(8,128)(2,1)} %copy-done.7, bf16[256,1536]{1,0:T(8,128)(2,1)} %copy-done.18), custom_call_target="tpu_custom_call" | custom-call | flops 4800000000 | bytes 1048576 | tf_op jit(solution)/shard_map/early_out/pallas_call | solution.py:751
  147.6 3.7 %late_out.1 = (f32[256,512]{1,0:T(8,128)}, f32[256,512]{1,0:T(8,128)}, f32[8,512]{1,0:T(8,128)S(1)}) custom-call(s32[4]{0:T(128)S(1)} %copy-done.6, bf16[256,512]{1,0:T(8,128)(2,1)S(1)} %late_gather.1.mine_ref, bf16[256,512]{1,0:T(8,128)(2,1)S(1)} %collective-permute-done.23.got_ref, bf16[80,512]{1,0:T(8,128)(2,1)S(1)} %late_line.1.own_ref, ...), custom_call_target="tpu_custom_call" | custom-call | flops 1700000000 | bytes 1048576 | tf_op jit(solution)/shard_map/late_out/pallas_call | solution.py:557
  151.3 0.6 fusion.3
  151.9 0.6 copy.32
  152.5 0.6 multiply_multiply_fusion
  (71 shorter events, 1.4 us)
Async XLA Ops:
  4.6 14.0 %copy-start.13 = (bf16[512,256]{1,0:T(8,128)(2,1)S(1)}, bf16[512,256]{1,0:T(8,128)(2,1)}, u32[]{:S(2)}) copy-start(bf16[512,256]{1,0:T(8,128)(2,1)} %param.25) | copy-start | bytes 786436
  4.6 14.1 %copy-start.14 = (bf16[512,256]{1,0:T(8,128)(2,1)S(1)}, bf16[512,256]{1,0:T(8,128)(2,1)}, u32[]{:S(2)}) copy-start(bf16[512,256]{1,0:T(8,128)(2,1)} %param.24) | copy-start | bytes 786436
  15.4 4.6 %collective-permute-start = (f32[4,1,512]{2,1,0:T(1,128)}, f32[4,1,512]{2,1,0:T(1,128)S(1)}, u32[]{:S(2)}, u32[]{:S(2)}) collective-permute-start(f32[4,1,512]{2,1,0:T(1,128)} %get-tuple-element.62), channel_id=1, source_target_pairs={{0,1},{1,2},{2,3},{4,5},{5,6},{6,7},{8,9},{9,10},{10,11},{12,13},{... | collective-permute-start | bytes 24584 | tf_op jit(solution)/shard_map/ppermute | solution.py:537
  20.0 0.6 copy-start.20
  20.6 52.0 %copy-start.3 = (s32[4]{0:T(128)S(1)}, s32[4]{0:T(128)}, u32[]{:S(2)}) copy-start(s32[4]{0:T(128)} %pad_add_fusion.first.place) | copy-start | bytes 52
  68.4 4.2 %collective-permute-start.1 = (bf16[256,1536]{1,0:T(8,128)(2,1)}, bf16[256,1536]{1,0:T(8,128)(2,1)S(1)}, u32[]{:S(2)}, u32[]{:S(2)}) collective-permute-start(bf16[256,1536]{1,0:T(8,128)(2,1)} %get-tuple-element.66), channel_id=1, source_target_pairs={{0,4},{4,0},{8,12},{12,8},{16,20},{20,16},{24,28},{28,24},{1,5},{5... | collective-permute-start | bytes 2359304 | tf_op jit(solution)/shard_map/ppermute | solution.py:565
  70.4 6.8 %collective-permute-start.2 = (f32[4,1,512]{2,1,0:T(1,128)}, f32[4,1,512]{2,1,0:T(1,128)S(1)}, u32[]{:S(2)}, u32[]{:S(2)}) collective-permute-start(f32[4,1,512]{2,1,0:T(1,128)} %get-tuple-element.71), channel_id=1, source_target_pairs={{1,0},{2,1},{3,2},{5,4},{6,5},{7,6},{9,8},{10,9},{11,10},{13,12},{... | collective-permute-start | bytes 24584 | tf_op jit(solution)/shard_map/ppermute | solution.py:537
  72.6 1.1 copy-start.11
  74.5 16.5 %collective-permute-start.3 = (bf16[64,1536]{1,0:T(8,128)(2,1)S(1)}, bf16[64,1536]{1,0:T(8,128)(2,1)S(1)}, u32[]{:S(2)}, u32[]{:S(2)}) collective-permute-start(bf16[64,1536]{1,0:T(8,128)(2,1)S(1)} %get-tuple-element.77), channel_id=1, source_target_pairs={{0,8},{4,12},{8,0},{12,4},{16,24},{20,28},{24,16},{28,20},{1,9},{5... | collective-permute-start | bytes 589832 | tf_op jit(solution)/shard_map/ppermute | solution.py:570
  75.8 15.3 %collective-permute-start.4 = (bf16[64,1536]{1,0:T(8,128)(2,1)S(1)}, bf16[64,1536]{1,0:T(8,128)(2,1)S(1)}, u32[]{:S(2)}, u32[]{:S(2)}) collective-permute-start(bf16[64,1536]{1,0:T(8,128)(2,1)S(1)} %get-tuple-element.78), channel_id=1, source_target_pairs={{0,16},{4,20},{8,24},{12,28},{16,0},{20,4},{24,8},{28,12},{1,17},{... | collective-permute-start | bytes 589832 | tf_op jit(solution)/shard_map/ppermute | solution.py:570
  77.0 14.1 %collective-permute-start.5 = (bf16[64,1536]{1,0:T(8,128)(2,1)S(1)}, bf16[64,1536]{1,0:T(8,128)(2,1)S(1)}, u32[]{:S(2)}, u32[]{:S(2)}) collective-permute-start(bf16[64,1536]{1,0:T(8,128)(2,1)S(1)} %get-tuple-element.79), channel_id=1, source_target_pairs={{0,24},{4,28},{8,16},{12,20},{16,8},{20,12},{24,0},{28,4},{1,25},{... | collective-permute-start | bytes 589832 | tf_op jit(solution)/shard_map/ppermute | solution.py:570
  77.2 0.6 copy-start.19
  89.8 2.6 %copy-start.4 = (s32[4]{0:T(128)S(1)}, s32[4]{0:T(128)}, u32[]{:S(2)}) copy-start(s32[4]{0:T(128)} %pad_add_fusion.first.place) | copy-start | bytes 52
  89.8 2.6 %copy-start.12 = (bf16[272,512]{1,0:T(8,128)(2,1)S(1)}, bf16[272,512]{1,0:T(8,128)(2,1)}, u32[]{:S(2)}) copy-start(bf16[272,512]{1,0:T(8,128)(2,1)} %get-tuple-element.81.mine_ref) | copy-start | bytes 835588
  89.8 2.6 %collective-permute-start.6 = (bf16[272,512]{1,0:T(8,128)(2,1)}, bf16[272,512]{1,0:T(8,128)(2,1)S(1)}, u32[]{:S(2)}, u32[]{:S(2)}) collective-permute-start(bf16[272,512]{1,0:T(8,128)(2,1)} %get-tuple-element.82), channel_id=1, source_target_pairs={{0,4},{4,0},{8,12},{12,8},{16,20},{20,16},{24,28},{28,24},{1,5},{5... | collective-permute-start | bytes 835592 | tf_op jit(solution)/shard_map/ppermute | solution.py:565
  93.1 5.1 %collective-permute-start.7 = (bf16[80,512]{1,0:T(8,128)(2,1)S(1)}, bf16[80,512]{1,0:T(8,128)(2,1)S(1)}, u32[]{:S(2)}, u32[]{:S(2)}) collective-permute-start(bf16[80,512]{1,0:T(8,128)(2,1)S(1)} %get-tuple-element.88), channel_id=1, source_target_pairs={{0,8},{4,12},{8,0},{12,4},{16,24},{20,28},{24,16},{28,20},{1,9},{5... | collective-permute-start | bytes 245768 | tf_op jit(solution)/shard_map/ppermute | solution.py:570
  94.3 14.7 %collective-permute-start.10 = (bf16[64,1536]{1,0:T(8,128)(2,1)S(1)}, bf16[64,1536]{1,0:T(8,128)(2,1)S(1)}, u32[]{:S(2)}, u32[]{:S(2)}) collective-permute-start(bf16[64,1536]{1,0:T(8,128)(2,1)S(1)} %early_plane.1.refs_0_), channel_id=1, source_target_pairs={{0,1},{1,0},{2,3},{3,2},{4,5},{5,4},{6,7},{7,6},{8,9},{9,8},{10,11... | collective-permute-start | bytes 589832 | tf_op jit(solution)/shard_map/ppermute | solution.py:574
  95.6 14.7 %collective-permute-start.11 = (bf16[64,1536]{1,0:T(8,128)(2,1)S(1)}, bf16[64,1536]{1,0:T(8,128)(2,1)S(1)}, u32[]{:S(2)}, u32[]{:S(2)}) collective-permute-start(bf16[64,1536]{1,0:T(8,128)(2,1)S(1)} %early_plane.1.refs_0_), channel_id=1, source_target_pairs={{0,2},{1,3},{2,0},{3,1},{4,6},{5,7},{6,4},{7,5},{8,10},{9,11},{10,... | collective-permute-start | bytes 589832 | tf_op jit(solution)/shard_map/ppermute | solution.py:574
  95.6 21.7 %collective-permute-start.12 = (bf16[64,1536]{1,0:T(8,128)(2,1)S(1)}, bf16[64,1536]{1,0:T(8,128)(2,1)S(1)}, u32[]{:S(2)}, u32[]{:S(2)}) collective-permute-start(bf16[64,1536]{1,0:T(8,128)(2,1)S(1)} %early_plane.1.refs_0_), channel_id=1, source_target_pairs={{0,3},{1,2},{2,1},{3,0},{4,7},{5,6},{6,5},{7,4},{8,11},{9,10},{10,... | collective-permute-start | bytes 589832 | tf_op jit(solution)/shard_map/ppermute | solution.py:574
  97.0 10.1 %collective-permute-start.8 = (bf16[80,512]{1,0:T(8,128)(2,1)S(1)}, bf16[80,512]{1,0:T(8,128)(2,1)S(1)}, u32[]{:S(2)}, u32[]{:S(2)}) collective-permute-start(bf16[80,512]{1,0:T(8,128)(2,1)S(1)} %get-tuple-element.89), channel_id=1, source_target_pairs={{0,16},{4,20},{8,24},{12,28},{16,0},{20,4},{24,8},{28,12},{1,17},{... | collective-permute-start | bytes 245768 | tf_op jit(solution)/shard_map/ppermute | solution.py:570
  98.2 8.9 %collective-permute-start.9 = (bf16[80,512]{1,0:T(8,128)(2,1)S(1)}, bf16[80,512]{1,0:T(8,128)(2,1)S(1)}, u32[]{:S(2)}, u32[]{:S(2)}) collective-permute-start(bf16[80,512]{1,0:T(8,128)(2,1)S(1)} %get-tuple-element.90), channel_id=1, source_target_pairs={{0,24},{4,28},{8,16},{12,20},{16,8},{20,12},{24,0},{28,4},{1,25},{... | collective-permute-start | bytes 245768 | tf_op jit(solution)/shard_map/ppermute | solution.py:570
  107.1 11.6 %collective-permute-start.13 = (bf16[80,512]{1,0:T(8,128)(2,1)S(1)}, bf16[80,512]{1,0:T(8,128)(2,1)S(1)}, u32[]{:S(2)}, u32[]{:S(2)}) collective-permute-start(bf16[80,512]{1,0:T(8,128)(2,1)S(1)} %late_plane.1.refs_0_), channel_id=1, source_target_pairs={{0,1},{1,0},{2,3},{3,2},{4,5},{5,4},{6,7},{7,6},{8,9},{9,8},{10,11... | collective-permute-start | bytes 245768 | tf_op jit(solution)/shard_map/ppermute | solution.py:574
  109.0 19.3 %collective-permute-start.14 = (bf16[80,512]{1,0:T(8,128)(2,1)S(1)}, bf16[80,512]{1,0:T(8,128)(2,1)S(1)}, u32[]{:S(2)}, u32[]{:S(2)}) collective-permute-start(bf16[80,512]{1,0:T(8,128)(2,1)S(1)} %late_plane.1.refs_0_), channel_id=1, source_target_pairs={{0,2},{1,3},{2,0},{3,1},{4,6},{5,7},{6,4},{7,5},{8,10},{9,11},{10,... | collective-permute-start | bytes 245768 | tf_op jit(solution)/shard_map/ppermute | solution.py:574
  109.0 19.3 %collective-permute-start.15 = (bf16[80,512]{1,0:T(8,128)(2,1)S(1)}, bf16[80,512]{1,0:T(8,128)(2,1)S(1)}, u32[]{:S(2)}, u32[]{:S(2)}) collective-permute-start(bf16[80,512]{1,0:T(8,128)(2,1)S(1)} %late_plane.1.refs_0_), channel_id=1, source_target_pairs={{0,3},{1,2},{2,1},{3,0},{4,7},{5,6},{6,5},{7,4},{8,11},{9,10},{10,... | collective-permute-start | bytes 245768 | tf_op jit(solution)/shard_map/ppermute | solution.py:574
  117.4 11.0 %collective-permute-start.16 = (bf16[64,1536]{1,0:T(8,128)(2,1)S(1)}, bf16[64,1536]{1,0:T(8,128)(2,1)S(1)}, u32[]{:S(2)}, u32[]{:S(2)}) collective-permute-start(bf16[64,1536]{1,0:T(8,128)(2,1)S(1)} %early_line.1.own_ref), channel_id=1, source_target_pairs={{0,8},{4,12},{8,0},{12,4},{16,24},{20,28},{24,16},{28,20},{1,9},{5... | collective-permute-start | bytes 589832 | tf_op jit(solution)/shard_map/ppermute | solution.py:570
  117.4 10.9 %collective-permute-start.17 = (bf16[64,1536]{1,0:T(8,128)(2,1)S(1)}, bf16[64,1536]{1,0:T(8,128)(2,1)S(1)}, u32[]{:S(2)}, u32[]{:S(2)}) collective-permute-start(bf16[64,1536]{1,0:T(8,128)(2,1)S(1)} %early_line.1.own_ref), channel_id=1, source_target_pairs={{0,16},{4,20},{8,24},{12,28},{16,0},{20,4},{24,8},{28,12},{1,17},{... | collective-permute-start | bytes 589832 | tf_op jit(solution)/shard_map/ppermute | solution.py:570
  118.7 9.6 %collective-permute-start.18 = (bf16[64,1536]{1,0:T(8,128)(2,1)S(1)}, bf16[64,1536]{1,0:T(8,128)(2,1)S(1)}, u32[]{:S(2)}, u32[]{:S(2)}) collective-permute-start(bf16[64,1536]{1,0:T(8,128)(2,1)S(1)} %early_line.1.own_ref), channel_id=1, source_target_pairs={{0,24},{4,28},{8,16},{12,20},{16,8},{20,12},{24,0},{28,4},{1,25},{... | collective-permute-start | bytes 589832 | tf_op jit(solution)/shard_map/ppermute | solution.py:570
  128.3 0.7 copy-start.5
  129.5 12.1 %copy-start.7 = (bf16[256,1536]{1,0:T(8,128)(2,1)}, bf16[256,1536]{1,0:T(8,128)(2,1)S(1)}, u32[]{:S(2)}) copy-start(bf16[256,1536]{1,0:T(8,128)(2,1)S(1)} %early_gather.1.mine_ref) | copy-start | bytes 2359300
  129.5 12.1 %collective-permute-start.22 = (bf16[256,1536]{1,0:T(8,128)(2,1)S(1)}, bf16[256,1536]{1,0:T(8,128)(2,1)S(1)}, u32[]{:S(2)}, u32[]{:S(2)}) collective-permute-start(bf16[256,1536]{1,0:T(8,128)(2,1)S(1)} %early_gather.1.mine_ref), channel_id=1, source_target_pairs={{0,4},{4,0},{8,12},{12,8},{16,20},{20,16},{24,28},{28,24},{1,5},{5... | collective-permute-start | bytes 2359304 | tf_op jit(solution)/shard_map/ppermute | solution.py:565
  133.6 3.6 %collective-permute-start.19 = (bf16[64,512]{1,0:T(8,128)(2,1)S(1)}, bf16[64,512]{1,0:T(8,128)(2,1)S(1)}, u32[]{:S(2)}, u32[]{:S(2)}) collective-permute-start(bf16[64,512]{1,0:T(8,128)(2,1)S(1)} %slice.43), channel_id=1, source_target_pairs={{0,8},{4,12},{8,0},{12,4},{16,24},{20,28},{24,16},{28,20},{1,9},{5... | collective-permute-start | bytes 196616 | tf_op jit(solution)/shard_map/ppermute | solution.py:570
  133.8 3.4 %collective-permute-start.20 = (bf16[64,512]{1,0:T(8,128)(2,1)S(1)}, bf16[64,512]{1,0:T(8,128)(2,1)S(1)}, u32[]{:S(2)}, u32[]{:S(2)}) collective-permute-start(bf16[64,512]{1,0:T(8,128)(2,1)S(1)} %slice.43), channel_id=1, source_target_pairs={{0,16},{4,20},{8,24},{12,28},{16,0},{20,4},{24,8},{28,12},{1,17},{... | collective-permute-start | bytes 196616 | tf_op jit(solution)/shard_map/ppermute | solution.py:570
  135.1 4.0 %collective-permute-start.21 = (bf16[64,512]{1,0:T(8,128)(2,1)S(1)}, bf16[64,512]{1,0:T(8,128)(2,1)S(1)}, u32[]{:S(2)}, u32[]{:S(2)}) collective-permute-start(bf16[64,512]{1,0:T(8,128)(2,1)S(1)} %slice.43), channel_id=1, source_target_pairs={{0,24},{4,28},{8,16},{12,20},{16,8},{20,12},{24,0},{28,4},{1,25},{... | collective-permute-start | bytes 196616 | tf_op jit(solution)/shard_map/ppermute | solution.py:570
  139.7 7.8 %copy-start = (bf16[512,512]{1,0:T(8,128)(2,1)S(1)}, bf16[512,512]{1,0:T(8,128)(2,1)}, u32[]{:S(2)}) copy-start(bf16[512,512]{1,0:T(8,128)(2,1)} %multiply_convert_fusion.scaled.scaled_ref) | copy-start | bytes 1572868
  139.7 7.8 %copy-start.1 = (bf16[256,512]{1,0:T(8,128)(2,1)S(1)}, bf16[256,512]{1,0:T(8,128)(2,1)}, u32[]{:S(2)}) copy-start(bf16[256,512]{1,0:T(8,128)(2,1)} %imag_ref.1) | copy-start | bytes 786436
  139.7 7.8 %copy-start.2 = (bf16[256,512]{1,0:T(8,128)(2,1)S(1)}, bf16[256,512]{1,0:T(8,128)(2,1)}, u32[]{:S(2)}) copy-start(bf16[256,512]{1,0:T(8,128)(2,1)} %real_ref.1) | copy-start | bytes 786436
  139.7 7.8 %copy-start.6 = (s32[4]{0:T(128)S(1)}, s32[4]{0:T(128)}, u32[]{:S(2)}) copy-start(s32[4]{0:T(128)} %pad_add_fusion.first.place) | copy-start | bytes 52
  139.7 7.8 %copy-start.8 = (f32[512]{0:T(512)S(1)}, f32[512]{0:T(512)}, u32[]{:S(2)}) copy-start(f32[512]{0:T(512)} %param.17) | copy-start | bytes 6148
  139.7 7.8 %copy-start.9 = (f32[512]{0:T(512)S(1)}, f32[512]{0:T(512)}, u32[]{:S(2)}) copy-start(f32[512]{0:T(512)} %param.18) | copy-start | bytes 6148
  139.7 7.8 %copy-start.10 = (f32[512]{0:T(512)S(1)}, f32[512]{0:T(512)}, u32[]{:S(2)}) copy-start(f32[512]{0:T(512)} %param.26) | copy-start | bytes 6148
  139.7 7.6 %collective-permute-start.23 = (bf16[256,512]{1,0:T(8,128)(2,1)S(1)}, bf16[256,512]{1,0:T(8,128)(2,1)S(1)}, u32[]{:S(2)}, u32[]{:S(2)}) collective-permute-start(bf16[256,512]{1,0:T(8,128)(2,1)S(1)} %late_gather.1.mine_ref), channel_id=1, source_target_pairs={{0,4},{4,0},{8,12},{12,8},{16,20},{20,16},{24,28},{28,24},{1,5},{5... | collective-permute-start | bytes 786440 | tf_op jit(solution)/shard_map/ppermute | solution.py:565
  141.6 0.9 copy-start.18
  147.3 5.2 %copy-start.15 = (f32[256]{0:T(256)S(1)}, f32[256]{0:T(256)}, u32[]{:S(2)}) copy-start(f32[256]{0:T(256)} %param.22) | copy-start | bytes 3076
  147.3 5.2 %copy-start.16 = (f32[256]{0:T(256)S(1)}, f32[256]{0:T(256)}, u32[]{:S(2)}) copy-start(f32[256]{0:T(256)} %param.21) | copy-start | bytes 3076
  147.3 5.2 %copy-start.17 = (f32[256]{0:T(256)S(1)}, f32[256]{0:T(256)}, u32[]{:S(2)}) copy-start(f32[256]{0:T(256)} %param.23) | copy-start | bytes 3076

commit v3 on v2

--- a/solution.py
+++ b/solution.py
@@ -12,10 +12,13 @@
 SUBLANES = 8
 LANES = 128
 EXTRA = 16
+INPUT_BLOCK = 512
+MIDDLE_CHUNK = 512
 F32 = jnp.float32
 BF16 = jnp.bfloat16
 VMEM_LIMIT = 60 * 1024 * 1024
 GLUE_LIMIT = 16 * 1024 * 1024
+FULL_LIMIT = 67043328
 
 
 def nt_dot(left, right):
@@ -163,14 +166,14 @@
 
 
 def forward_kernel(
-    lens, first, x_ref, gain, bias, scaled, lam, drive_ref, xhat_ref, rstd_ref, ends_ref,
+    lens, x_ref, gain, bias, scaled, lam, drive_ref, xhat_ref, rstd_ref, ends_ref,
     fin_ref, work, keep, segs
 ):
     row = pl.program_id(0)
     toks = x_ref.shape[1]
     n = lam.shape[1]
     span = toks // SEGMENTS
-    fill_keep(lens, row, first[0], keep, segs, span)
+    fill_keep(lens, row, lax.axis_index("seq") * toks, keep, segs, span)
     chunk = 256
     for c in range(toks // chunk):
         part = slice(c * chunk, (c + 1) * chunk)
@@ -184,7 +187,7 @@
         drive = nt_dot(low, scaled[...]).astype(BF16)
         drive_ref[0, part, :] = drive
         to_blocks(work, part, drive.astype(F32))
-    real, imag = lam[0:1, :], lam[1:2, :]
+    real, imag = lam[6:7, :], lam[7:8, :]
     ends = ends_ref.at[0]
     segment_ends(work, keep, lane_blocks(real), lane_blocks(imag), ends, span, False)
     zero = jnp.zeros((1, n), F32)
@@ -193,12 +196,13 @@
     fin_ref[0, :, n : 2 * n] = ci
 
 
+LOG2E = 1.4426950408889634
 TAIL_P = 0.3275911 * 0.7071067811865476
 TAIL = (0.254829592, -0.284496736, 1.421413741, -1.453152027, 1.061405429)
 
 
 def gelu_parts(m):
-    bell = jnp.exp(-0.5 * m * m)
+    bell = jnp.exp2((-0.5 * LOG2E) * (m * m))
     t = 1.0 / (1.0 + TAIL_P * jnp.abs(m))
     poly = t * (0.5 * TAIL[0] + t * (0.5 * TAIL[1] + t * (0.5 * TAIL[2] + t * (0.5 * TAIL[3] + t * (0.5 * TAIL[4])))))
     tail = poly * bell
@@ -207,7 +211,7 @@
 
 def middle_kernel(
     lens, first, drive_ref, ends_ref, carry_ref, xhat_ref, x_ref, og_ref, lam, out_cat, gain,
-    bias, skip, wv, wg, gbias, block_ref, gm_ref, gs_ref, st_ref, bends_ref, bfin_ref, mine_ref,
+    bias, skip, wv_ref, wg_ref, gbias, block_ref, gm_ref, gs_ref, st_ref, bends_ref, bfin_ref, mine_ref,
     send_ref, gbias_ref, sums_ref, work, keep, segs, done, inits, act_s, gvg_s, acc
 ):
     row = pl.program_id(0)
@@ -225,7 +229,7 @@
     fill_keep(lens, row, first[0], keep, segs, span)
     everything = slice(0, toks)
     to_blocks(work, everything, drive_ref[0].astype(F32))
-    real, imag = lam[0:1, :], lam[1:2, :]
+    real, imag = lam[6:7, :], lam[7:8, :]
     half = n // LANES
     real_b, imag_b = lane_blocks(real), lane_blocks(imag)
     compose_segments(
@@ -255,46 +259,44 @@
     limit = -first[0]
     for j in range(docs - 1):
         limit = limit + lens[row, j]
-    chunk = 256
-    ones = jnp.ones((SUBLANES, chunk), BF16)
-
-    @pl.loop(0, toks // chunk)
-    def _(c):
-        part = pl.ds(pl.multiple_of(c * chunk, chunk), chunk)
+    chunk = MIDDLE_CHUNK
+    mix_gain, mix_bias = gain[...] * skip[...], bias[...] * skip[...]
+    half_bias = 0.5 * gbias[...]
+    wv, wg = wv_ref[...] * BF16(0.5), wg_ref[...] * BF16(0.5)
+    for c in range(toks // chunk):
+        part = slice(c * chunk, (c + 1) * chunk)
         state = from_blocks(done, part).astype(BF16)
         st_ref[0, part, :] = state
         xhat = xhat_ref[0, part, :].astype(F32)
-        mixed = nt_dot(state, out_cat[...]) + (xhat * (gain[...] * skip[...]) + bias[...] * skip[...])
+        mixed = nt_dot(state, out_cat[...]) + (xhat * mix_gain + mix_bias)
         cdf, bell = gelu_parts(mixed)
         act = (mixed * cdf).astype(BF16)
         act_s[part, :] = act
         slope = cdf + mixed * (bell * 0.3989422804014327)
-        value = nn_dot(act, wv[...]) + gbias[:, 0:width]
-        gate = nn_dot(act, wg[...]) + gbias[:, width : 2 * width]
-        sigma = 0.5 * jnp.tanh(0.5 * gate) + 0.5
-        gated = value * sigma
+        value = nn_dot(act, wv) + half_bias[:, 0:width]
+        tanh = jnp.tanh(nn_dot(act, wg) + half_bias[:, width : 2 * width])
+        u = 1.0 + tanh
+        gated = value * u
         block_ref[0, part, :] = (x_ref[0, part, :].astype(F32) + gated).astype(BF16)
         place = lax.broadcasted_iota(jnp.int32, (chunk, width), 0) + c * chunk
         grad = jnp.where(place < limit, og_ref[0, part, :].astype(F32), 0.0)
-        gv = (grad * sigma).astype(BF16)
-        gg = (grad * gated * (1.0 - sigma)).astype(BF16)
+        gv = grad * u
+        gg = grad * gated * (1.0 - tanh)
+        gbias_ref[0:1, 0:width] += jnp.sum(gv, axis=0, keepdims=True)
+        gbias_ref[0:1, width : 2 * width] += jnp.sum(gg, axis=0, keepdims=True)
+        gv, gg = gv.astype(BF16), gg.astype(BF16)
         gvg_s[part, 0:width] = gv
         gvg_s[part, width : 2 * width] = gg
-        gbias_ref[0:1, 0:width] += jnp.sum(gv.astype(F32), axis=0, keepdims=True)
-        gbias_ref[0:1, width : 2 * width] += jnp.sum(gg.astype(F32), axis=0, keepdims=True)
-        gact = nt_dot(gv, wv[...]) + nt_dot(gg, wg[...])
-        gm = (gact * slope).astype(BF16)
+        gm = (nt_dot(gv, wv) + nt_dot(gg, wg)) * slope
+        sums_ref[0:1, :] += jnp.sum(gm, axis=0, keepdims=True)
+        sums_ref[1:2, :] += jnp.sum(gm * xhat, axis=0, keepdims=True)
+        gm = gm.astype(BF16)
         gm_ref[0, part, :] = gm
-        gmf = gm.astype(F32)
-        sums_ref[0:1, :] += jnp.sum(gmf, axis=0, keepdims=True)
-        sums_ref[1:2, :] += jnp.sum(gmf * xhat, axis=0, keepdims=True)
-        gs = nn_dot(gm, out_cat[...]).astype(BF16)
-        gs_ref[0, part, :] = gs
-        to_blocks(work, part, gs.astype(F32))
-
+        gs = nn_dot(gm, out_cat[...])
+        gs_ref[0, part, :] = gs.astype(BF16)
+        to_blocks(work, part, gs)
     acc[:, 0 : 2 * width] += tn_dot(act_s[...], gvg_s[...])
     acc[:, 2 * width :] += tn_dot(gm_ref[0], st_ref[0])
-
     fill_keep(lens, row, first[0] + 1, keep, segs, span)
     bends = bends_ref.at[0]
     segment_ends(work, keep, real_b, lane_blocks(imag, -1.0), bends, span, True)
@@ -305,6 +307,8 @@
 
     @pl.when(row == pl.num_programs(0) - 1)
     def _():
+        acc[:, 0 : 2 * width] = 0.5 * acc[:, 0 : 2 * width]
+        gbias_ref[...] = 0.5 * gbias_ref[...]
         split_halves(acc, first[1], mine_ref, send_ref)
 
 
@@ -346,7 +350,7 @@
     everything = slice(0, toks)
     to_blocks(work, everything, gs_ref[0].astype(F32))
     to_blocks(state, everything, st_ref[0].astype(F32))
-    real, imag = lam[0:1, :], -lam[1:2, :]
+    real, imag = lam[6:7, :], -lam[7:8, :]
     half = n // LANES
     real_b, imag_b = lane_blocks(real), lane_blocks(imag)
     compose_segments(
@@ -409,25 +413,18 @@
 ):
     ig_ref = refs[-1]
     row = pl.program_id(0) + begin
-    toks, width = xhat_ref.shape[1], xhat_ref.shape[2]
-    docs = lens.shape[1]
-    limit = -first[0]
-    for j in range(docs - 1):
+    tall, width = xhat_ref.shape[1], xhat_ref.shape[2]
+    limit = -first[0] - pl.program_id(1) * tall
+    for j in range(lens.shape[1] - 1):
         limit = limit + lens[row, j]
-    chunk = 256
-    mix = gain[...] * skip[...]
-
-    @pl.loop(0, toks // chunk)
-    def _(c):
-        part = pl.ds(pl.multiple_of(c * chunk, chunk), chunk)
-        xhat = xhat_ref[0, part, :].astype(F32)
-        g = nn_dot(adj_ref[0, part, :], scaled[...]) * gain[...]
-        g = g + gm_ref[0, part, :].astype(F32) * mix
-        place = lax.broadcasted_iota(jnp.int32, (chunk, width), 0) + c * chunk
-        grad = jnp.where(place < limit, og_ref[0, part, :].astype(F32), 0.0)
-        m1 = jnp.mean(g, axis=-1, keepdims=True)
-        m2 = jnp.mean(g * xhat, axis=-1, keepdims=True)
-        ig_ref[0, part, :] = (grad + rstd_ref[0, part, 0:1] * (g - m1 - xhat * m2)).astype(BF16)
+    xhat = xhat_ref[0].astype(F32)
+    g = nn_dot(adj_ref[0], scaled[...]) * gain[...]
+    g = g + gm_ref[0].astype(F32) * (gain[...] * skip[...])
+    place = lax.broadcasted_iota(jnp.int32, (tall, width), 0)
+    grad = jnp.where(place < limit, og_ref[0].astype(F32), 0.0)
+    m1 = jnp.mean(g, axis=-1, keepdims=True)
+    m2 = jnp.mean(g * xhat, axis=-1, keepdims=True)
+    ig_ref[0] = (grad + rstd_ref[0, :, 0:1] * (g - m1 - xhat * m2)).astype(BF16)
 
 
 def tree_sum(items):
@@ -436,21 +433,29 @@
     return items[0]
 
 
-def split_kernel(extra, place, mine_ref, got_ref, own_ref, *send_refs):
+def split_kernel(extra, bits, place, mine_ref, got_ref, *refs):
     half = mine_ref.shape[0] - extra
-    piece = own_ref.shape[0] - extra
+    piece = refs[0].shape[0] - extra
+    own = seat_of(place, bits)
 
     def part(index):
         rows = pl.ds(pl.multiple_of(index * piece, piece), piece)
         return mine_ref[rows, :].astype(F32) + got_ref[rows, :].astype(F32)
 
-    refs = (own_ref,) + send_refs
     for j, ref in enumerate(refs):
-        ref[0:piece, :] = part(place[2] ^ j).astype(BF16)
+        ref[0:piece, :] = part(own ^ j).astype(BF16)
     if extra:
         vec = get_pair(mine_ref, half) + get_pair(got_ref, half)
         for ref in refs:
             put_pair(vec, ref, piece)
+
+
+def seat_of(place, bits):
+    low, high = bits
+    index = place[1 + low]
+    for k in range(low + 1, high):
+        index = index + (place[1 + k] << (k - low))
+    return index
 
 
 def sum_kernel(extra, *refs):
@@ -461,61 +466,94 @@
         put_pair(tree_sum([get_pair(r, rows) for r in refs[:-1]]), out, rows)
 
 
-def gather_kernel(place, own_ref, *refs):
+def gather_kernel(bits, place, *refs):
     out_ref = refs[-1]
-    piece = refs[0].shape[0]
-    for j, ref in enumerate((own_ref,) + refs[:-1]):
-        rows = pl.ds(pl.multiple_of((place[2] ^ j) * piece, piece), piece)
+    count = len(refs) - 1
+    piece = out_ref.shape[0] // count
+    own = seat_of(place, bits)
+    for j, ref in enumerate(refs[:-1]):
+        rows = pl.ds(pl.multiple_of((own ^ j) * piece, piece), piece)
         out_ref[rows, :] = ref[0:piece, :]
 
 
 def weights_kernel(place, mine_ref, got_ref, value_ref, gate_ref, real_ref, imag_ref):
     width = value_ref.shape[1]
     n = real_ref.shape[1]
-    total = jnp.where(pl.program_id(0) == 0, mine_ref[...], got_ref[...]).astype(F32)
-    value_ref[...] = total[:, 0:width]
-    gate_ref[...] = total[:, width : 2 * width]
-    real_ref[...] = total[:, 2 * width : 2 * width + n]
-    imag_ref[...] = -total[:, 2 * width + n :]
-
-
-def exact_dot(left, right, dims):
-    return lax.dot_general(
-        left, right, (dims, ((), ())), precision=lax.Precision.HIGHEST, preferred_element_type=F32
-    )
+
+    def put(ref):
+        value_ref[...] = ref[:, 0:width].astype(F32)
+        gate_ref[...] = ref[:, width : 2 * width].astype(F32)
+        real_ref[...] = ref[:, 2 * width : 2 * width + n].astype(F32)
+        imag_ref[...] = -ref[:, 2 * width + n :].astype(F32)
+
+    @pl.when(pl.program_id(0) == 0)
+    def _():
+        put(mine_ref)
+
+    @pl.when(pl.program_id(0) == 1)
+    def _():
+        put(got_ref)
 
 
 def last_kernel(
-    place, mine_ref, got_ref, own_ref, scaled_ref, real_ref, imag_ref, scale_ref, gain, bias, skip,
-    real_out, imag_out, small_out
+    place, mine_ref, got_ref, own_ref, scaled_ref, real_ref, imag_ref, coef, gain, bias, skip,
+    real_out, imag_out, gain_out, shift_out, skip_out, decay_out, angle_out, scale_out, gbias_out
 ):
     n, width = real_ref.shape
     vec = get_pair(own_ref, own_ref.shape[0] - 2 * SUBLANES)
     sum_gm, sum_gmx = vec[2:3, :], vec[3:4, :]
-    col = jnp.broadcast_to(vec[5:6, :], (SUBLANES, 2 * n))
-    lead = lax.broadcasted_iota(jnp.int32, (SUBLANES, width), 0) == 0
-    spread = exact_dot(jnp.where(lead, col, 0.0), jnp.broadcast_to(bias[...], (SUBLANES, width)),
-                       ((0,), (0,)))
-    ones = jnp.ones((SUBLANES, width), F32)
-    shift = exact_dot(col, scaled_ref[...].astype(F32), ((1,), (0,)))
-    gain_sum = jnp.zeros((1, width), F32)
-    scale_grad = jnp.zeros((SUBLANES, n), F32)
+    col = jnp.transpose(vec)[:, 5:6]
+    scale = jnp.transpose(coef[...])[:, 5:6]
+    gain_sum = skip[...] * sum_gmx
+    shift = skip[...] * sum_gm
     first_core = place[1] == 0
+    scale_sums = jnp.zeros((n, 1), F32)
     for part, weight_ref, out_ref in ((0, real_ref, real_out), (1, imag_ref, imag_out)):
         rows = slice(part * n, (part + 1) * n)
         keep_mine = first_core if part == 0 else jnp.logical_not(first_core)
         total = jnp.where(keep_mine, mine_ref[...], got_ref[...]).astype(F32)
-        gain_sum = gain_sum + jnp.sum(total * scaled_ref[rows, :].astype(F32), axis=0, keepdims=True)
-        full = total * gain[...] + spread[rows, :]
-        out_ref[...] = full * scale_ref[rows, 0:1]
-        scale_grad = scale_grad + exact_dot(ones, full * weight_ref[...].astype(F32), ((1,), (1,)))
-    small_out[0:1, :] = gain_sum + skip[...] * sum_gmx
-    small_out[1:2, :] = shift[0:1, :] + skip[...] * sum_gm
-    small_out[2:3, :] = gain[...] * sum_gmx + bias[...] * sum_gm
-    small_out[3:4, :] = jnp.concatenate([scale_grad[0:1, :]] * 2, axis=1)
-    small_out[4:5, :] = vec[4:5, :]
-    small_out[5:7, :] = vec[0:2, :]
-    small_out[7:8, :] = jnp.zeros((1, width), F32)
+        scaled = scaled_ref[rows, :].astype(F32)
+        gain_sum = gain_sum + jnp.sum(total * scaled, axis=0, keepdims=True)
+        shift = shift + jnp.sum(col[rows, :] * scaled, axis=0, keepdims=True)
+        full = total * gain[...] + col[rows, :] * bias[...]
+        out_ref[...] = full * scale
+        scale_sums = scale_sums + jnp.sum(
+            full * weight_ref[...].astype(F32), axis=1, keepdims=True
+        )
+    scale_grad = jnp.transpose(jnp.broadcast_to(scale_sums, (n, LANES)))[0:1, :]
+    lr, li = vec[4:5, 0:n], vec[4:5, n : 2 * n]
+    radius_grad = lr * coef[0:1, :] + li * coef[1:2, :]
+    gain_out[...] = gain_sum.reshape(width)
+    shift_out[...] = shift.reshape(width)
+    skip_out[...] = (gain[...] * sum_gmx + bias[...] * sum_gm).reshape(width)
+    decay_out[...] = (scale_grad * coef[4:5, :] - radius_grad * coef[3:4, :]).reshape(n)
+    angle_out[...] = (coef[2:3, :] * (li * coef[0:1, :] - lr * coef[1:2, :])).reshape(n)
+    scale_out[...] = (scale_grad * coef[5:6, :]).reshape(n)
+    gbias_out[0:width] = vec[0, :]
+    gbias_out[width : 2 * width] = vec[1, :]
+
+
+def prepare_kernel(
+    decay_log, angle_log, scale_log, real_ref, imag_ref, out_real, out_imag, coef, scaled_ref, out_cat
+):
+    n = real_ref.shape[0]
+    rate = jnp.exp(decay_log[...])
+    radius = jnp.exp(-rate)
+    angle = jnp.exp(angle_log[...])
+    cosine, sine = jnp.cos(angle), jnp.sin(angle)
+    shrink = jnp.exp(-2.0 * rate)
+    root = jnp.sqrt(1.0 - shrink)
+    grown = jnp.exp(scale_log[...])
+    scale = grown * root
+    rows = (cosine, sine, radius * angle, radius * rate, grown * shrink * rate / root, scale,
+            radius * cosine, radius * sine)
+    for i, row in enumerate(rows):
+        coef[i : i + 1, :] = row
+    column = jnp.transpose(coef[...])[:, 5:6]
+    scaled_ref[0:n, :] = (real_ref[...].astype(F32) * column).astype(BF16)
+    scaled_ref[n : 2 * n, :] = (imag_ref[...].astype(F32) * column).astype(BF16)
+    out_cat[:, 0:n] = out_real[...]
+    out_cat[:, n : 2 * n] = -out_imag[...]
 
 
 def whole(shape):
@@ -548,7 +586,7 @@
     return total
 
 
-def glue(kernel, outs, *args, name, scalars=True):
+def glue(kernel, outs, *args, name, scalars=True, grant=GLUE_LIMIT):
     def spec(v):
         return pl.BlockSpec(v.shape, lambda i: (0,) * len(v.shape))
 
@@ -557,17 +595,13 @@
     return pl.pallas_call(
         kernel, grid=(1,), in_specs=specs, out_specs=[spec(v) for v in outs] if many else spec(outs),
         out_shape=outs, cost_estimate=cost(1.7),
-        compiler_params=pltpu.CompilerParams(vmem_limit_bytes=GLUE_LIMIT), name=name,
+        compiler_params=pltpu.CompilerParams(vmem_limit_bytes=grant), name=name,
     )(*args)
 
 
-def from_core(v):
-    return lax.ppermute(v, "rows", [(i, i ^ 1) for i in range(lax.axis_size("rows"))])
-
-
-def from_plane(v, offset):
+def from_row(v, offset):
     count = lax.axis_size("rows")
-    return lax.ppermute(v, "rows", [(i, i ^ (2 * offset)) for i in range(count)])
+    return lax.ppermute(v, "rows", [(i, i ^ offset) for i in range(count)])
 
 
 def from_line(v, offset):
@@ -579,46 +613,63 @@
 
 
 class Exchange:
-    def __init__(self, place, mine, send, extra, name):
-        self.place, self.mine, self.extra, self.name = place, mine, extra, name
-        self.plane = lax.axis_size("rows") // 2
-        self.line = lax.axis_size("seq")
-        self.half, self.cols = mine.shape[0] - extra, mine.shape[1]
-        self.piece = SDS((self.half // self.plane + extra, self.cols), BF16)
-        self.got = [from_core(send)]
+    def __init__(self, mine, send, extra, stages, name, hops):
+        self.mine, self.extra, self.stages, self.name = mine, extra, stages, name
+        self.hops = hops
+        self.cut, self.back = 0, len(stages) - 1
+        self.got = [from_row(send, 1)]
+
+    def rows(self, count):
+        return SDS((count, self.mine.shape[1]), BF16)
 
     def split(self, place):
-        self.own, *cuts = glue(
-            functools.partial(split_kernel, self.extra), [self.piece] * self.plane, place,
+        self.cut += 1
+        bits = self.stages[self.cut]
+        pieces = 1 << (bits[1] - bits[0])
+        piece = (self.mine.shape[0] - self.extra) // pieces + self.extra
+        self.mine, *cuts = glue(
+            functools.partial(split_kernel, self.extra, bits), [self.rows(piece)] * pieces, place,
             self.mine, *self.got, name=self.name + "_split"
         )
-        self.got = [from_plane(c, j + 1) for j, c in enumerate(cuts)]
-        return self.own
-
-    def add(self, step, own=None):
-        return glue(
-            functools.partial(sum_kernel, self.extra), self.piece,
-            self.own if own is None else own, *self.got, name=self.name + step, scalars=False
+        self.got = [from_row(c, (j + 1) << bits[0]) for j, c in enumerate(cuts)]
+        return self.mine
+
+    def add(self, place):
+        self.mine = glue(
+            drop_place(functools.partial(sum_kernel, self.extra)), self.rows(self.mine.shape[0]),
+            place, self.mine, *self.got, name=self.name + "_sum"
         )
-
-    def add_plane(self, own=None):
-        self.own = self.add("_plane", own)
-        self.got = [from_line(self.own, j) for j in range(1, self.line)]
-        return self.own
-
-    def add_line(self, own=None):
-        self.own = self.add("_line", own)
-        total = self.own[: self.half // self.plane] if self.extra else self.own
-        self.got = [from_plane(total, j) for j in range(1, self.plane)]
-        return self.own
+        if self.hops:
+            offsets, *self.hops = self.hops
+            self.got = [from_line(self.mine, j) for j in offsets]
+            return self.mine
+        self.total = self.mine
+        if self.extra:
+            self.mine = self.mine[: self.mine.shape[0] - self.extra]
+        self.send_back()
+        return self.total
+
+    def send_back(self):
+        low, high = self.stages[self.back]
+        self.got = [from_row(self.mine, j << low) for j in range(1, 1 << (high - low))]
 
     def gather(self, place):
+        bits = self.stages[self.back]
+        pieces = [self.mine] + self.got
         self.mine = glue(
-            gather_kernel, SDS((self.half, self.cols), BF16), place, self.own, *self.got,
-            name=self.name + "_gather"
+            functools.partial(gather_kernel, bits), self.rows(len(pieces) * self.mine.shape[0]),
+            place, *pieces, name=self.name + "_gather"
         )
-        self.got = [from_core(self.mine)]
+        self.back -= 1
+        self.send_back()
         return self.mine
+
+
+def drop_place(kernel):
+    def call(place, *refs):
+        kernel(*refs)
+
+    return call
 
 
 def cost(us):
@@ -638,15 +689,15 @@
     ]
 
 
-def run_forward(lens, place, x, gain, bias, scaled, lam):
+def run_forward(lens, x, gain, bias, scaled, lam):
     rows_here, toks, width = x.shape
     n = lam.shape[1]
     act = per_row(toks, width)
     return pl.pallas_call(
         forward_kernel,
         grid=(rows_here,),
-        in_specs=[SCALARS, SCALARS, act, whole((1, width)), whole((1, width)),
-                  whole((2 * n, width)), whole((2, n))],
+        in_specs=[SCALARS, act, whole((1, width)), whole((1, width)),
+                  whole((2 * n, width)), whole((8, n))],
         out_specs=[per_row(toks, 2 * n), act, per_row(toks, 128), per_row(SEGMENTS, 2 * n),
                    per_row(1, 2 * n)],
         out_shape=[SDS((rows_here, toks, 2 * n), BF16), SDS(x.shape, BF16),
@@ -656,7 +707,7 @@
         compiler_params=PARAMS,
         cost_estimate=cost(10.6),
         name="forward",
-    )(lens, place, x, gain, bias, scaled, lam)
+    )(lens, x, gain, bias, scaled, lam)
 
 
 def run_middle(
@@ -670,7 +721,7 @@
         middle_kernel,
         grid=(rows_here,),
         in_specs=[SCALARS, SCALARS, chan, per_row(SEGMENTS, 2 * n),
-                  per_row(1, 2 * n), act, act, act, whole((2, n)), whole((width, 2 * n)),
+                  per_row(1, 2 * n), act, act, act, whole((8, n)), whole((width, 2 * n)),
                   whole((1, width)), whole((1, width)), whole((1, width)),
                   whole((width, width)), whole((width, width)), whole((1, 2 * width))],
         out_specs=[act, act, chan, chan, per_row(SEGMENTS, 2 * n), per_row(1, 2 * n),
@@ -683,8 +734,8 @@
                    SDS((2, width), F32)],
         scratch_shapes=scan_scratch(toks, n) + [
             pltpu.VMEM((2 * n // LANES, toks, LANES), F32), pltpu.VMEM((SEGMENTS, 2 * n), F32),
-            pltpu.VMEM((toks, width), BF16),
-            pltpu.VMEM((toks, 2 * width), BF16), pltpu.VMEM((width, cols), F32)],
+            pltpu.VMEM((toks, width), BF16), pltpu.VMEM((toks, 2 * width), BF16),
+            pltpu.VMEM((width, cols), F32)],
         compiler_params=PARAMS,
         cost_estimate=cost(48),
         name="middle",
@@ -699,7 +750,7 @@
         adjoint_kernel,
         grid=(rows_here,),
         in_specs=[SCALARS, SCALARS, chan, per_row(SEGMENTS, 2 * n), per_row(1, 2 * n), chan, act,
-                  whole((2, n)), whole((1, 2 * width)), whole((2, width))],
+                  whole((8, n)), whole((1, 2 * width)), whole((2, width))],
         out_specs=[chan, whole((n + EXTRA, width)), whole((n + EXTRA, width))],
         out_shape=[SDS((rows_here, toks, 2 * n), BF16), SDS((n + EXTRA, width), BF16),
                    SDS((n + EXTRA, width), BF16)],
@@ -717,23 +768,28 @@
     rows_here, toks, width = xhat.shape
     end = rows_here if end is None else end
 
-    def rows(*shape):
-        return pl.BlockSpec((1,) + shape, lambda r: (r + begin if begin else r, 0, 0))
+    tall = INPUT_BLOCK
+
+    def rows(_, lanes):
+        return pl.BlockSpec((1, tall, lanes), lambda r, t: (r + begin if begin else r, t, 0))
+
+    def fixed(shape):
+        return pl.BlockSpec(shape, lambda r, t: (0,) * len(shape))
 
     act = rows(toks, width)
     args = (lens, place, adj, xhat, gm, og, rstd, scaled, gain, skip)
     specs = [SCALARS, SCALARS, rows(toks, adj.shape[2]), act, act, act,
-             rows(toks, 128), whole(scaled.shape), whole((1, width)), whole((1, width))]
+             rows(toks, 128), fixed(scaled.shape), fixed((1, width)), fixed((1, width))]
     if into is not None:
         args, specs = args + (into,), specs + [pl.BlockSpec(memory_space=pl.ANY)]
     return pl.pallas_call(
         functools.partial(input_kernel, begin),
-        grid=(end - begin,),
+        grid=(end - begin, toks // tall),
         in_specs=specs,
         out_specs=act,
         out_shape=SDS(xhat.shape, BF16),
         input_output_aliases={} if into is None else {len(args) - 1: 0},
-        compiler_params=PARAMS,
+        compiler_params=pltpu.CompilerParams(vmem_limit_bytes=VMEM_LIMIT),
         cost_estimate=cost(8),
         name="input",
     )(*args)
@@ -741,9 +797,10 @@
 
 def run_weights(place, mine, got, width, n):
     half, cols = mine.shape
-    blocks = 2
+    blocks = 1
     tall = half // blocks
-    source = pl.BlockSpec((tall, cols), lambda p, i, place: (i, 0))
+    mine_spec = pl.BlockSpec((tall, cols), lambda p, i, place: (jnp.where(p == 0, i, blocks - 1), 0))
+    got_spec = pl.BlockSpec((tall, cols), lambda p, i, place: (jnp.where(p == 0, 0, i), 0))
 
     def out(c):
         return pl.BlockSpec((tall, c), lambda p, i, place: ((place[1] ^ p) * blocks + i, 0))
@@ -751,7 +808,7 @@
     return pl.pallas_call(
         weights_kernel,
         grid_spec=pltpu.PrefetchScalarGridSpec(
-            num_scalar_prefetch=1, grid=(2, blocks), in_specs=[source, source],
+            num_scalar_prefetch=1, grid=(2, blocks), in_specs=[mine_spec, got_spec],
             out_specs=[out(width), out(width), out(n), out(n)],
         ),
         out_shape=[SDS((2 * half, width), F32)] * 2 + [SDS((2 * half, n), F32)] * 2,
@@ -759,6 +816,22 @@
         cost_estimate=cost(4.8),
         name="early_out",
     )(place, mine, got)
+
+
+ORDER = (
+    "early_split",
+    "adjoint",
+    "early_add",
+    "late_split",
+    "input0",
+    "late_add",
+    "early_add",
+    "input1",
+    "late_add",
+    "early_gather",
+    "late_gather",
+    "early_out",
+)
 
 
 def body(
@@ -773,19 +846,16 @@
     length = toks * parts
     hops = max(1, (length // 4) // toks)
     row_seat = lax.axis_index("rows")
-    place = jnp.stack([seat * toks, row_seat % 2, row_seat // 2, seat]).astype(jnp.int32)
-    rate = jnp.exp(decay_log)
-    radius = jnp.exp(-rate)
-    angle = jnp.exp(angle_log)
-    cosine, sine = jnp.cos(angle), jnp.sin(angle)
-    norm_root = jnp.sqrt(1.0 - jnp.exp(-2.0 * rate))
-    scale = jnp.exp(scale_log) * norm_root
-    lam = jnp.stack([radius * cosine, radius * sine])
-    inputs = jnp.concatenate([input_real, input_imag], axis=0).astype(F32)
-    scale2 = jnp.concatenate([scale, scale])
-    scaled = (inputs * scale2[:, None]).astype(BF16)
-    scale_b = jnp.broadcast_to(scale2[:, None], (2 * n, LANES))
-    out_cat = jnp.concatenate([output_real, -output_imag], axis=1)
+    seat_bits = lax.axis_size("rows").bit_length() - 1
+    place = jnp.stack(
+        [seat * toks] + [(row_seat >> k) & 1 for k in range(seat_bits)]
+    ).astype(jnp.int32)
+    coef, scaled, out_cat = glue(
+        prepare_kernel,
+        [SDS((8, n), F32), SDS((2 * n, width), BF16), SDS((width, 2 * n), BF16)],
+        decay_log[None], angle_log[None], scale_log[None], input_real, input_imag, output_real,
+        output_imag, name="prepare", scalars=False, grant=FULL_LIMIT
+    )
     gain, bias, skip = layer_norm_gain[None], layer_norm_bias[None], skip_gain[None]
     gbias = glu_bias[None]
     through = back_through = None
@@ -793,59 +863,57 @@
         starts = jnp.cumsum(doc_lengths, axis=1) - doc_lengths - seat * toks
         clear = 1.0 - jnp.any((starts >= 0) & (starts < toks), axis=1).astype(F32)
         clear_next = 1.0 - jnp.any((starts >= 1) & (starts < toks + 1), axis=1).astype(F32)
-        fr, fi = power_of(lam[0], lam[1], toks)
+        fr, fi = power_of(coef[6], coef[7], toks)
         through = clear[:, None, None] * jnp.concatenate([fr, fi])[None, None]
         back_through = clear_next[:, None, None] * jnp.concatenate([fr, -fi])[None, None]
 
     drive, xhat, rstd, ends, fin = run_forward(
-        doc_lengths, place, tokens_in, gain, bias, scaled, lam
+        doc_lengths, tokens_in, gain, bias, scaled, coef
     )
     carry = carry_over(fin, through, "seq", parts, hops, False)
     block_out, gm, gs, st, bends, bfin, mine, send, gbias_g, sums = run_middle(
-        doc_lengths, place, drive, ends, carry, xhat, tokens_in, out_grad, lam, out_cat, gain,
+        doc_lengths, place, drive, ends, carry, xhat, tokens_in, out_grad, coef, out_cat, gain,
         bias, skip, glu_value, glu_gate, gbias
     )
     back_carry = carry_over(bfin, back_through, "seq", parts, hops, True)
-    early = Exchange(place, mine, send, 0, "early")
-    done = early.split(place)
-    adj, mine_in, send_in = run_adjoint(
-        doc_lengths, after(place, done), gs, bends, back_carry, st, xhat, lam, gbias_g, sums
-    )
-    late = Exchange(place, mine_in, send_in, EXTRA, "late")
-    early.add_plane(after(early.own, adj))
-    done = late.split(after(place, early.own))
+    stages = [(0, 1), (1, seat_bits)]
+    doubling = [[1 << k] for k in range(parts.bit_length() - 1)]
+    at_once = [list(range(1, parts))]
+    early = Exchange(mine, send, 0, stages, "early", at_once)
+    late = input_grad = None
+    done = place
     half_rows = rows_here // 2
-    args = (adj, xhat, gm, out_grad, rstd, scaled, gain, skip)
-    input_grad = run_input(doc_lengths, after(place, done), *args, 0, half_rows)
-    late.add_plane(after(late.own, input_grad))
-    early.add_line(after(early.own, late.own))
-    input_grad = run_input(
-        doc_lengths, after(place, early.own, late.own), *args, half_rows, rows_here, input_grad
-    )
-    late.add_line(after(late.own, input_grad))
-    done = early.gather(after(place, late.own))
-    done = late.gather(after(place, done))
-    value_g, gate_g, real_g, imag_g = run_weights(
-        after(place, done), early.mine, early.got[0], width, n
-    )
-    in_real_g, in_imag_g, small = glue(
+    for task in ORDER:
+        now = after(place, done)
+        if task == "adjoint":
+            adj, mine_in, send_in = run_adjoint(
+                doc_lengths, now, gs, bends, back_carry, st, xhat, coef, gbias_g, sums
+            )
+            late = Exchange(mine_in, send_in, EXTRA, stages, "late", at_once)
+            done = adj
+        elif task in ("input0", "input1"):
+            begin = 0 if input_grad is None else half_rows
+            input_grad = done = run_input(
+                doc_lengths, now, adj, xhat, gm, out_grad, rstd, scaled, gain, skip, begin,
+                begin + half_rows, input_grad
+            )
+        elif task == "early_out":
+            value_g, gate_g, real_g, imag_g = run_weights(now, early.mine, early.got[0], width, n)
+            done = value_g
+        else:
+            which, step = task.split("_")
+            done = getattr(early if which == "early" else late, step)(now)
+    in_real_g, in_imag_g, *vectors = glue(
         last_kernel,
-        [SDS((n, width), F32), SDS((n, width), F32), SDS((SUBLANES, width), F32)],
-        after(place, value_g), late.mine, late.got[0], late.own, scaled, input_real, input_imag,
-        scale_b, gain, bias, skip, name="late_out",
-    )
-    gain_grad, shift_grad, skip_grad = small[0], small[1], small[2]
-    scale_grad, lamg, gbias_g = small[3, :n], small[4], small[5:7].reshape(2 * width)
-    lr, li = lamg[:n], lamg[n:]
-    radius_grad = lr * cosine + li * sine
-    angle_grad = radius * (li * cosine - lr * sine) * angle
-    decay_grad = (
-        -radius_grad * radius * rate
-        + scale_grad * jnp.exp(scale_log) * jnp.exp(-2.0 * rate) * rate / norm_root
-    )
+        [SDS((n, width), F32)] * 2 + [SDS((width,), F32)] * 3 + [SDS((n,), F32)] * 3
+        + [SDS((2 * width,), F32)],
+        after(place, done), late.mine, late.got[0], late.total, scaled, input_real, input_imag,
+        coef, gain, bias, skip, name="late_out",
+    )
+    gain_grad, shift_grad, skip_grad, decay_grad, angle_grad, scale_grad, gbias_g = vectors
     return (
         block_out, input_grad, gain_grad, shift_grad, in_real_g, in_imag_g, decay_grad,
-        angle_grad, scale_grad * scale, real_g, imag_g, skip_grad, value_g, gate_g, gbias_g
+        angle_grad, scale_grad, real_g, imag_g, skip_grad, value_g, gate_g, gbias_g
     )
 
 

time: 154 us -> 140 us (0.909)
  the two profiles are of different devices: /device:TPU:17 before, /device:TPU:0 now
where the time goes in v3:
time: 140 us
  Pallas kernels  92.2 us (66%)
  starting transfers between devices  30.4 us (22%)
  waiting for transfers between devices  12.3 us (9%)
  local copies, waits for them, and re-layouts  3.3 us (2%)
    pallas_call x1, Pallas kernels, run_middle(): pl.pallas_call(middle_kernel, grid=(rows_here,), in_specs=[SCALARS, SCALA...  40.9 us
    pallas_call x2, Pallas kernels, run_input(): pl.pallas_call(functools.partial(input_kernel, begin), grid=(end - begin,...  15.1 us
    ppermute x16, starting transfers between devices, from_row(): return lax.ppermute(v, 'rows', [(i, i ^ offset) for i in range(count)])  14.6 us
    pallas_call x1, Pallas kernels, run_adjoint(): pl.pallas_call(adjoint_kernel, grid=(rows_here,), in_specs=[SCALARS, SCAL...  12 us
    pallas_call x1, Pallas kernels, run_forward(): pl.pallas_call(forward_kernel, grid=(rows_here,), in_specs=[SCALARS, act,...  10.7 us
    pallas_call x10, Pallas kernels, glue(): pl.pallas_call(kernel, grid=(1,), in_specs=specs, out_specs=[spec(v) for...  9.6 us
    ppermute x6, starting transfers between devices, from_line(): lax.ppermute(v, 'seq', [(i, i ^ offset) for i in range(lax.axis_size('seq...  9.44 us
    ppermute x2, starting transfers between devices, shift(): return lax.ppermute(v, axis, pairs)  6.41 us
  transfers between devices with their start and end apart: 24, of which 7 were waited for; matrix products, arithmetic and copies ran while one was open for 0% of the time, Pallas kernels for 25%

profile of v3, /device:TPU:0, one launch (start us, length us, event | category | flops | bytes accessed | tf_op | source)
XLA Modules:
  0.0 139.9 jit_solution(6246880609188011067)
XLA Ops:
  0.6 2.5 %prepare.1 = (f32[8,256]{1,0:T(8,128)}, bf16[512,512]{1,0:T(8,128)(2,1)}, bf16[512,512]{1,0:T(8,128)(2,1)}) custom-call(f32[1,256]{1,0:T(1,128)} %bitcast.24, f32[1,256]{1,0:T(1,128)} %bitcast.25, f32[1,256]{1,0:T(1,128)} %bitcast.26, bf16[256,512]{1,0:T(8,128)(2,1)} %real_ref.3, bf16[256,512]{1,0:T(8,128)(2,1)} %imag_ref.3, bf16[512,256]{1,0:T(8,128)(2,1)} %out_real.1, ...), custom_call_target="tpu_custom_call" | custom-call | flops 1700000000 | bytes 1048576 | tf_op jit(solution)/shard_map/prepare/pallas_call | solution.py:595
  3.2 10.7 %forward.1 = (bf16[4,1024,512]{2,1,0:T(8,128)(2,1)}, bf16[4,1024,512]{2,1,0:T(8,128)(2,1)}, f32[4,1024,128]{2,1,0:T(8,128)}, f32[4,16,512]{2,1,0:T(8,128)}, f32[4,1,512]{2,1,0:T(1,128)}) custom-call(s32[4,8]{1,0:T(4,128)} %lens.9, bf16[4,1024,512]{2,1,0:T(8,128)(2,1)} %x_ref.3, f32[1,512]{1,0:T(1,128)} %bitcast.11, f32[1,512]{1,0:T(1,128)} %bitcast.16, ...), custom_call_target="tpu_custom_call" | custom-call | flops 10599999488 | bytes 1048576 | tf_op jit(solution)/shard_map/forward/pallas_call | solution.py:696
  13.9 4.9 %collective-permute-start = (f32[4,1,512]{2,1,0:T(1,128)}, f32[4,1,512]{2,1,0:T(1,128)S(1)}, u32[]{:S(2)}, u32[]{:S(2)}) collective-permute-start(f32[4,1,512]{2,1,0:T(1,128)} %get-tuple-element.74), channel_id=1, source_target_pairs={{0,1},{1,2},{2,3},{4,5},{5,6},{6,7},{8,9},{9,10},{10,11},{12,13},{... | collective-permute-start | bytes 24584 | tf_op jit(solution)/shard_map/ppermute | solution.py:575
  18.9 0.6 pad_add_fusion.first.place
  19.5 1.0 collective-permute-done.carry_ref
  20.4 0.6 copy-done.16
  21.0 40.9 %middle.1 = (bf16[4,1024,512]{2,1,0:T(8,128)(2,1)}, bf16[4,1024,512]{2,1,0:T(8,128)(2,1)}, bf16[4,1024,512]{2,1,0:T(8,128)(2,1)}, bf16[4,1024,512]{2,1,0:T(8,128...) custom-call(s32[4,8]{1,0:T(4,128)} %lens.9, ...), custom_call_target="tpu_custom_call" | custom-call | flops 48000000000 | bytes 1048576 | tf_op jit(solution)/shard_map/middle/pallas_call | solution.py:720
  62.0 1.5 %collective-permute-start.2 = (f32[4,1,512]{2,1,0:T(1,128)}, f32[4,1,512]{2,1,0:T(1,128)S(1)}, u32[]{:S(2)}, u32[]{:S(2)}) collective-permute-start(f32[4,1,512]{2,1,0:T(1,128)} %get-tuple-element.85), channel_id=1, source_target_pairs={{1,0},{2,1},{3,2},{5,4},{6,5},{7,6},{9,8},{10,9},{11,10},{13,12},{... | collective-permute-start | bytes 24584 | tf_op jit(solution)/shard_map/ppermute | solution.py:575
  63.5 1.0 collective-permute-done.1.got_ref
  64.5 1.1 copy-done.12
  65.7 0.8 early_split.1
  66.4 1.6 %collective-permute-start.3 = (bf16[64,1536]{1,0:T(8,128)(2,1)S(1)}, bf16[64,1536]{1,0:T(8,128)(2,1)S(1)}, u32[]{:S(2)}, u32[]{:S(2)}) collective-permute-start(bf16[64,1536]{1,0:T(8,128)(2,1)S(1)} %get-tuple-element.91), channel_id=1, source_target_pairs={{0,8},{4,12},{8,0},{12,4},{16,24},{20,28},{24,16},{28,20},{1,9},{5... | collective-permute-start | bytes 589832 | tf_op jit(solution)/shard_map/ppermute | solution.py:604
  68.0 1.5 %collective-permute-start.4 = (bf16[64,1536]{1,0:T(8,128)(2,1)S(1)}, bf16[64,1536]{1,0:T(8,128)(2,1)S(1)}, u32[]{:S(2)}, u32[]{:S(2)}) collective-permute-start(bf16[64,1536]{1,0:T(8,128)(2,1)S(1)} %get-tuple-element.92), channel_id=1, source_target_pairs={{0,16},{4,20},{8,24},{12,28},{16,0},{20,4},{24,8},{28,12},{1,17},{... | collective-permute-start | bytes 589832 | tf_op jit(solution)/shard_map/ppermute | solution.py:604
  69.5 0.5 collective-permute-start.5
  70.0 0.6 copy-done.17
  70.6 12.0 %adjoint.1 = (bf16[4,1024,512]{2,1,0:T(8,128)(2,1)}, bf16[272,512]{1,0:T(8,128)(2,1)}, bf16[272,512]{1,0:T(8,128)(2,1)}) custom-call(s32[4,8]{1,0:T(4,128)} %lens.9, s32[4]{0:T(128)} %pad_add_fusion.first.place, bf16[4,1024,512]{2,1,0:T(8,128)(2,1)} %get-tuple-element.83.gs_ref, f32[4,16,512]{2,1,0:T(8,128)} %get-tuple-element.84.bends_ref, ...), custom_call_target="tpu_custom_call" | custom-call | flops 12000000000 | bytes 1048576 | tf_op jit(solution)/shard_map/adjoint/pallas_call | solution.py:749
  82.7 0.6 early_sum.2.refs_0_
  83.4 1.1 collective-permute-done.6.got_ref
  84.4 0.6 late_split.1
  85.1 1.6 %collective-permute-start.7 = (bf16[80,512]{1,0:T(8,128)(2,1)S(1)}, bf16[80,512]{1,0:T(8,128)(2,1)S(1)}, u32[]{:S(2)}, u32[]{:S(2)}) collective-permute-start(bf16[80,512]{1,0:T(8,128)(2,1)S(1)} %get-tuple-element.102), channel_id=1, source_target_pairs={{0,8},{4,12},{8,0},{12,4},{16,24},{20,28},{24,16},{28,20},{1,9},{5... | collective-permute-start | bytes 245768 | tf_op jit(solution)/shard_map/ppermute | solution.py:604
  86.7 4.3 %collective-permute-start.12 = (bf16[64,1536]{1,0:T(8,128)(2,1)S(1)}, bf16[64,1536]{1,0:T(8,128)(2,1)S(1)}, u32[]{:S(2)}, u32[]{:S(2)}) collective-permute-start(bf16[64,1536]{1,0:T(8,128)(2,1)S(1)} %early_sum.2.refs_0_), channel_id=1, source_target_pairs={{0,3},{1,2},{2,1},{3,0},{4,7},{5,6},{6,5},{7,4},{8,11},{9,10},{10,... | collective-permute-start | bytes 589832 | tf_op jit(solution)/shard_map/ppermute | solution.py:608
  91.0 0.6 collective-permute-start.10
  91.6 1.5 %collective-permute-start.8 = (bf16[80,512]{1,0:T(8,128)(2,1)S(1)}, bf16[80,512]{1,0:T(8,128)(2,1)S(1)}, u32[]{:S(2)}, u32[]{:S(2)}) collective-permute-start(bf16[80,512]{1,0:T(8,128)(2,1)S(1)} %get-tuple-element.103), channel_id=1, source_target_pairs={{0,16},{4,20},{8,24},{12,28},{16,0},{20,4},{24,8},{28,12},{1,17},{... | collective-permute-start | bytes 245768 | tf_op jit(solution)/shard_map/ppermute | solution.py:604
  93.1 0.5 collective-permute-start.9
  93.6 7.6 %input.2.refs_0_ = bf16[4,1024,512]{2,1,0:T(8,128)(2,1)} custom-call(s32[4,8]{1,0:T(4,128)} %lens.9, s32[4]{0:T(128)} %pad_add_fusion.first.place, bf16[4,1024,512]{2,1,0:T(8,128)(2,1)} %get-tuple-element.89.adj_ref, bf16[4,1024,512]{2,1,0:T(8,128)(2,1)} %get-tuple-element.75.xhat_ref, bf16[4,1024,512]{2,1,0:T(8,128)(2,1)} %get-tuple-element.99.gm_ref, ...), custom_call_target="tpu_custom_call" | custom-call | flops 8000000000 | bytes 1048576 | tf_op jit(solution)/shard_map/input/pallas_call | solution.py:785
  101.2 0.6 late_sum.2.refs_0_
  101.8 3.9 %collective-permute-start.15 = (bf16[80,512]{1,0:T(8,128)(2,1)S(1)}, bf16[80,512]{1,0:T(8,128)(2,1)S(1)}, u32[]{:S(2)}, u32[]{:S(2)}) collective-permute-start(bf16[80,512]{1,0:T(8,128)(2,1)S(1)} %late_sum.2.refs_0_), channel_id=1, source_target_pairs={{0,3},{1,2},{2,1},{3,0},{4,7},{5,6},{6,5},{7,4},{8,11},{9,10},{10,... | collective-permute-start | bytes 245768 | tf_op jit(solution)/shard_map/ppermute | solution.py:608
  105.7 0.6 collective-permute-start.13
  106.3 5.9 %collective-permute-done.11.refs_2_ = bf16[64,1536]{1,0:T(8,128)(2,1)S(1)} collective-permute-done((bf16[64,1536]{1,0:T(8,128)(2,1)S(1)}, bf16[64,1536]{1,0:T(8,128)(2,1)S(1)}, u32[]{:S(2)}, u32[]{:S(2)}) %collective-permute-start.11) | collective-permute-done | bytes 196640 | tf_op jit(solution)/shard_map/ppermute | solution.py:608
  112.2 0.6 early_sum.3.refs_0_
  112.9 1.5 %collective-permute-start.18 = (bf16[64,1536]{1,0:T(8,128)(2,1)S(1)}, bf16[64,1536]{1,0:T(8,128)(2,1)S(1)}, u32[]{:S(2)}, u32[]{:S(2)}) collective-permute-start(bf16[64,1536]{1,0:T(8,128)(2,1)S(1)} %early_sum.3.refs_0_), channel_id=1, source_target_pairs={{0,24},{4,28},{8,16},{12,20},{16,8},{20,12},{24,0},{28,4},{1,25},{... | collective-permute-start | bytes 589832 | tf_op jit(solution)/shard_map/ppermute | solution.py:604
  114.4 0.5 collective-permute-start.17
  115.0 1.5 %collective-permute-start.16 = (bf16[64,1536]{1,0:T(8,128)(2,1)S(1)}, bf16[64,1536]{1,0:T(8,128)(2,1)S(1)}, u32[]{:S(2)}, u32[]{:S(2)}) collective-permute-start(bf16[64,1536]{1,0:T(8,128)(2,1)S(1)} %early_sum.3.refs_0_), channel_id=1, source_target_pairs={{0,8},{4,12},{8,0},{12,4},{16,24},{20,28},{24,16},{28,20},{1,9},{5... | collective-permute-start | bytes 589832 | tf_op jit(solution)/shard_map/ppermute | solution.py:604
  116.4 7.6 %input.3 = bf16[4,1024,512]{2,1,0:T(8,128)(2,1)} custom-call(s32[4,8]{1,0:T(4,128)} %lens.9, s32[4]{0:T(128)} %pad_add_fusion.first.place, bf16[4,1024,512]{2,1,0:T(8,128)(2,1)} %get-tuple-element.89.adj_ref, bf16[4,1024,512]{2,1,0:T(8,128)(2,1)} %get-tuple-element.75.xhat_ref, ...), custom_call_target="tpu_custom_call", output_to_operand_aliasing={{}: (10, {})} | custom-call | flops 8000000000 | bytes 1048576 | tf_op jit(solution)/shard_map/input/pallas_call | solution.py:785
  124.0 0.6 late_sum.3.own_ref
  124.7 0.6 early_gather.1.mine_ref
  125.3 0.1 collective-permute-start.22
  125.4 1.5 %collective-permute-start.21 = (bf16[64,512]{1,0:T(8,128)(2,1)S(1)}, bf16[64,512]{1,0:T(8,128)(2,1)S(1)}, u32[]{:S(2)}, u32[]{:S(2)}) collective-permute-start(bf16[64,512]{1,0:T(8,128)(2,1)S(1)} %slice.4.refs_0_), channel_id=1, source_target_pairs={{0,24},{4,28},{8,16},{12,20},{16,8},{20,12},{24,0},{28,4},{1,25},{... | collective-permute-start | bytes 196616 | tf_op jit(solution)/shard_map/ppermute | solution.py:604
  126.9 0.5 collective-permute-start.20
  127.4 1.5 %collective-permute-start.19 = (bf16[64,512]{1,0:T(8,128)(2,1)S(1)}, bf16[64,512]{1,0:T(8,128)(2,1)S(1)}, u32[]{:S(2)}, u32[]{:S(2)}) collective-permute-start(bf16[64,512]{1,0:T(8,128)(2,1)S(1)} %slice.4.refs_0_), channel_id=1, source_target_pairs={{0,8},{4,12},{8,0},{12,4},{16,24},{20,28},{24,16},{28,20},{1,9},{5... | collective-permute-start | bytes 196616 | tf_op jit(solution)/shard_map/ppermute | solution.py:604
  128.9 1.9 %collective-permute-done.21.refs_3_ = bf16[64,512]{1,0:T(8,128)(2,1)S(1)} collective-permute-done((bf16[64,512]{1,0:T(8,128)(2,1)S(1)}, bf16[64,512]{1,0:T(8,128)(2,1)S(1)}, u32[]{:S(2)}, u32[]{:S(2)}) %collective-permute-start.21) | collective-permute-done | bytes 65568 | tf_op jit(solution)/shard_map/ppermute | solution.py:604
  130.8 1.3 collective-permute-done.20.refs_2_
  132.2 0.1 collective-permute-done.19.refs_1_
  132.2 0.6 late_gather.1.mine_ref
  132.9 0.1 collective-permute-start.23
  133.0 0.9 copy-done.15
  133.9 3.8 %early_out.1 = (f32[512,512]{1,0:T(8,128)}, f32[512,512]{1,0:T(8,128)}, f32[512,256]{1,0:T(8,128)}, f32[512,256]{1,0:T(8,128)}) custom-call(s32[4]{0:T(128)} %pad_add_fusion.first.place, bf16[256,1536]{1,0:T(8,128)(2,1)} %copy-done.5, bf16[256,1536]{1,0:T(8,128)(2,1)} %copy-done.15), custom_call_target="tpu_custom_call" | custom-call | flops 4800000000 | bytes 1048576 | tf_op jit(solution)/shard_map/early_out/pallas_call | solution.py:808
  137.8 2.1 %late_out.1 = (f32[256,512]{1,0:T(8,128)}, f32[256,512]{1,0:T(8,128)}, f32[512]{0:T(512)}, f32[512]{0:T(512)}, f32[512]{0:T(512)}, /*index=5*/f32[256]{0:T(256)}, f32[256]{0:T(256)}, f32[256]{0:T(256)}, f32[1024]{0:T(1024)}) custom-call(s32[4]{0:T(128)S(1)} %copy-done.4, bf16[256,512]{1,0:T(8,128)(2,1)S(1)} %late_gather.1.mine_ref, ...), custom_call_target="tpu_custom_call" | custom-call | flops 1700000000 | bytes 1048576 | tf_op jit(solution)/shard_map/late_out/pallas_call | solution.py:595
  (54 shorter events, 0.3 us)
Async XLA Ops:
  13.9 6.5 %collective-permute-start = (f32[4,1,512]{2,1,0:T(1,128)}, f32[4,1,512]{2,1,0:T(1,128)S(1)}, u32[]{:S(2)}, u32[]{:S(2)}) collective-permute-start(f32[4,1,512]{2,1,0:T(1,128)} %get-tuple-element.74), channel_id=1, source_target_pairs={{0,1},{1,2},{2,3},{4,5},{5,6},{6,7},{8,9},{9,10},{10,11},{12,13},{... | collective-permute-start | bytes 24584 | tf_op jit(solution)/shard_map/ppermute | solution.py:575
  20.4 0.6 copy-start.16
  21.0 43.5 %copy-start = (s32[4]{0:T(128)S(1)}, s32[4]{0:T(128)}, u32[]{:S(2)}) copy-start(s32[4]{0:T(128)} %pad_add_fusion.first.place) | copy-start | bytes 52
  62.0 2.6 %collective-permute-start.1 = (bf16[256,1536]{1,0:T(8,128)(2,1)}, bf16[256,1536]{1,0:T(8,128)(2,1)S(1)}, u32[]{:S(2)}, u32[]{:S(2)}) collective-permute-start(bf16[256,1536]{1,0:T(8,128)(2,1)} %get-tuple-element.80), channel_id=1, source_target_pairs={{0,4},{4,0},{8,12},{12,8},{16,20},{20,16},{24,28},{28,24},{1,5},{5... | collective-permute-start | bytes 2359304 | tf_op jit(solution)/shard_map/ppermute | solution.py:604
  62.0 7.9 %collective-permute-start.2 = (f32[4,1,512]{2,1,0:T(1,128)}, f32[4,1,512]{2,1,0:T(1,128)S(1)}, u32[]{:S(2)}, u32[]{:S(2)}) collective-permute-start(f32[4,1,512]{2,1,0:T(1,128)} %get-tuple-element.85), channel_id=1, source_target_pairs={{1,0},{2,1},{3,2},{5,4},{6,5},{7,6},{9,8},{10,9},{11,10},{13,12},{... | collective-permute-start | bytes 24584 | tf_op jit(solution)/shard_map/ppermute | solution.py:575
  64.5 1.1 copy-start.12
  66.4 16.3 %collective-permute-start.3 = (bf16[64,1536]{1,0:T(8,128)(2,1)S(1)}, bf16[64,1536]{1,0:T(8,128)(2,1)S(1)}, u32[]{:S(2)}, u32[]{:S(2)}) collective-permute-start(bf16[64,1536]{1,0:T(8,128)(2,1)S(1)} %get-tuple-element.91), channel_id=1, source_target_pairs={{0,8},{4,12},{8,0},{12,4},{16,24},{20,28},{24,16},{28,20},{1,9},{5... | collective-permute-start | bytes 589832 | tf_op jit(solution)/shard_map/ppermute | solution.py:604
  68.0 14.7 %collective-permute-start.4 = (bf16[64,1536]{1,0:T(8,128)(2,1)S(1)}, bf16[64,1536]{1,0:T(8,128)(2,1)S(1)}, u32[]{:S(2)}, u32[]{:S(2)}) collective-permute-start(bf16[64,1536]{1,0:T(8,128)(2,1)S(1)} %get-tuple-element.92), channel_id=1, source_target_pairs={{0,16},{4,20},{8,24},{12,28},{16,0},{20,4},{24,8},{28,12},{1,17},{... | collective-permute-start | bytes 589832 | tf_op jit(solution)/shard_map/ppermute | solution.py:604
  69.5 13.2 %collective-permute-start.5 = (bf16[64,1536]{1,0:T(8,128)(2,1)S(1)}, bf16[64,1536]{1,0:T(8,128)(2,1)S(1)}, u32[]{:S(2)}, u32[]{:S(2)}) collective-permute-start(bf16[64,1536]{1,0:T(8,128)(2,1)S(1)} %get-tuple-element.93), channel_id=1, source_target_pairs={{0,24},{4,28},{8,16},{12,20},{16,8},{20,12},{24,0},{28,4},{1,25},{... | collective-permute-start | bytes 589832 | tf_op jit(solution)/shard_map/ppermute | solution.py:604
  70.0 0.6 copy-start.17
  70.6 12.1 %copy-start.1 = (s32[4]{0:T(128)S(1)}, s32[4]{0:T(128)}, u32[]{:S(2)}) copy-start(s32[4]{0:T(128)} %pad_add_fusion.first.place) | copy-start | bytes 52
  82.6 1.8 %copy-start.13 = (bf16[272,512]{1,0:T(8,128)(2,1)S(1)}, bf16[272,512]{1,0:T(8,128)(2,1)}, u32[]{:S(2)}) copy-start(bf16[272,512]{1,0:T(8,128)(2,1)} %get-tuple-element.95.mine_ref) | copy-start | bytes 835588
  82.6 1.8 %collective-permute-start.6 = (bf16[272,512]{1,0:T(8,128)(2,1)}, bf16[272,512]{1,0:T(8,128)(2,1)S(1)}, u32[]{:S(2)}, u32[]{:S(2)}) collective-permute-start(bf16[272,512]{1,0:T(8,128)(2,1)} %get-tuple-element.96), channel_id=1, source_target_pairs={{0,4},{4,0},{8,12},{12,8},{16,20},{20,16},{24,28},{28,24},{1,5},{5... | collective-permute-start | bytes 835592 | tf_op jit(solution)/shard_map/ppermute | solution.py:604
  85.1 8.1 %collective-permute-start.7 = (bf16[80,512]{1,0:T(8,128)(2,1)S(1)}, bf16[80,512]{1,0:T(8,128)(2,1)S(1)}, u32[]{:S(2)}, u32[]{:S(2)}) collective-permute-start(bf16[80,512]{1,0:T(8,128)(2,1)S(1)} %get-tuple-element.102), channel_id=1, source_target_pairs={{0,8},{4,12},{8,0},{12,4},{16,24},{20,28},{24,16},{28,20},{1,9},{5... | collective-permute-start | bytes 245768 | tf_op jit(solution)/shard_map/ppermute | solution.py:604
  86.7 19.0 %collective-permute-start.12 = (bf16[64,1536]{1,0:T(8,128)(2,1)S(1)}, bf16[64,1536]{1,0:T(8,128)(2,1)S(1)}, u32[]{:S(2)}, u32[]{:S(2)}) collective-permute-start(bf16[64,1536]{1,0:T(8,128)(2,1)S(1)} %early_sum.2.refs_0_), channel_id=1, source_target_pairs={{0,3},{1,2},{2,1},{3,0},{4,7},{5,6},{6,5},{7,4},{8,11},{9,10},{10,... | collective-permute-start | bytes 589832 | tf_op jit(solution)/shard_map/ppermute | solution.py:608
  91.0 21.2 %collective-permute-start.11 = (bf16[64,1536]{1,0:T(8,128)(2,1)S(1)}, bf16[64,1536]{1,0:T(8,128)(2,1)S(1)}, u32[]{:S(2)}, u32[]{:S(2)}) collective-permute-start(bf16[64,1536]{1,0:T(8,128)(2,1)S(1)} %early_sum.2.refs_0_), channel_id=1, source_target_pairs={{0,2},{1,3},{2,0},{3,1},{4,6},{5,7},{6,4},{7,5},{8,10},{9,11},{10,... | collective-permute-start | bytes 589832 | tf_op jit(solution)/shard_map/ppermute | solution.py:608
  91.0 21.2 %collective-permute-start.10 = (bf16[64,1536]{1,0:T(8,128)(2,1)S(1)}, bf16[64,1536]{1,0:T(8,128)(2,1)S(1)}, u32[]{:S(2)}, u32[]{:S(2)}) collective-permute-start(bf16[64,1536]{1,0:T(8,128)(2,1)S(1)} %early_sum.2.refs_0_), channel_id=1, source_target_pairs={{0,1},{1,0},{2,3},{3,2},{4,5},{5,4},{6,7},{7,6},{8,9},{9,8},{10,11... | collective-permute-start | bytes 589832 | tf_op jit(solution)/shard_map/ppermute | solution.py:608
  91.6 9.6 %collective-permute-start.8 = (bf16[80,512]{1,0:T(8,128)(2,1)S(1)}, bf16[80,512]{1,0:T(8,128)(2,1)S(1)}, u32[]{:S(2)}, u32[]{:S(2)}) collective-permute-start(bf16[80,512]{1,0:T(8,128)(2,1)S(1)} %get-tuple-element.103), channel_id=1, source_target_pairs={{0,16},{4,20},{8,24},{12,28},{16,0},{20,4},{24,8},{28,12},{1,17},{... | collective-permute-start | bytes 245768 | tf_op jit(solution)/shard_map/ppermute | solution.py:604
  93.1 8.1 %collective-permute-start.9 = (bf16[80,512]{1,0:T(8,128)(2,1)S(1)}, bf16[80,512]{1,0:T(8,128)(2,1)S(1)}, u32[]{:S(2)}, u32[]{:S(2)}) collective-permute-start(bf16[80,512]{1,0:T(8,128)(2,1)S(1)} %get-tuple-element.104), channel_id=1, source_target_pairs={{0,24},{4,28},{8,16},{12,20},{16,8},{20,12},{24,0},{28,4},{1,25},{... | collective-permute-start | bytes 245768 | tf_op jit(solution)/shard_map/ppermute | solution.py:604
  93.6 7.6 %copy-start.2 = (s32[4]{0:T(128)S(1)}, s32[4]{0:T(128)}, u32[]{:S(2)}) copy-start(s32[4]{0:T(128)} %pad_add_fusion.first.place) | copy-start | bytes 52
  101.8 13.2 %collective-permute-start.15 = (bf16[80,512]{1,0:T(8,128)(2,1)S(1)}, bf16[80,512]{1,0:T(8,128)(2,1)S(1)}, u32[]{:S(2)}, u32[]{:S(2)}) collective-permute-start(bf16[80,512]{1,0:T(8,128)(2,1)S(1)} %late_sum.2.refs_0_), channel_id=1, source_target_pairs={{0,3},{1,2},{2,1},{3,0},{4,7},{5,6},{6,5},{7,4},{8,11},{9,10},{10,... | collective-permute-start | bytes 245768 | tf_op jit(solution)/shard_map/ppermute | solution.py:608
  105.7 18.3 %collective-permute-start.14 = (bf16[80,512]{1,0:T(8,128)(2,1)S(1)}, bf16[80,512]{1,0:T(8,128)(2,1)S(1)}, u32[]{:S(2)}, u32[]{:S(2)}) collective-permute-start(bf16[80,512]{1,0:T(8,128)(2,1)S(1)} %late_sum.2.refs_0_), channel_id=1, source_target_pairs={{0,2},{1,3},{2,0},{3,1},{4,6},{5,7},{6,4},{7,5},{8,10},{9,11},{10,... | collective-permute-start | bytes 245768 | tf_op jit(solution)/shard_map/ppermute | solution.py:608
  105.7 18.3 %collective-permute-start.13 = (bf16[80,512]{1,0:T(8,128)(2,1)S(1)}, bf16[80,512]{1,0:T(8,128)(2,1)S(1)}, u32[]{:S(2)}, u32[]{:S(2)}) collective-permute-start(bf16[80,512]{1,0:T(8,128)(2,1)S(1)} %late_sum.2.refs_0_), channel_id=1, source_target_pairs={{0,1},{1,0},{2,3},{3,2},{4,5},{5,4},{6,7},{7,6},{8,9},{9,8},{10,11... | collective-permute-start | bytes 245768 | tf_op jit(solution)/shard_map/ppermute | solution.py:608
  112.9 11.1 %copy-start.3 = (s32[4]{0:T(128)S(1)}, s32[4]{0:T(128)}, u32[]{:S(2)}) copy-start(s32[4]{0:T(128)} %pad_add_fusion.first.place) | copy-start | bytes 52
  112.9 11.7 %collective-permute-start.18 = (bf16[64,1536]{1,0:T(8,128)(2,1)S(1)}, bf16[64,1536]{1,0:T(8,128)(2,1)S(1)}, u32[]{:S(2)}, u32[]{:S(2)}) collective-permute-start(bf16[64,1536]{1,0:T(8,128)(2,1)S(1)} %early_sum.3.refs_0_), channel_id=1, source_target_pairs={{0,24},{4,28},{8,16},{12,20},{16,8},{20,12},{24,0},{28,4},{1,25},{... | collective-permute-start | bytes 589832 | tf_op jit(solution)/shard_map/ppermute | solution.py:604
  114.4 10.2 %collective-permute-start.17 = (bf16[64,1536]{1,0:T(8,128)(2,1)S(1)}, bf16[64,1536]{1,0:T(8,128)(2,1)S(1)}, u32[]{:S(2)}, u32[]{:S(2)}) collective-permute-start(bf16[64,1536]{1,0:T(8,128)(2,1)S(1)} %early_sum.3.refs_0_), channel_id=1, source_target_pairs={{0,16},{4,20},{8,24},{12,28},{16,0},{20,4},{24,8},{28,12},{1,17},{... | collective-permute-start | bytes 589832 | tf_op jit(solution)/shard_map/ppermute | solution.py:604
  115.0 9.7 %collective-permute-start.16 = (bf16[64,1536]{1,0:T(8,128)(2,1)S(1)}, bf16[64,1536]{1,0:T(8,128)(2,1)S(1)}, u32[]{:S(2)}, u32[]{:S(2)}) collective-permute-start(bf16[64,1536]{1,0:T(8,128)(2,1)S(1)} %early_sum.3.refs_0_), channel_id=1, source_target_pairs={{0,8},{4,12},{8,0},{12,4},{16,24},{20,28},{24,16},{28,20},{1,9},{5... | collective-permute-start | bytes 589832 | tf_op jit(solution)/shard_map/ppermute | solution.py:604
  125.3 7.7 %copy-start.5 = (bf16[256,1536]{1,0:T(8,128)(2,1)}, bf16[256,1536]{1,0:T(8,128)(2,1)S(1)}, u32[]{:S(2)}) copy-start(bf16[256,1536]{1,0:T(8,128)(2,1)S(1)} %early_gather.1.mine_ref) | copy-start | bytes 2359300
  125.3 7.7 %collective-permute-start.22 = (bf16[256,1536]{1,0:T(8,128)(2,1)S(1)}, bf16[256,1536]{1,0:T(8,128)(2,1)S(1)}, u32[]{:S(2)}, u32[]{:S(2)}) collective-permute-start(bf16[256,1536]{1,0:T(8,128)(2,1)S(1)} %early_gather.1.mine_ref), channel_id=1, source_target_pairs={{0,4},{4,0},{8,12},{12,8},{16,20},{20,16},{24,28},{28,24},{1,5},{5... | collective-permute-start | bytes 2359304 | tf_op jit(solution)/shard_map/ppermute | solution.py:604
  125.4 5.5 %collective-permute-start.21 = (bf16[64,512]{1,0:T(8,128)(2,1)S(1)}, bf16[64,512]{1,0:T(8,128)(2,1)S(1)}, u32[]{:S(2)}, u32[]{:S(2)}) collective-permute-start(bf16[64,512]{1,0:T(8,128)(2,1)S(1)} %slice.4.refs_0_), channel_id=1, source_target_pairs={{0,24},{4,28},{8,16},{12,20},{16,8},{20,12},{24,0},{28,4},{1,25},{... | collective-permute-start | bytes 196616 | tf_op jit(solution)/shard_map/ppermute | solution.py:604
  126.9 5.2 %collective-permute-start.20 = (bf16[64,512]{1,0:T(8,128)(2,1)S(1)}, bf16[64,512]{1,0:T(8,128)(2,1)S(1)}, u32[]{:S(2)}, u32[]{:S(2)}) collective-permute-start(bf16[64,512]{1,0:T(8,128)(2,1)S(1)} %slice.4.refs_0_), channel_id=1, source_target_pairs={{0,16},{4,20},{8,24},{12,28},{16,0},{20,4},{24,8},{28,12},{1,17},{... | collective-permute-start | bytes 196616 | tf_op jit(solution)/shard_map/ppermute | solution.py:604
  127.4 4.8 %collective-permute-start.19 = (bf16[64,512]{1,0:T(8,128)(2,1)S(1)}, bf16[64,512]{1,0:T(8,128)(2,1)S(1)}, u32[]{:S(2)}, u32[]{:S(2)}) collective-permute-start(bf16[64,512]{1,0:T(8,128)(2,1)S(1)} %slice.4.refs_0_), channel_id=1, source_target_pairs={{0,8},{4,12},{8,0},{12,4},{16,24},{20,28},{24,16},{28,20},{1,9},{5... | collective-permute-start | bytes 196616 | tf_op jit(solution)/shard_map/ppermute | solution.py:604
  132.8 4.9 %copy-start.4 = (s32[4]{0:T(128)S(1)}, s32[4]{0:T(128)}, u32[]{:S(2)}) copy-start(s32[4]{0:T(128)} %pad_add_fusion.first.place) | copy-start | bytes 52
  132.8 4.9 %copy-start.6 = (bf16[256,512]{1,0:T(8,128)(2,1)S(1)}, bf16[256,512]{1,0:T(8,128)(2,1)}, u32[]{:S(2)}) copy-start(bf16[256,512]{1,0:T(8,128)(2,1)} %real_ref.3) | copy-start | bytes 786436
  132.8 4.9 %copy-start.7 = (bf16[256,512]{1,0:T(8,128)(2,1)S(1)}, bf16[256,512]{1,0:T(8,128)(2,1)}, u32[]{:S(2)}) copy-start(bf16[256,512]{1,0:T(8,128)(2,1)} %imag_ref.3) | copy-start | bytes 786436
  132.8 4.9 %copy-start.8 = (f32[512]{0:T(512)S(1)}, f32[512]{0:T(512)}, u32[]{:S(2)}) copy-start(f32[512]{0:T(512)} %param.17) | copy-start | bytes 6148
  132.9 4.9 %copy-start.9 = (f32[512]{0:T(512)S(1)}, f32[512]{0:T(512)}, u32[]{:S(2)}) copy-start(f32[512]{0:T(512)} %param.18) | copy-start | bytes 6148
  132.9 4.9 %copy-start.10 = (f32[512]{0:T(512)S(1)}, f32[512]{0:T(512)}, u32[]{:S(2)}) copy-start(f32[512]{0:T(512)} %param.26) | copy-start | bytes 6148
  132.9 4.9 %copy-start.11 = (bf16[512,512]{1,0:T(8,128)(2,1)S(1)}, bf16[512,512]{1,0:T(8,128)(2,1)}, u32[]{:S(2)}) copy-start(bf16[512,512]{1,0:T(8,128)(2,1)} %get-tuple-element.70.scaled.scaled_ref) | copy-start | bytes 1572868
  132.9 4.9 %copy-start.14 = (f32[8,256]{1,0:T(8,128)S(1)}, f32[8,256]{1,0:T(8,128)}, u32[]{:S(2)}) copy-start(f32[8,256]{1,0:T(8,128)} %get-tuple-element.71.lam.coef) | copy-start | bytes 24580
  132.9 4.8 %collective-permute-start.23 = (bf16[256,512]{1,0:T(8,128)(2,1)S(1)}, bf16[256,512]{1,0:T(8,128)(2,1)S(1)}, u32[]{:S(2)}, u32[]{:S(2)}) collective-permute-start(bf16[256,512]{1,0:T(8,128)(2,1)S(1)} %late_gather.1.mine_ref), channel_id=1, source_target_pairs={{0,4},{4,0},{8,12},{12,8},{16,20},{20,16},{24,28},{28,24},{1,5},{5... | collective-permute-start | bytes 786440 | tf_op jit(solution)/shard_map/ppermute | solution.py:604
  133.0 0.9 copy-start.15
